TPU v7x, 32 devices: a whole 2x2x4 slice. The times are simulated.
32 devices in a mesh: dp: 2 (over y), tm: 4 (over z), label: 4 (over x, core).
Axes of the slice: x: 2, y: 2, z: 4, core: 2. Of those that a mesh axis runs over, the one named last changes fastest.
Arguments:
- encoder_out: bfloat16 [2, 512, 512], P('dp', 'tm', 'label'), may hold values from -8 to 8
- predictor_out: bfloat16 [2, 128, 512], P('dp', 'label', 'tm'), may hold values from -6 to 6
- label_ids: int32 [2, 128], P('dp', 'label'), may hold values from 1 to 511
- log_alpha: float32 [2, 512, 128], P('dp', 'tm', 'label'), may hold values from -2 to 0
- log_beta: float32 [2, 512, 128], P('dp', 'tm', 'label'), may hold values from -2 to 0
- frame_count: int32 [2], P('dp'), may hold values from 256 to 512, as said below
- label_count: int32 [2], P('dp'), may hold values from 32 to 127, as said below
- joint_weight: bfloat16 [512, 512], replicated, may hold values from -2 to 2
- joint_bias: float32 [512], replicated, may hold values from -5 to 10
Outputs:
- encoder_gradient: float32 [2, 512, 512], P('dp', 'tm', 'label')
- predictor_gradient: float32 [2, 128, 512], P('dp', 'label', 'tm')
- weight_gradient: float32 [512, 512], P(('tm', 'label'))
- bias_gradient: float32 [512], P(('tm', 'label'))
Inputs may be any that keep to these rules, and one draw needn't show every extreme that they name: `frame_count`: some utterance has all 512 frames. `label_count`: some utterance has 127 labels.
All inputs are finite; a program needn't handle non-finite values.
Results may differ from a plain program's by a relative error of at most 0.0003.
The roundings to bfloat16 on the way count: a program that leaves them out, or rounds other values in their place, can miss the bound.
Values may be sent and summed in bfloat16 or wider, within the bound.
No kernel may reach another device: no remote copies, remote signals or barrier semaphores. Data moves between devices by JAX's collectives and lax.ppermute only.
A program may use at most 64 MiB of HBM per device.

v0:
```python
import jax
import jax.numpy as jnp
from jax import lax
from jax.sharding import PartitionSpec as P


def shifted(block, axis, distance):
    devices = range(lax.axis_size(axis))
    route = [(i - distance, i) for i in devices if i - distance in devices]
    return lax.ppermute(block, axis, route)


def from_root(value, axis, source):
    kept = jnp.where(lax.axis_index(axis) == source, value, 0).astype(value.dtype)
    return lax.psum(kept, axis)


def lattice(
    frame_rows,
    label_rows,
    label_row,
    alpha_rows,
    beta_rows,
    beta_down,
    beta_right,
    row_start,
    col_start,
    frame_limit,
    label_limit,
    score,
    weight_matrix,
    bias_vector,
):
    row_count, joint_width = frame_rows.shape
    col_count = label_rows.shape[0]
    vocab_size = weight_matrix.shape[1]
    summed = frame_rows.astype(jnp.float32)[:, None, :] + label_rows.astype(jnp.float32)[None, :, :]
    joint_act = jnp.tanh(summed).astype(jnp.bfloat16).reshape(row_count * col_count, joint_width)
    logits = (
        jnp.dot(joint_act, weight_matrix, preferred_element_type=jnp.float32) + bias_vector[None, :]
    )
    peak_value = jnp.max(logits, axis=1, keepdims=True)
    log_total = peak_value + jnp.log(jnp.sum(jnp.exp(logits - peak_value), axis=1, keepdims=True))
    probability = jnp.exp(logits - log_total)
    symbol = lax.broadcasted_iota(jnp.int32, (1, vocab_size), 1)
    label_cells = jnp.broadcast_to(label_row[None, :], (row_count, col_count)).reshape(
        row_count * col_count, 1
    )
    chosen = symbol == label_cells
    blank_score = (logits[:, 0] - log_total[:, 0]).reshape(row_count, col_count)
    label_score = (jnp.sum(jnp.where(chosen, logits, 0.0), axis=1) - log_total[:, 0]).reshape(
        row_count, col_count
    )
    frame_pos = row_start + jnp.arange(row_count, dtype=jnp.int32)[:, None]
    col_pos = col_start + jnp.arange(col_count, dtype=jnp.int32)[None, :]
    inside = (frame_pos < frame_limit) & (col_pos <= label_limit)
    blank_live = inside & ((frame_pos + 1 < frame_limit) | (col_pos == label_limit))
    label_live = inside & (col_pos < label_limit)
    after_blank = jnp.where(frame_pos + 1 < frame_limit, beta_down, 0.0)
    occupancy = jnp.where(inside, jnp.exp(alpha_rows + beta_rows - score), 0.0).reshape(-1, 1)
    blank_weight = jnp.where(
        blank_live, jnp.exp(alpha_rows + blank_score + after_blank - score), 0.0
    ).reshape(-1, 1)
    label_weight = jnp.where(
        label_live, jnp.exp(alpha_rows + label_score + beta_right - score), 0.0
    ).reshape(-1, 1)
    logit_gradient = (
        occupancy * probability
        - jnp.where(symbol == 0, blank_weight, 0.0)
        - jnp.where(chosen, label_weight, 0.0)
    ).astype(jnp.bfloat16)
    back_gradient = lax.dot_general(
        logit_gradient, weight_matrix, (((1,), (1,)), ((), ())), preferred_element_type=jnp.float32
    )
    joint_wide = joint_act.astype(jnp.float32)
    cell_gradient = (back_gradient * (1.0 - joint_wide * joint_wide)).reshape(
        row_count, col_count, joint_width
    )
    weight_term = lax.dot_general(
        joint_act, logit_gradient, (((0,), (0,)), ((), ())), preferred_element_type=jnp.float32
    )
    return (
        cell_gradient.sum(axis=1),
        cell_gradient.sum(axis=0),
        weight_term,
        logit_gradient.astype(jnp.float32).sum(axis=0),
    )


def per_device(
    encoder_out,
    predictor_out,
    label_ids,
    log_alpha,
    log_beta,
    frame_count,
    label_count,
    joint_weight,
    joint_bias,
):
    frames = encoder_out.shape[1]
    columns = label_ids.shape[1]
    joint_width, vocab_size = joint_weight.shape
    block_rows = 16
    block_count = frames // block_rows
    frame_full = lax.all_gather(encoder_out, "label", axis=2, tiled=True)
    label_full = lax.all_gather(predictor_out, "tm", axis=2, tiled=True)
    next_row = shifted(log_beta[:, :1, :], "tm", -1)
    beside = shifted(log_beta[:, :, :1], "label", -1)
    total_score = from_root(log_beta[:, 0, 0], ("tm", "label"), 0)
    beta_down = jnp.concatenate([log_beta[:, 1:, :], next_row], axis=1)
    beta_right = jnp.concatenate([log_beta[:, :, 1:], beside], axis=2)
    row_base = lax.axis_index("tm") * frames
    col_base = lax.axis_index("label") * columns
    weight_sum = jnp.zeros((joint_width, vocab_size), jnp.float32)
    bias_sum = jnp.zeros((vocab_size,), jnp.float32)
    utterance = 0

    def advance(running, block_idx, utterance=utterance):
        first_row = block_idx * block_rows

        def take_rows(source):
            return lax.dynamic_slice_in_dim(source[utterance], first_row, block_rows, 0)

        frame_term, label_term, weight_term, bias_term = lattice(
            take_rows(frame_full),
            label_full[utterance],
            label_ids[utterance],
            take_rows(log_alpha),
            take_rows(log_beta),
            take_rows(beta_down),
            take_rows(beta_right),
            row_base + first_row,
            col_base,
            frame_count[utterance],
            label_count[utterance],
            total_score[utterance],
            joint_weight,
            joint_bias,
        )
        return (
            (running[0] + label_term, running[1] + weight_term, running[2] + bias_term),
            frame_term,
        )

    start_state = (jnp.zeros((columns, joint_width), jnp.float32), weight_sum, bias_sum)
    (label_sum, weight_sum, bias_sum), frame_blocks = lax.scan(
        advance, start_state, jnp.arange(block_count, dtype=jnp.int32)
    )
    frame_parts = [frame_blocks.reshape(frames, frame_blocks.shape[2])]
    label_parts = [label_sum]
    frame_stack = jnp.stack(frame_parts)
    label_stack = jnp.stack(label_parts)
    encoder_gradient = lax.psum_scatter(frame_stack, "label", scatter_dimension=2, tiled=True)
    predictor_gradient = lax.psum_scatter(label_stack, "tm", scatter_dimension=2, tiled=True)
    whole_weight, whole_bias = lax.psum((weight_sum, bias_sum), ("dp", "tm", "label"))
    share_count = lax.axis_size(("tm", "label"))
    position = lax.axis_index(("tm", "label"))
    weight_rows = joint_width // share_count
    bias_rows = vocab_size // share_count
    weight_gradient = lax.dynamic_slice_in_dim(whole_weight, position * weight_rows, weight_rows, 0)
    bias_gradient = lax.dynamic_slice_in_dim(whole_bias, position * bias_rows, bias_rows, 0)
    return (encoder_gradient, predictor_gradient, weight_gradient, bias_gradient)


def solution(mesh):
    return jax.shard_map(
        per_device,
        mesh=mesh,
        in_specs=(
            P("dp", "tm", "label"),
            P("dp", "label", "tm"),
            P("dp", "label"),
            P("dp", "tm", "label"),
            P("dp", "tm", "label"),
            P("dp"),
            P("dp"),
            P(),
            P(),
        ),
        out_specs=(
            P("dp", "tm", "label"),
            P("dp", "label", "tm"),
            P(("tm", "label"), None),
            P(("tm", "label")),
        ),
        check_vma=False,
    )
```

profile of v0, /device:TPU:0, one launch (start us, length us, event | category | flops | bytes accessed | tf_op | source)
XLA Modules:
  0.0 285.6 jit_solution(2784752214590504254)
XLA Ops:
  8.1 0.7 slice.22
  8.8 1.3 collective-permute-start.1
  10.1 1.3 collective-permute-start
  11.4 1.2 slice.18
  12.6 0.7 slice.21
  13.3 0.8 slice.19
  14.1 0.8 copy.25
  15.6 37.5 %psum.21 = f32[1]{0:T(128)} all-reduce(f32[1]{0:T(128)S(6)} %select_n.62), channel_id=1, replica_groups=mesh['dp'=2,'tm'=4,'label'=4] {'tm','label'}, use_global_device_ids=true, to_apply=%region_0.1 | all-reduce | flops 1 | bytes 8 | tf_op jit(solution)/shard_map/psum | solution.py:15
  53.1 12.1 %all_gather.7 = bf16[1,32,512]{2,1,0:T(8,128)(2,1)S(1)} all-gather(bf16[1,32,128]{2,1,0:T(8,128)(2,1)} %param.12), channel_id=1, replica_groups=mesh['dp'=2,'tm'=4,'label'=4] {'tm'}, dimensions={2}, use_global_device_ids=true | all-gather | bytes 40960 | tf_op jit(solution)/shard_map/all_gather | solution.py:107
  65.2 5.6 %all_gather.6 = bf16[1,128,512]{2,1,0:T(8,128)(2,1)S(1)} all-gather(bf16[1,128,128]{2,1,0:T(8,128)(2,1)} %param.11), channel_id=1, replica_groups=mesh['dp'=2,'tm'=4,'label'=4] {'label'}, dimensions={2}, use_global_device_ids=true | all-gather | bytes 163840 | tf_op jit(solution)/shard_map/all_gather | solution.py:106
  70.8 0.8 copy.24
  72.6 74.2 %while.17 = (s32[]{:T(128)}, f32[32,512]{1,0:T(8,128)S(1)}, f32[512,512]{1,0:T(8,128)S(1)}, f32[512]{0:T(512)S(1)}, f32[8,16,512]{2,1,0:T(8,128)}, /*index=5*/s3...) while((s32[]{:T(128)}, f32[32,512]{1,0:T(8,128)S(1)}, ...), condition=%wide.region_8.9_spmd.clone, body=%wide.region_1.8_spmd.clone.sunk | while | flops 812426496 | bytes 12778731 | solution.py:147
  78.1 0.7 exponential_select_fusion.3
  78.8 0.7 and_select_fusion.2
  87.4 0.7 exponential_select_fusion.3
  88.0 0.7 and_select_fusion.2
  96.7 0.7 exponential_select_fusion.3
  97.3 0.7 and_select_fusion.2
  105.9 0.7 exponential_select_fusion.3
  106.6 0.7 and_select_fusion.2
  115.2 0.7 exponential_select_fusion.3
  115.9 0.7 and_select_fusion.2
  124.5 0.7 exponential_select_fusion.3
  125.2 0.7 and_select_fusion.2
  133.8 0.7 exponential_select_fusion.3
  134.4 0.7 and_select_fusion.2
  143.0 0.7 exponential_select_fusion.3
  143.7 0.7 and_select_fusion.2
  146.9 1.0 copy-done.1
  149.0 37.9 %psum.23 = f32[512]{0:T(512)S(1)} all-reduce(f32[512]{0:T(512)S(1)} %get-tuple-element.112), channel_id=1, replica_groups=mesh['dp'=2,'tm'=4,'label'=4] {'dp','tm','label'}, use_global_device_ids=true, to_apply=%region_12.13 | all-reduce | flops 512 | bytes 4096 | tf_op jit(solution)/shard_map/psum | solution.py:156
  187.5 89.2 %all-reduce.2.cloned.1.call-done = f32[512,512]{1,0:T(8,128)} async-done(((f32[512,512]{1,0:T(8,128)}), f32[512,512]{1,0:T(8,128)}) %all-reduce.2.cloned.1.call-update) | async-done | bytes 1048592 | tf_op jit(solution)/shard_map/psum | solution.py:156
  276.7 1.5 constant_dynamic-slice_fusion.4
  (309 shorter events, 59.9 us)
Async XLA Ops:
  8.0 64.0 %copy-start = (bf16[512,512]{1,0:T(8,128)(2,1)S(1)}, bf16[512,512]{1,0:T(8,128)(2,1)}, u32[]{:S(2)}) copy-start(bf16[512,512]{1,0:T(8,128)(2,1)} %param.18) | copy-start | bytes 1572868
  8.0 268.7 %all-reduce.2.cloned.1.call-start = ((), (), s32[]{:S(2)}) async-start(), calls=%async_computation.4 | async-start | bytes 2097152 | tf_op jit(solution)/shard_map/psum | solution.py:156
  8.8 63.0 %collective-permute-start.1 = (f32[1,128,1]{1,2,0:T(1,128)S(1)}, f32[1,128,1]{1,2,0:T(1,128)S(1)}, u32[]{:S(2)}, u32[]{:S(2)}) collective-permute-start(f32[1,128,1]{1,2,0:T(1,128)S(1)} %slice.22), channel_id=1, source_target_pairs={{1,0},{2,1},{3,2},{5,4},{6,5},{7,6},{9,8},{10,9},{11,10},{13,12},{... | collective-permute-start | bytes 1544 | tf_op jit(solution)/shard_map/ppermute | solution.py:10
  10.1 61.6 %collective-permute-start = (f32[1,1,32]{1,2,0:T(8,128)}, f32[1,1,32]{1,2,0:T(8,128)S(1)}, u32[]{:S(2)}, u32[]{:S(2)}) collective-permute-start(f32[1,1,32]{1,2,0:T(8,128)} %bitcast.75), channel_id=1, source_target_pairs={{4,0},{8,4},{12,8},{5,1},{9,5},{13,9},{6,2},{10,6},{14,10},{7,3},{... | collective-permute-start | bytes 392 | tf_op jit(solution)/shard_map/ppermute | solution.py:10
  71.8 0.7 copy-start.3
  71.9 0.7 copy-start.4
  146.8 1.0 copy-start.1
  146.9 1.0 copy-start.2
  147.9 130.3 %reduce-scatter.5.cloned.1.call-start = ((), (), s32[]{:S(2)}) async-start(), calls=%async_computation.3 | async-start | bytes 81920 | tf_op jit(solution)/shard_map/reduce_scatter | solution.py:155
  148.5 129.7 %reduce-scatter.3.cloned.1.call-start = ((), (), s32[]{:S(2)}) async-start(), calls=%async_computation.2 | async-start | bytes 327680 | tf_op jit(solution)/shard_map/reduce_scatter | solution.py:154
Sparse Core Ops, SparseCore 0:
  148.0 128.6 all-reduce.1
Sparse Core Ops, SparseCore 1:
  151.2 16.9 reduce-scatter.4
  171.0 18.3 reduce-scatter.2
where the time goes:
time: 287 us; the launch traced here: 286 us
  blocking collectives  93.1 us (32%)
  waiting for transfers between devices  90.3 us (31%)
  other arithmetic  36.4 us (13%)
  local copies, waits for them, and re-layouts  27.2 us (9%)
  between operations  16.3 us (6%)
  matrix products  13.2 us (5%)
  loops' own time  6.44 us (2%)
    psum x1, waiting for transfers between devices, per_device(): lax.psum((weight_sum, bias_sum), ('dp', 'tm', 'label'))  89.2 us
    psum x1, blocking collectives, per_device(): lax.psum((weight_sum, bias_sum), ('dp', 'tm', 'label'))  37.9 us
    psum x1, blocking collectives, from_root(): return lax.psum(kept, axis)  37.5 us
    all_gather x1, blocking collectives, per_device(): label_full = lax.all_gather(predictor_out, 'tm', axis=2, tiled=True)  12.1 us
    another operation x1, loops' own time, per_device(): lax.scan(advance, start_state, jnp.arange(block_count, dtype=jnp.int32))  6.44 us
  transfers between devices with their start and end apart: 5, of which 1 were waited for; matrix products, arithmetic and copies ran while one was open for 2% of the time, Pallas kernels for 0%

commit v1 on v0

v1 whole, which is shorter than its diff:
```python
import functools

import jax
import jax.numpy as jnp
from jax import lax
from jax.experimental import pallas as pl
from jax.experimental.pallas import tpu as pltpu
from jax.sharding import PartitionSpec as P

GROUP = 4
CHUNK = 16
LANES = 128
FAR = -1e30


def bits_of(size):
    return [1 << i for i in range(size.bit_length() - 1)]


def reverse_bits(value, size):
    width = size.bit_length() - 1
    result = 0
    for i in range(width):
        result = result | (((value >> i) & 1) << (width - 1 - i))
    return result


def swap(value, axis, bit):
    return lax.ppermute(value, axis, [(i, i ^ bit) for i in range(lax.axis_size(axis))])


def gather_slots(value, axis):
    slots = value[None]
    for bit in bits_of(lax.axis_size(axis)):
        slots = jnp.concatenate([slots, swap(slots, axis, bit)], axis=0)
    return slots


def scatter_slots(slots, axis):
    for bit in bits_of(lax.axis_size(axis)):
        half = slots.shape[0] // 2
        slots = slots[:half] + swap(slots[half:], axis, bit)
    return slots[0]


def forward_kernel(
    ids_ref,
    frames_ref,
    labels_ref,
    enc_ref,
    pred_ref,
    side_ref,
    alpha_ref,
    beta_ref,
    wt_ref,
    bias_ref,
    act_ref,
    grad_ref,
    *rest,
    tm_size,
    label_size,
):
    out_refs, (enc_t, pred_t, bias_t, occ_s, blank_s, label_s, lt, acc) = rest[:-8], rest[-8:]
    step = pl.program_id(0)
    columns, frames = alpha_ref.shape
    width, vocab = wt_ref.shape[1], wt_ref.shape[0]
    mine, row = lax.axis_index("label"), lax.axis_index("tm")

    @pl.when(step == 0)
    def _():
        enc_width = enc_ref.shape[2]
        for s in range(label_size):
            start = pl.multiple_of((mine ^ s) * enc_width, enc_width)
            enc_t[pl.ds(start, enc_width), :] = enc_ref[s].astype(jnp.float32).T
        pred_width = pred_ref.shape[2]
        pred_t[...] = jnp.zeros_like(pred_t)
        for s in range(tm_size):
            start = pl.multiple_of((row ^ s) * pred_width, pred_width)
            pred_t[pl.ds(start, pred_width), :columns] = pred_ref[s, :columns, :].T
        bias_t[...] = jnp.broadcast_to(bias_ref[...], (frames, vocab)).T
        acc[...] = jnp.zeros_like(acc)
        alpha, beta = alpha_ref[...], beta_ref[...]
        score = pred_ref[row, columns + 1 : columns + 2, 0:1]
        below = pred_ref[row ^ jnp.minimum(row + 1, tm_size - 1), columns : columns + 1, :columns]
        beside = side_ref[mine ^ jnp.minimum(mine + 1, label_size - 1)]
        lane = lax.broadcasted_iota(jnp.int32, (columns, frames), 1)
        line = lax.broadcasted_iota(jnp.int32, (columns, frames), 0)
        below = jnp.broadcast_to(below, (columns, columns))
        below = jnp.sum(
            jnp.where(
                lax.broadcasted_iota(jnp.int32, (columns, columns), 0)
                == lax.broadcasted_iota(jnp.int32, (columns, columns), 1),
                below,
                0.0,
            ),
            axis=1,
            keepdims=True,
        )
        down = jnp.where(lane == frames - 1, below, pltpu.roll(beta, frames - 1, 1))
        right = jnp.where(line == columns - 1, beside, pltpu.roll(beta, columns - 1, 0))
        frame = row * frames + lane
        column = mine * columns + line
        frame_limit, label_limit = frames_ref[0], labels_ref[0]
        inside = (frame < frame_limit) & (column <= label_limit)
        more = frame + 1 < frame_limit
        occ_s[...] = jnp.where(inside, jnp.exp(alpha + beta - score), 0.0)
        blank_s[...] = jnp.where(
            inside & (more | (column == label_limit)),
            alpha + jnp.where(more, down, 0.0) - score,
            FAR,
        )
        label_s[...] = jnp.where(inside & (column < label_limit), alpha + right - score, FAR)

    shift = lax.rem(LANES - step * GROUP, LANES)
    turned = pltpu.roll(pred_t[...], shift, 1)
    for j in range(GROUP):
        here = slice(j * frames, (j + 1) * frames)
        for c in range(0, width, 64):
            total = enc_t[c : c + 64, :] + turned[c : c + 64, j : j + 1]
            act_ref[c : c + 64, here] = jnp.tanh(total).astype(jnp.bfloat16)
    act_ref[width:, :] = jnp.ones((act_ref.shape[0] - width, GROUP * frames), jnp.bfloat16)
    product = jnp.dot(wt_ref[...], act_ref[:width, :], preferred_element_type=jnp.float32)
    for j in range(GROUP):
        lt[j] = product[:, j * frames : (j + 1) * frames]

    peak = jnp.full((GROUP, 8, frames), FAR, jnp.float32)
    for c in range(0, vocab, CHUNK):
        logits = lt[:, c : c + CHUNK, :] + bias_t[c : c + CHUNK, :][None]
        lt[:, c : c + CHUNK, :] = logits
        for k in range(0, CHUNK, 8):
            peak = jnp.maximum(peak, logits[:, k : k + 8, :])
    peak = jnp.max(peak, axis=1, keepdims=True)

    ids = [ids_ref[0, step * GROUP + j] for j in range(GROUP)]
    blank_logit = lt[:, 0:1, :]
    label_logit = jnp.concatenate([lt[j, pl.ds(ids[j], 1), :][None] for j in range(GROUP)], axis=0)

    def line_of(ref):
        return jnp.concatenate(
            [ref[pl.ds(step * GROUP + j, 1), :][None] for j in range(GROUP)], axis=0
        )

    total = jnp.zeros((GROUP, 8, frames), jnp.float32)
    for c in range(0, vocab, CHUNK):
        lifted = jnp.exp(lt[:, c : c + CHUNK, :] - peak)
        lt[:, c : c + CHUNK, :] = lifted
        for k in range(0, CHUNK, 8):
            total = total + lifted[:, k : k + 8, :]
    total = jnp.sum(total, axis=1, keepdims=True)
    log_total = peak + jnp.log(total)
    scale = line_of(occ_s) / total
    blank_weight = jnp.exp(line_of(blank_s) + (blank_logit - log_total))
    label_weight = jnp.exp(line_of(label_s) + (label_logit - log_total))

    place = lax.broadcasted_iota(jnp.int32, (CHUNK, frames), 0)
    for j in range(GROUP):
        here = slice(j * frames, (j + 1) * frames)
        for c in range(0, vocab, CHUNK):
            grad_ref[c : c + CHUNK, here] = (lt[j, c : c + CHUNK, :] * scale[j]).astype(jnp.bfloat16)
        for first in (0, pl.multiple_of((ids[j] // CHUNK) * CHUNK, CHUNK)):
            value = lt[j, pl.ds(first, CHUNK), :] * scale[j]
            value = value - jnp.where(place + first == 0, blank_weight[j], 0.0)
            value = value - jnp.where(place + first == ids[j], label_weight[j], 0.0)
            grad_ref[pl.ds(first, CHUNK), here] = value.astype(jnp.bfloat16)

    acc[...] += lax.dot_general(
        act_ref[...], grad_ref[...], (((1,), (1,)), ((), ())), preferred_element_type=jnp.float32
    )

    @pl.when(step == pl.num_programs(0) - 1)
    def _():
        if len(out_refs) == 1:
            out_refs[0][...] = acc[: width + 8, :]
            return
        parts = tm_size * label_size
        rows = width // parts
        for s in range(parts):
            label = reverse_bits(s // tm_size, label_size) ^ mine
            tm = reverse_bits(s % tm_size, tm_size) ^ row
            start = pl.multiple_of((tm * label_size + label) * rows, rows)
            ref = out_refs[s // (parts // 2)]
            to = (s % (parts // 2)) * rows
            ref[to : to + rows, :] = acc[pl.ds(start, rows), :]
        for ref in out_refs:
            ref[width // 2 :, :] = acc[width : width + 8, :]


def backward_kernel(
    act_ref, grad_ref, w_ref, enc_out, pred_out, bt, enc_acc, pred_acc, *, tm_size, label_size, columns
):
    step = pl.program_id(0)
    width = w_ref.shape[0]
    frames = enc_acc.shape[1]

    @pl.when(step == 0)
    def _():
        enc_acc[...] = jnp.zeros_like(enc_acc)
        pred_acc[...] = jnp.zeros_like(pred_acc)

    bt[...] = jnp.dot(w_ref[...], grad_ref[...], preferred_element_type=jnp.float32)
    lane = lax.broadcasted_iota(jnp.int32, (CHUNK, LANES), 1)
    for c in range(0, width, CHUNK):
        act = act_ref[c : c + CHUNK, :].astype(jnp.float32)
        cell = bt[c : c + CHUNK, :] * (1.0 - act * act)
        total = enc_acc[c : c + CHUNK, :]
        kept = pred_acc[c : c + CHUNK, :]
        for j in range(GROUP):
            part = cell[:, j * frames : (j + 1) * frames]
            total = total + part
            kept = jnp.where(lane == step * GROUP + j, jnp.sum(part, axis=1, keepdims=True), kept)
        enc_acc[c : c + CHUNK, :] = total
        pred_acc[c : c + CHUNK, :] = kept

    @pl.when(step == pl.num_programs(0) - 1)
    def _():
        mine, row = lax.axis_index("label"), lax.axis_index("tm")
        enc_width, pred_width = enc_out.shape[2], pred_out.shape[2]
        for s in range(label_size):
            start = pl.multiple_of((reverse_bits(s, label_size) ^ mine) * enc_width, enc_width)
            enc_out[s] = enc_acc[pl.ds(start, enc_width), :].T
        for s in range(tm_size):
            start = pl.multiple_of((reverse_bits(s, tm_size) ^ row) * pred_width, pred_width)
            pred_out[s] = pred_acc[pl.ds(start, pred_width), :].T[:columns, :]


def whole(shape):
    return pl.BlockSpec(shape, lambda i, *_: (0,) * len(shape))


def run_forward(
    ids, frame_count, label_count, enc, pred, side, alpha, beta, weight_t, bias, split, tm_size, label_size
):
    columns, frames = alpha.shape
    vocab, width = weight_t.shape
    cells = GROUP * frames
    operands = (enc, pred, side, alpha, beta, weight_t, bias)
    out_shape = [
        jax.ShapeDtypeStruct((width + 16, columns * frames), jnp.bfloat16),
        jax.ShapeDtypeStruct((vocab, columns * frames), jnp.bfloat16),
    ]
    out_specs = [
        pl.BlockSpec((width + 16, cells), lambda i, *_: (0, i)),
        pl.BlockSpec((vocab, cells), lambda i, *_: (0, i)),
    ]
    count, rows = (2, width // 2 + 8) if split else (1, width + 8)
    for _ in range(count):
        out_shape.append(jax.ShapeDtypeStruct((rows, vocab), jnp.float32))
        out_specs.append(whole((rows, vocab)))
    return pl.pallas_call(
        functools.partial(forward_kernel, tm_size=tm_size, label_size=label_size),
        grid_spec=pltpu.PrefetchScalarGridSpec(
            num_scalar_prefetch=3,
            grid=(columns // GROUP,),
            in_specs=[whole(x.shape) for x in operands],
            out_specs=out_specs,
            scratch_shapes=[
                pltpu.VMEM((width, frames), jnp.float32),
                pltpu.VMEM((width, LANES), jnp.float32),
                pltpu.VMEM((vocab, frames), jnp.float32),
                pltpu.VMEM((columns, frames), jnp.float32),
                pltpu.VMEM((columns, frames), jnp.float32),
                pltpu.VMEM((columns, frames), jnp.float32),
                pltpu.VMEM((GROUP, vocab, frames), jnp.float32),
                pltpu.VMEM((width + 16, vocab), jnp.float32),
            ],
        ),
        out_shape=out_shape,
        name="forward",
    )(ids, frame_count, label_count, *operands)


def run_backward(act, grad, weight, frames, columns, tm_size, label_size):
    width, vocab = weight.shape
    cells = GROUP * frames
    enc_shape = (label_size, frames, width // label_size)
    pred_shape = (tm_size, columns, width // tm_size)
    return pl.pallas_call(
        functools.partial(
            backward_kernel, tm_size=tm_size, label_size=label_size, columns=columns
        ),
        grid=(columns // GROUP,),
        in_specs=[
            pl.BlockSpec((width, cells), lambda i: (0, i)),
            pl.BlockSpec((vocab, cells), lambda i: (0, i)),
            whole((width, vocab)),
        ],
        out_specs=[whole(enc_shape), whole(pred_shape)],
        scratch_shapes=[
            pltpu.VMEM((width, cells), jnp.float32),
            pltpu.VMEM((width, frames), jnp.float32),
            pltpu.VMEM((width, LANES), jnp.float32),
        ],
        out_shape=[
            jax.ShapeDtypeStruct(enc_shape, jnp.float32),
            jax.ShapeDtypeStruct(pred_shape, jnp.float32),
        ],
        name="backward",
    )(act, grad, weight)


def per_device(
    encoder_out,
    predictor_out,
    label_ids,
    log_alpha,
    log_beta,
    frame_count,
    label_count,
    joint_weight,
    joint_bias,
):
    frames, columns = encoder_out.shape[1], label_ids.shape[1]
    width, vocab = joint_weight.shape
    tm_size, label_size = lax.axis_size("tm"), lax.axis_size("label")
    parts = tm_size * label_size
    rows = width // parts
    row, mine = lax.axis_index("tm"), lax.axis_index("label")
    alpha, beta = log_alpha[0].T, log_beta[0].T

    side = gather_slots(beta[0:1, :], "label")
    enc = gather_slots(encoder_out[0], "label")
    pred_width = predictor_out.shape[2]
    first_score = side[mine, 0, 0]
    extra = jnp.concatenate(
        [
            jnp.pad(beta[:, 0][None, :], ((0, 0), (0, pred_width - columns))),
            jnp.broadcast_to(first_score, (7, pred_width)),
        ],
        axis=0,
    )
    pred = gather_slots(
        jnp.concatenate([predictor_out[0].astype(jnp.float32), extra], axis=0), "tm"
    )
    split = rows % 8 == 0
    act, grad, *weight_parts = run_forward(
        label_ids,
        frame_count,
        label_count,
        enc,
        pred,
        side,
        alpha,
        beta,
        joint_weight.T,
        joint_bias[None, :],
        split,
        tm_size,
        label_size,
    )
    if split:
        keep, send = weight_parts
        keep, bias_sum = keep[: width // 2], keep[width // 2 :]
    else:
        total, bias_sum = weight_parts[0][:width], weight_parts[0][width:]
        slots = total.reshape(tm_size, label_size, rows, vocab)
        for axis, size, index in ((0, tm_size, row), (1, label_size, mine)):
            order = jnp.array([reverse_bits(s, size) for s in range(size)], jnp.int32) ^ index
            slots = jnp.take(slots, order, axis=axis)
        slots = jnp.swapaxes(slots, 0, 1).reshape(width, vocab)
        keep, send = slots[: width // 2], slots[width // 2 :]
        send = jnp.concatenate([send, bias_sum], axis=0)

    stages = [("label", bit) for bit in bits_of(label_size)] + [("tm", bit) for bit in bits_of(tm_size)]
    first = swap(send, *stages[0])
    enc_slots, pred_slots = run_backward(
        act, grad, joint_weight, frames, columns, tm_size, label_size
    )
    arrived = first
    for i, _ in enumerate(stages):
        count = keep.shape[0]
        keep, bias_sum = keep + arrived[:count], bias_sum + arrived[count:]
        if i + 1 < len(stages):
            half = count // 2
            send = jnp.concatenate([keep[half:], bias_sum], axis=0)
            keep = keep[:half]
            arrived = swap(send, *stages[i + 1])
    final = jnp.concatenate([keep, bias_sum], axis=0)
    for bit in bits_of(lax.axis_size("dp")):
        final = final + swap(final, "dp", bit)
    weight_gradient = final[:rows]
    bias_rows = vocab // parts
    position = row * label_size + mine
    bias_gradient = lax.dynamic_slice_in_dim(final[rows], position * bias_rows, bias_rows, 0)

    encoder_gradient = scatter_slots(enc_slots, "label")[None]
    predictor_gradient = scatter_slots(pred_slots, "tm")[None]
    return (encoder_gradient, predictor_gradient, weight_gradient, bias_gradient)


def solution(mesh):
    return jax.shard_map(
        per_device,
        mesh=mesh,
        in_specs=(
            P("dp", "tm", "label"),
            P("dp", "label", "tm"),
            P("dp", "label"),
            P("dp", "tm", "label"),
            P("dp", "tm", "label"),
            P("dp"),
            P("dp"),
            P(),
            P(),
        ),
        out_specs=(
            P("dp", "tm", "label"),
            P("dp", "label", "tm"),
            P(("tm", "label"), None),
            P(("tm", "label")),
        ),
        check_vma=False,
    )
```

time: 287 us -> 80.7 us (0.28)
  blocking collectives: 93.1 us -> 0 us
  waiting for transfers between devices: 90.3 us -> 15.8 us
  Pallas kernels: 0 us -> 27.9 us
  other arithmetic: 36.4 us -> 8.54 us
  local copies, waits for them, and re-layouts: 27.2 us -> 7.74 us
  starting transfers between devices: 2.69 us -> 17.7 us
  between operations: 16.3 us -> 2.09 us
  matrix products: 13.2 us -> 0 us
  loops' own time: 6.44 us -> 0 us
    psum x1 -> x0, waiting for transfers between devices: 89.2 us -> none  [per_device(): lax.psum((weight_sum, bias_sum), ('dp', 'tm', 'label'))]
    psum x2 -> x0, blocking collectives: 75.4 us -> none  [the longest x1 37.9 us: per_device(): lax.psum((weight_sum, bias_sum), ('dp', 'tm', 'label'))]
    pallas_call x0 -> x2, Pallas kernels: none -> 27.9 us  [the longest x1 18.3 us: run_forward(): pl.pallas_call(functools.partial(forward_kernel, tm_size=tm_size, label_s...]
    all_gather x2 -> x0, blocking collectives: 17.7 us -> none  [the longest x1 12.1 us: per_device(): label_full = lax.all_gather(predictor_out, 'tm', axis=2, tiled=True)]
    ppermute x2 -> x15, waiting for transfers between devices: 0.01 us -> 15.8 us  [swap(): lax.ppermute(value, axis, [(i, i ^ bit) for i in range(lax.axis_size(axis...]
    ppermute x2 -> x15, starting transfers between devices: 2.57 us -> 17.7 us  [swap(): lax.ppermute(value, axis, [(i, i ^ bit) for i in range(lax.axis_size(axis...]
    dot_general x24 -> x0, matrix products: 13.2 us -> none  [the longest x8 4.87 us: lattice(): lax.dot_general(joint_act, logit_gradient, (((0,), (0,)), ((), ())), pref...]
    select_n x16 -> x0, other arithmetic: 10.6 us -> none  [the longest x8 5.32 us: lattice(): jnp.where(blank_live, jnp.exp(alpha_rows + blank_score + after_blank - sc...]
  transfers between devices with their start and end apart: 5 -> 15, of which waited for: 1 -> 11; matrix products, arithmetic and copies ran while one was open for 2% -> 12% of each run, Pallas kernels for 0% -> 12%
where the time goes in v1:
time: 80.7 us; the launch traced here: 79.8 us
  Pallas kernels  27.9 us (35%)
  starting transfers between devices  17.7 us (22%)
  waiting for transfers between devices  15.8 us (20%)
  other arithmetic  8.54 us (11%)
  local copies, waits for them, and re-layouts  7.74 us (10%)
  between operations  2.09 us (3%)
    pallas_call x1, Pallas kernels, run_forward(): pl.pallas_call(functools.partial(forward_kernel, tm_size=tm_size, label_s...  18.3 us
    ppermute x15, starting transfers between devices, swap(): lax.ppermute(value, axis, [(i, i ^ bit) for i in range(lax.axis_size(axis...  17.7 us
    ppermute x15, waiting for transfers between devices, swap(): lax.ppermute(value, axis, [(i, i ^ bit) for i in range(lax.axis_size(axis...  15.8 us
    pallas_call x1, Pallas kernels, run_backward(): pl.pallas_call(functools.partial(backward_kernel, tm_size=tm_size, label_...  9.57 us
    add x4, other arithmetic, scatter_slots(): slots = slots[:half] + swap(slots[half:], axis, bit)  2.94 us
    concatenate x6, other arithmetic, gather_slots(): slots = jnp.concatenate([slots, swap(slots, axis, bit)], axis=0)  2.83 us
    unnamed x3, local copies, waits for them, and re-layouts  2.05 us
    add x8, other arithmetic, per_device(): keep, bias_sum = (keep + arrived[:count], bias_sum + arrived[count:])  1.93 us
  transfers between devices with their start and end apart: 15, of which 11 were waited for; matrix products, arithmetic and copies ran while one was open for 12% of the time, Pallas kernels for 12%

profile of v1, /device:TPU:0, one launch (start us, length us, event | category | flops | bytes accessed | tf_op | source)
XLA Modules:
  0.0 79.8 jit_solution(13423735234445152300)
XLA Ops:
  0.6 0.7 slice_bitcast_fusion
  1.8 0.7 bitcast_convert_fusion
  2.6 2.8 %collective-permute-start.3 = (f32[2,1,128]{2,1,0:T(1,128)S(1)}, f32[2,1,128]{2,1,0:T(1,128)S(1)}, u32[]{:S(2)}, u32[]{:S(2)}) collective-permute-start(f32[2,1,128]{2,1,0:T(1,128)S(1)} %pad_maximum_fusion.9), channel_id=1, source_target_pairs={{0,2},{1,3},{2,0},{3,1},{4,6},{5,7},{6,4},{7,5},{8,10},{9,11},{10,... | collective-permute-start | bytes 3080 | tf_op jit(solution)/shard_map/ppermute | solution.py:29
  5.5 0.8 %slice_reduce_fusion = f32[32]{0:T(128)S(1)} fusion(f32[32,128]{1,0:T(8,128)} %bitcast.21), kind=kLoop, calls=%fused_computation.26 | loop fusion | bytes 256 | tf_op jit(solution)/shard_map/slice | solution.py:326
  6.3 0.7 collective-permute-done.3
  7.5 0.6 broadcast_in_dim.13
  8.3 2.1 %collective-permute-start.4 = (f32[1,40,128]{2,1,0:T(8,128)S(1)}, f32[1,40,128]{2,1,0:T(8,128)S(1)}, u32[]{:S(2)}, u32[]{:S(2)}) collective-permute-start(f32[1,40,128]{2,1,0:T(8,128)S(1)} %fusion.1), channel_id=1, source_target_pairs={{0,4},{4,0},{8,12},{12,8},{1,5},{5,1},{9,13},{13,9},{2,6},{6,2},{1... | collective-permute-start | bytes 61448 | tf_op jit(solution)/shard_map/ppermute | solution.py:29
  11.8 2.0 %copy.14 = bf16[512,512]{0,1:T(8,128)(2,1)} copy(bf16[512,512]{1,0:T(8,128)(2,1)} %w_ref.1) | data formatting | bytes 1048576 | tf_op args[7]
  13.8 2.6 %collective-permute-start.5 = (f32[2,40,128]{2,1,0:T(8,128)S(1)}, f32[2,40,128]{2,1,0:T(8,128)S(1)}, u32[]{:S(2)}, u32[]{:S(2)}) collective-permute-start(f32[2,40,128]{2,1,0:T(8,128)S(1)} %pad_maximum_fusion.7), channel_id=1, source_target_pairs={{0,8},{4,12},{8,0},{12,4},{1,9},{5,13},{9,1},{13,5},{2,10},{6,14},... | collective-permute-start | bytes 122888 | tf_op jit(solution)/shard_map/ppermute | solution.py:29
  16.5 0.8 pad_maximum_fusion.6
  17.2 1.5 %collective-permute-start.1 = (bf16[2,128,128]{2,1,0:T(8,128)(2,1)S(1)}, bf16[2,128,128]{2,1,0:T(8,128)(2,1)S(1)}, u32[]{:S(2)}, u32[]{:S(2)}) collective-permute-start(bf16[2,128,128]{2,1,0:T(8,128)(2,1)S(1)} %pad_maximum_fusion.6), channel_id=1, source_target_pairs={{0,2},{1,3},{2,0},{3,1},{4,6},{5,7},{6,4},{7,5},{8,10},{9,11},{10,... | collective-permute-start | bytes 196616 | tf_op jit(solution)/shard_map/ppermute | solution.py:29
  18.7 0.7 collective-permute-done.5
  19.5 0.6 pad_maximum_fusion.3.pred_ref
  20.1 1.4 %collective-permute-done.1 = bf16[2,128,128]{2,1,0:T(8,128)(2,1)S(1)} collective-permute-done((bf16[2,128,128]{2,1,0:T(8,128)(2,1)S(1)}, bf16[2,128,128]{2,1,0:T(8,128)(2,1)S(1)}, u32[]{:S(2)}, u32[]{:S(2)}) %collective-permute-start.1) | collective-permute-done | bytes 65568 | tf_op jit(solution)/shard_map/ppermute | solution.py:29
  21.5 1.4 %pad_maximum_fusion.2.enc_ref = bf16[4,128,128]{2,1,0:T(8,128)(2,1)} fusion(bf16[2,128,128]{2,1,0:T(8,128)(2,1)S(1)} %collective-permute-done.1, bf16[1,128,128]{2,1,0:T(8,128)(2,1)S(1)} %collective-permute-done, bf16[1,128,128]{2,1,0:T(8,128)(2,1)} %param.9), kind=kLoop, calls=%fused_computation.5 | loop fusion | flops 131072 | bytes 262144 | tf_op jit(solution)/shard_map/concatenate | solution.py:35
  22.9 18.3 %forward.1 = (bf16[528,4096]{1,0:T(8,128)(2,1)}, bf16[512,4096]{1,0:T(8,128)(2,1)}, f32[264,512]{1,0:T(8,128)}, f32[264,512]{1,0:T(8,128)}) custom-call(s32[1,32]{1,0:T(1,128)} %ids_ref.1, s32[1]{0:T(128)S(6)} %copy.15.frames_ref, s32[1]{0:T(128)S(6)} %copy.16.labels_ref, bf16[4,128,128]{2,1,0:T(8,128)(2,1)} %pad_maximum_fusion.2.enc_ref, ...), custom_call_target="tpu_custom_call" | custom-call | tf_op jit(solution)/shard_map/forward/pallas_call | solution.py:249
  41.3 2.1 %collective-permute-done.10 = f32[264,512]{1,0:T(8,128)S(1)} collective-permute-done((f32[264,512]{1,0:T(8,128)}, f32[264,512]{1,0:T(8,128)S(1)}, u32[]{:S(2)}, u32[]{:S(2)}) %collective-permute-start.10) | collective-permute-done | bytes 540704 | tf_op jit(solution)/shard_map/ppermute | solution.py:29
  43.5 1.1 %slice_add_fusion = f32[256,512]{1,0:T(8,128)S(1)} fusion(f32[264,512]{1,0:T(8,128)S(1)} %collective-permute-done.10, f32[264,512]{1,0:T(8,128)} %get-tuple-element.14), kind=kLoop, calls=%fused_computation | loop fusion | flops 131072 | bytes 1572864 | tf_op jit(solution)/shard_map/add | solution.py:371
  44.6 0.7 slice_add_fusion.10
  45.4 1.6 %collective-permute-start.11 = (f32[136,512]{1,0:T(8,128)S(1)}, f32[136,512]{1,0:T(8,128)S(1)}, u32[]{:S(2)}, u32[]{:S(2)}) collective-permute-start(f32[136,512]{1,0:T(8,128)S(1)} %pad_maximum_fusion), channel_id=1, source_target_pairs={{0,2},{1,3},{2,0},{3,1},{4,6},{5,7},{6,4},{7,5},{8,10},{9,11},{10,... | collective-permute-start | bytes 835592 | tf_op jit(solution)/shard_map/ppermute | solution.py:29
  46.9 9.6 %backward.1 = (f32[4,128,128]{2,1,0:T(8,128)}, f32[4,32,128]{2,1,0:T(8,128)}) custom-call(bf16[528,4096]{1,0:T(8,128)(2,1)} %get-tuple-element.10.act_ref, bf16[512,4096]{1,0:T(8,128)(2,1)} %get-tuple-element.11.grad_ref, bf16[512,512]{1,0:T(8,128)(2,1)} %w_ref.1), custom_call_target="tpu_custom_call" | custom-call | tf_op jit(solution)/shard_map/backward/pallas_call | solution.py:277
  56.5 0.8 slice.91
  57.7 0.9 %slice.87 = f32[2,128,128]{2,1,0:T(8,128)S(1)} slice(f32[4,128,128]{2,1,0:T(8,128)} %get-tuple-element.12), slice={[2:4], [0:128], [0:128]} | slice | bytes 262144 | tf_op jit(solution)/shard_map/slice | solution.py:42
  58.7 2.5 %collective-permute-done.8 = f32[2,32,128]{2,1,0:T(8,128)S(1)} collective-permute-done((f32[2,32,128]{2,1,0:T(8,128)S(1)}, f32[2,32,128]{2,1,0:T(8,128)S(1)}, u32[]{:S(2)}, u32[]{:S(2)}) %collective-permute-start.8) | collective-permute-done | bytes 32800 | tf_op jit(solution)/shard_map/ppermute | solution.py:29
  61.2 0.8 slice_add_fusion.6
  63.1 3.7 %collective-permute-done.9 = f32[1,32,128]{2,1,0:T(8,128)S(1)} collective-permute-done((f32[1,32,128]{2,1,0:T(8,128)S(1)}, f32[1,32,128]{2,1,0:T(8,128)S(1)}, u32[]{:S(2)}, u32[]{:S(2)}) %collective-permute-start.9) | collective-permute-done | bytes 16416 | tf_op jit(solution)/shard_map/ppermute | solution.py:29
  68.0 2.8 %collective-permute-start.13 = (f32[40,512]{1,0:T(8,128)S(1)}, f32[40,512]{1,0:T(8,128)S(1)}, u32[]{:S(2)}, u32[]{:S(2)}) collective-permute-start(f32[40,512]{1,0:T(8,128)S(1)} %pad_maximum_fusion.4), channel_id=1, source_target_pairs={{0,8},{4,12},{8,0},{12,4},{1,9},{5,13},{9,1},{13,5},{2,10},{6,14},... | collective-permute-start | bytes 245768 | tf_op jit(solution)/shard_map/ppermute | solution.py:29
  70.8 0.9 %slice_add_fusion.3 = f32[2,128,128]{2,1,0:T(8,128)S(1)} fusion(f32[2,128,128]{2,1,0:T(8,128)S(1)} %collective-permute-done.6, f32[4,128,128]{2,1,0:T(8,128)} %get-tuple-element.12), kind=kLoop, calls=%fused_computation.6 | loop fusion | flops 32768 | bytes 393216 | tf_op jit(solution)/shard_map/add | solution.py:42
  72.4 1.6 %collective-permute-done.13 = f32[40,512]{1,0:T(8,128)S(1)} collective-permute-done((f32[40,512]{1,0:T(8,128)S(1)}, f32[40,512]{1,0:T(8,128)S(1)}, u32[]{:S(2)}, u32[]{:S(2)}) %collective-permute-start.13) | collective-permute-done | bytes 81952 | tf_op jit(solution)/shard_map/ppermute | solution.py:29
  74.0 1.6 %collective-permute-start.14 = (f32[40,512]{1,0:T(8,128)S(1)}, f32[40,512]{1,0:T(8,128)S(1)}, u32[]{:S(2)}, u32[]{:S(2)}) collective-permute-start(f32[40,512]{1,0:T(8,128)S(1)} %pad_maximum_fusion.5), channel_id=1, source_target_pairs={{0,16},{16,0},{1,17},{17,1},{2,18},{18,2},{3,19},{19,3},{4,20},{20... | collective-permute-start | bytes 245768 | tf_op jit(solution)/shard_map/ppermute | solution.py:29
  76.1 0.6 slice_add_fusion.5
  76.7 1.8 %collective-permute-done.14 = f32[40,512]{1,0:T(8,128)S(1)} collective-permute-done((f32[40,512]{1,0:T(8,128)S(1)}, f32[40,512]{1,0:T(8,128)S(1)}, u32[]{:S(2)}, u32[]{:S(2)}) %collective-permute-start.14) | collective-permute-done | bytes 81952 | tf_op jit(solution)/shard_map/ppermute | solution.py:29
  (43 shorter events, 6.6 us)
Async XLA Ops:
  1.3 1.3 %collective-permute-start.2 = (f32[1,1,128]{2,1,0:T(1,128)S(1)}, f32[1,1,128]{2,1,0:T(1,128)S(1)}, u32[]{:S(2)}, u32[]{:S(2)}) collective-permute-start(f32[1,1,128]{2,1,0:T(1,128)S(1)} %slice_bitcast_fusion), channel_id=1, source_target_pairs={{0,1},{1,0},{2,3},{3,2},{4,5},{5,4},{6,7},{7,6},{8,9},{9,8},{10,11... | collective-permute-start | bytes 1544 | tf_op jit(solution)/shard_map/ppermute | solution.py:29
  2.6 4.4 %collective-permute-start.3 = (f32[2,1,128]{2,1,0:T(1,128)S(1)}, f32[2,1,128]{2,1,0:T(1,128)S(1)}, u32[]{:S(2)}, u32[]{:S(2)}) collective-permute-start(f32[2,1,128]{2,1,0:T(1,128)S(1)} %pad_maximum_fusion.9), channel_id=1, source_target_pairs={{0,2},{1,3},{2,0},{3,1},{4,6},{5,7},{6,4},{7,5},{8,10},{9,11},{10,... | collective-permute-start | bytes 3080 | tf_op jit(solution)/shard_map/ppermute | solution.py:29
  7.0 15.9 %copy-start = (f32[4,1,128]{2,1,0:T(1,128)}, f32[4,1,128]{2,1,0:T(1,128)S(1)}, u32[]{:S(2)}) copy-start(f32[4,1,128]{2,1,0:T(1,128)S(1)} %pad_maximum_fusion.8.side_ref) | copy-start | bytes 6148
  8.3 5.5 %collective-permute-start.4 = (f32[1,40,128]{2,1,0:T(8,128)S(1)}, f32[1,40,128]{2,1,0:T(8,128)S(1)}, u32[]{:S(2)}, u32[]{:S(2)}) collective-permute-start(f32[1,40,128]{2,1,0:T(8,128)S(1)} %fusion.1), channel_id=1, source_target_pairs={{0,4},{4,0},{8,12},{12,8},{1,5},{5,1},{9,13},{13,9},{2,6},{6,2},{1... | collective-permute-start | bytes 61448 | tf_op jit(solution)/shard_map/ppermute | solution.py:29
  10.4 6.0 %collective-permute-start = (bf16[1,128,128]{2,1,0:T(8,128)(2,1)}, bf16[1,128,128]{2,1,0:T(8,128)(2,1)S(1)}, u32[]{:S(2)}, u32[]{:S(2)}) collective-permute-start(bf16[1,128,128]{2,1,0:T(8,128)(2,1)} %param.9), channel_id=1, source_target_pairs={{0,1},{1,0},{2,3},{3,2},{4,5},{5,4},{6,7},{7,6},{8,9},{9,8},{10,11... | collective-permute-start | bytes 98312 | tf_op jit(solution)/shard_map/ppermute | solution.py:29
  13.8 5.7 %collective-permute-start.5 = (f32[2,40,128]{2,1,0:T(8,128)S(1)}, f32[2,40,128]{2,1,0:T(8,128)S(1)}, u32[]{:S(2)}, u32[]{:S(2)}) collective-permute-start(f32[2,40,128]{2,1,0:T(8,128)S(1)} %pad_maximum_fusion.7), channel_id=1, source_target_pairs={{0,8},{4,12},{8,0},{12,4},{1,9},{5,13},{9,1},{13,5},{2,10},{6,14},... | collective-permute-start | bytes 122888 | tf_op jit(solution)/shard_map/ppermute | solution.py:29
  17.2 4.3 %collective-permute-start.1 = (bf16[2,128,128]{2,1,0:T(8,128)(2,1)S(1)}, bf16[2,128,128]{2,1,0:T(8,128)(2,1)S(1)}, u32[]{:S(2)}, u32[]{:S(2)}) collective-permute-start(bf16[2,128,128]{2,1,0:T(8,128)(2,1)S(1)} %pad_maximum_fusion.6), channel_id=1, source_target_pairs={{0,2},{1,3},{2,0},{3,1},{4,6},{5,7},{6,4},{7,5},{8,10},{9,11},{10,... | collective-permute-start | bytes 196616 | tf_op jit(solution)/shard_map/ppermute | solution.py:29
  41.2 2.2 %collective-permute-start.10 = (f32[264,512]{1,0:T(8,128)}, f32[264,512]{1,0:T(8,128)S(1)}, u32[]{:S(2)}, u32[]{:S(2)}) collective-permute-start(f32[264,512]{1,0:T(8,128)} %get-tuple-element.15), channel_id=1, source_target_pairs={{0,1},{1,0},{2,3},{3,2},{4,5},{5,4},{6,7},{7,6},{8,9},{9,8},{10,11... | collective-permute-start | bytes 1622024 | tf_op jit(solution)/shard_map/ppermute | solution.py:29
  45.4 17.1 %collective-permute-start.11 = (f32[136,512]{1,0:T(8,128)S(1)}, f32[136,512]{1,0:T(8,128)S(1)}, u32[]{:S(2)}, u32[]{:S(2)}) collective-permute-start(f32[136,512]{1,0:T(8,128)S(1)} %pad_maximum_fusion), channel_id=1, source_target_pairs={{0,2},{1,3},{2,0},{3,1},{4,6},{5,7},{6,4},{7,5},{8,10},{9,11},{10,... | collective-permute-start | bytes 835592 | tf_op jit(solution)/shard_map/ppermute | solution.py:29
  57.2 3.9 %collective-permute-start.8 = (f32[2,32,128]{2,1,0:T(8,128)S(1)}, f32[2,32,128]{2,1,0:T(8,128)S(1)}, u32[]{:S(2)}, u32[]{:S(2)}) collective-permute-start(f32[2,32,128]{2,1,0:T(8,128)S(1)} %slice.91), channel_id=1, source_target_pairs={{0,4},{4,0},{8,12},{12,8},{1,5},{5,1},{9,13},{13,9},{2,6},{6,2},{1... | collective-permute-start | bytes 98312 | tf_op jit(solution)/shard_map/ppermute | solution.py:29
  58.6 12.2 %collective-permute-start.6 = (f32[2,128,128]{2,1,0:T(8,128)S(1)}, f32[2,128,128]{2,1,0:T(8,128)S(1)}, u32[]{:S(2)}, u32[]{:S(2)}) collective-permute-start(f32[2,128,128]{2,1,0:T(8,128)S(1)} %slice.87), channel_id=1, source_target_pairs={{0,1},{1,0},{2,3},{3,2},{4,5},{5,4},{6,7},{7,6},{8,9},{9,8},{10,11... | collective-permute-start | bytes 393224 | tf_op jit(solution)/shard_map/ppermute | solution.py:29
  61.9 4.9 %collective-permute-start.9 = (f32[1,32,128]{2,1,0:T(8,128)S(1)}, f32[1,32,128]{2,1,0:T(8,128)S(1)}, u32[]{:S(2)}, u32[]{:S(2)}) collective-permute-start(f32[1,32,128]{2,1,0:T(8,128)S(1)} %slice.117), channel_id=1, source_target_pairs={{0,8},{4,12},{8,0},{12,4},{1,9},{5,13},{9,1},{13,5},{2,10},{6,14},... | collective-permute-start | bytes 49160 | tf_op jit(solution)/shard_map/ppermute | solution.py:29
  62.5 5.4 %collective-permute-start.12 = (f32[72,512]{1,0:T(8,128)S(1)}, f32[72,512]{1,0:T(8,128)S(1)}, u32[]{:S(2)}, u32[]{:S(2)}) collective-permute-start(f32[72,512]{1,0:T(8,128)S(1)} %pad_maximum_fusion.1), channel_id=1, source_target_pairs={{0,4},{4,0},{8,12},{12,8},{1,5},{5,1},{9,13},{13,9},{2,6},{6,2},{1... | collective-permute-start | bytes 442376 | tf_op jit(solution)/shard_map/ppermute | solution.py:29
  68.0 6.0 %collective-permute-start.13 = (f32[40,512]{1,0:T(8,128)S(1)}, f32[40,512]{1,0:T(8,128)S(1)}, u32[]{:S(2)}, u32[]{:S(2)}) collective-permute-start(f32[40,512]{1,0:T(8,128)S(1)} %pad_maximum_fusion.4), channel_id=1, source_target_pairs={{0,8},{4,12},{8,0},{12,4},{1,9},{5,13},{9,1},{13,5},{2,10},{6,14},... | collective-permute-start | bytes 245768 | tf_op jit(solution)/shard_map/ppermute | solution.py:29
  71.8 4.3 %collective-permute-start.7 = (f32[1,128,128]{2,1,0:T(8,128)S(1)}, f32[1,128,128]{2,1,0:T(8,128)S(1)}, u32[]{:S(2)}, u32[]{:S(2)}) collective-permute-start(f32[1,128,128]{2,1,0:T(8,128)S(1)} %slice.115), channel_id=1, source_target_pairs={{0,2},{1,3},{2,0},{3,1},{4,6},{5,7},{6,4},{7,5},{8,10},{9,11},{10,... | collective-permute-start | bytes 196616 | tf_op jit(solution)/shard_map/ppermute | solution.py:29
  74.0 4.5 %collective-permute-start.14 = (f32[40,512]{1,0:T(8,128)S(1)}, f32[40,512]{1,0:T(8,128)S(1)}, u32[]{:S(2)}, u32[]{:S(2)}) collective-permute-start(f32[40,512]{1,0:T(8,128)S(1)} %pad_maximum_fusion.5), channel_id=1, source_target_pairs={{0,16},{16,0},{1,17},{17,1},{2,18},{18,2},{3,19},{19,3},{4,20},{20... | collective-permute-start | bytes 245768 | tf_op jit(solution)/shard_map/ppermute | solution.py:29

commit v2 on v0

v2 whole, which is shorter than its diff:
```python
import functools

import jax
import jax.numpy as jnp
from jax import lax
from jax.experimental import pallas as pl
from jax.experimental.pallas import tpu as pltpu
from jax.sharding import PartitionSpec as P

GROUP = 4
CHUNK = 16
LANES = 128
FAR = -1e30
MIB = 1 << 20


def bits_of(size):
    return [1 << i for i in range(size.bit_length() - 1)]


def reverse_bits(value, size):
    width = size.bit_length() - 1
    result = 0
    for i in range(width):
        result = result | (((value >> i) & 1) << (width - 1 - i))
    return result


def swap(value, axis, bit):
    return lax.ppermute(value, axis, [(i, i ^ bit) for i in range(lax.axis_size(axis))])


def gather_slots(value, axis):
    return [value] + [swap(value, axis, s) for s in range(1, lax.axis_size(axis))]


def vmem():
    return pl.BlockSpec(memory_space=pltpu.VMEM)


def loaded(kernel, loads, outputs):
    def body(*refs):
        sources, others, outs = refs[:loads], refs[loads:-loads - 1 - outputs], refs[-loads - 1 - outputs : -loads - 1]
        targets, done = refs[-loads - 1 : -1], refs[-1]
        copies = [
            pltpu.make_async_copy(source, target, done.at[i])
            for i, (source, target) in enumerate(zip(sources, targets))
        ]
        for copy in copies:
            copy.start()
        for copy in copies:
            copy.wait()
        kernel(*targets, *others, *outs)

    return body


def call(kernel, out_shape, operands, scratch=(), scalars=0, loads=0, limit=16, flops=0):
    resident = len(operands) - scalars - loads
    scratch = list(scratch)
    operands = list(operands)
    for i in range(scalars, scalars + loads):
        operands[i] = pltpu.with_memory_space_constraint(operands[i], pltpu.HBM)
    if loads:
        kernel = loaded(kernel, loads, len(out_shape))
        scratch += [pltpu.VMEM(x.shape, x.dtype) for x in operands[scalars : scalars + loads]]
        scratch.append(pltpu.SemaphoreType.DMA((loads,)))
    return pl.pallas_call(
        kernel,
        grid_spec=pltpu.PrefetchScalarGridSpec(
            num_scalar_prefetch=scalars,
            grid=(1,),
            in_specs=[pl.BlockSpec(memory_space=pltpu.HBM)] * loads + [vmem()] * resident,
            out_specs=[vmem()] * len(out_shape),
            scratch_shapes=scratch,
        ),
        out_shape=out_shape,
        compiler_params=pltpu.CompilerParams(vmem_limit_bytes=limit * MIB),
        cost_estimate=pl.CostEstimate(flops=flops, bytes_accessed=0, transcendentals=0) if flops else None,
    )(*operands)


def pack_encoder(enc_ref, beta_ref, out_ref):
    frames = enc_ref.shape[0]
    first = beta_ref[0:1, :]
    high = first.astype(jnp.bfloat16).astype(jnp.float32)
    middle = (first - high).astype(jnp.bfloat16).astype(jnp.float32)
    low = first - high - middle
    pieces = jnp.concatenate([high, middle, low, jnp.zeros((13, frames), jnp.float32)], axis=0)
    out_ref[:frames, :] = enc_ref[...]
    out_ref[frames:, :] = pieces.astype(jnp.bfloat16)


def side_line(ref, packed):
    if not packed:
        return ref[0:1, :]
    pieces = ref[ref.shape[0] - 16 :, :].astype(jnp.float32)
    return pieces[0:1, :] + pieces[1:2, :] + pieces[2:3, :]


def pick(refs, index, packed):
    return sum(jnp.where(index == s, side_line(ref, packed), 0.0) for s, ref in enumerate(refs))


def prepare(
    pred_ref, beta_ref, alpha_ref, w_ref, bias_ref, ids_ref, pred_out, alpha_out, beta_out, w_out, wt_out, bias_t, ids_out
):
    ids_out[...] = ids_ref[...]
    columns = pred_ref.shape[0]
    pred_out[:columns, :] = pred_ref[...].astype(jnp.float32)
    pred_out[columns:, :] = jnp.zeros((8, pred_out.shape[1]), jnp.float32)
    pred_out[columns : columns + 1, :columns] = beta_ref[...].T[0:1, :]
    alpha_out[...] = alpha_ref[...]
    beta_out[...] = beta_ref[...]
    w_out[...] = w_ref[...]
    wt_out[...] = w_ref[...].T
    bias_t[...] = jnp.broadcast_to(bias_ref[...], (bias_t.shape[1], bias_t.shape[0])).T


def pack_predictor(pred_ref, *rest, packed):
    side_refs, out_ref = rest[:-1], rest[-1]
    columns = pred_ref.shape[0] - 8
    out_ref[...] = pred_ref[...]
    score = pick(side_refs, lax.axis_index("label"), packed)[0:1, 0:1]
    out_ref[columns + 1 : columns + 2, :] = jnp.broadcast_to(score, (1, out_ref.shape[1]))


def forward_kernel(*refs, tm_size, label_size, packed, split):
    refs = iter(refs)
    take = lambda count: [next(refs) for _ in range(count)]
    ids_ref, frames_ref, labels_ref, alpha_ref, beta_ref, wt_ref, bias_t = take(7)
    enc_refs, pred_refs = take(label_size), take(tm_size)
    side_refs = enc_refs if packed else take(label_size)
    act_ref, grad_ref = take(2)
    out_refs = take(2 if split else 1)
    enc_t, pred_t, occ_s, blank_s, label_s, acc = take(6)
    lts = list(refs)
    columns, frames = alpha_ref.shape
    vocab, width = wt_ref.shape
    mine, row = lax.axis_index("label"), lax.axis_index("tm")

    enc_width, pred_width = enc_refs[0].shape[1], pred_refs[0].shape[1]
    for s, ref in enumerate(enc_refs):
        start = pl.multiple_of((mine ^ s) * enc_width, enc_width)
        enc_t[pl.ds(start, enc_width), :] = ref[:frames, :].astype(jnp.float32).T
    for s, ref in enumerate(pred_refs):
        start = pl.multiple_of((row ^ s) * pred_width, pred_width)
        pred_t[pl.ds(start, pred_width), :columns] = ref[:columns, :].T

    alpha, beta = alpha_ref[...], beta_ref[...]
    score, below = 0.0, 0.0
    after = row ^ jnp.minimum(row + 1, tm_size - 1)
    for s, ref in enumerate(pred_refs):
        score = score + jnp.where(row == s, ref[columns + 1 : columns + 2, 0:1], 0.0)
        below = below + jnp.where(after == s, ref[columns : columns + 1, :columns], 0.0)
    beside = pick(side_refs, mine ^ jnp.minimum(mine + 1, label_size - 1), packed)
    diagonal = lax.broadcasted_iota(jnp.int32, (columns, columns), 0) == lax.broadcasted_iota(
        jnp.int32, (columns, columns), 1
    )
    below = jnp.sum(jnp.where(diagonal, below, 0.0), axis=1, keepdims=True)
    lane = lax.broadcasted_iota(jnp.int32, (columns, frames), 1)
    line = lax.broadcasted_iota(jnp.int32, (columns, frames), 0)
    down = jnp.where(lane == frames - 1, below, pltpu.roll(beta, frames - 1, 1))
    right = jnp.where(line == columns - 1, beside, pltpu.roll(beta, columns - 1, 0))
    frame, column = row * frames + lane, mine * columns + line
    frame_limit, label_limit = frames_ref[0], labels_ref[0]
    inside = (frame < frame_limit) & (column <= label_limit)
    more = frame + 1 < frame_limit
    occ_s[...] = jnp.where(inside, jnp.exp(alpha + beta - score), 0.0)
    blank_s[...] = jnp.where(
        inside & (more | (column == label_limit)),
        alpha + jnp.where(more, down, 0.0) - score,
        FAR,
    )
    label_s[...] = jnp.where(inside & (column < label_limit), alpha + right - score, FAR)

    act_ref[width:, :] = jnp.ones((act_ref.shape[0] - width, columns * frames), jnp.bfloat16)
    groups = columns // GROUP
    cells = GROUP * frames
    peaks = {}

    def column_of(g, j):
        return reverse_bits(g, groups) + groups * j

    def activate(g):
        for j in range(GROUP):
            u, at = column_of(g, j), (g * GROUP + j) * frames
            for c in range(0, width, 64):
                total = enc_t[c : c + 64, :] + pred_t[c : c + 64, u : u + 1]
                act_ref[c : c + 64, at : at + frames] = jnp.tanh(total).astype(jnp.bfloat16)

    def score_logits(g):
        product = jnp.dot(
            wt_ref[...],
            act_ref[:width, g * cells : (g + 1) * cells],
            preferred_element_type=jnp.float32,
        )
        for j in range(GROUP):
            lt = lts[(g % 2) * GROUP + j]
            logits = product[:, j * frames : (j + 1) * frames] + bias_t[...]
            lt[...] = logits
            peaks[g, j] = jnp.max(logits, axis=0, keepdims=True)

    place = lax.broadcasted_iota(jnp.int32, (CHUNK, frames), 0)

    def differentiate(g):
        for j in range(GROUP):
            u, at = column_of(g, j), (g * GROUP + j) * frames
            lt, peak = lts[(g % 2) * GROUP + j], peaks[g, j]
            here = slice(at, at + frames)
            label = ids_ref[0, u]
            blank_logit, label_logit = lt[0:1, :], lt[pl.ds(label, 1), :]
            total = jnp.zeros((8, frames), jnp.float32)
            for c in range(0, vocab, CHUNK):
                lifted = jnp.exp(lt[c : c + CHUNK, :] - peak)
                lt[c : c + CHUNK, :] = lifted
                total = total + (lifted[:8, :] + lifted[8:, :])
            total = jnp.sum(total, axis=0, keepdims=True)
            log_total = peak + jnp.log(total)
            scale = occ_s[u : u + 1, :] / total
            blank_weight = jnp.exp(blank_s[u : u + 1, :] + (blank_logit - log_total))
            label_weight = jnp.exp(label_s[u : u + 1, :] + (label_logit - log_total))
            for c in range(0, vocab, CHUNK):
                grad_ref[c : c + CHUNK, here] = (lt[c : c + CHUNK, :] * scale).astype(jnp.bfloat16)
            for first in (0, pl.multiple_of((label // CHUNK) * CHUNK, CHUNK)):
                value = lt[pl.ds(first, CHUNK), :] * scale
                value = value - jnp.where(place + first == 0, blank_weight, 0.0)
                value = value - jnp.where(place + first == label, label_weight, 0.0)
                grad_ref[pl.ds(first, CHUNK), here] = value.astype(jnp.bfloat16)

    def accumulate(g, count):
        here = slice(g * cells, (g + count) * cells)
        term = lax.dot_general(
            act_ref[:, here],
            grad_ref[:, here],
            (((1,), (1,)), ((), ())),
            preferred_element_type=jnp.float32,
        )
        acc[...] = term if g == 0 else acc[...] + term

    activate(0)
    score_logits(0)
    for g in range(groups):
        if g + 1 < groups:
            activate(g + 1)
            score_logits(g + 1)
        differentiate(g)
        if g % 2 == 1:
            accumulate(g - 1, 2)

    if not split:
        out_refs[0][...] = acc[: width + 8, :]
        return
    parts = tm_size * label_size
    rows = width // parts
    for s in range(parts):
        label = reverse_bits(s // tm_size, label_size) ^ mine
        tm = reverse_bits(s % tm_size, tm_size) ^ row
        start = pl.multiple_of((tm * label_size + label) * rows, rows)
        to = (s % (parts // 2)) * rows
        out_refs[s // (parts // 2)][to : to + rows, :] = acc[pl.ds(start, rows), :]
    for ref in out_refs:
        ref[width // 2 :, :] = acc[width : width + 8, :]


def lane_swap(value, distance):
    lane = lax.broadcasted_iota(jnp.int32, value.shape, 1)
    return jnp.take_along_axis(value, lane ^ distance, axis=1)


def merge(low, high, distance):
    clear = (lax.broadcasted_iota(jnp.int32, low.shape, 1) & distance) == 0
    return jnp.where(clear, low, high) + lane_swap(jnp.where(clear, high, low), distance)


def backward_kernel(act_ref, grad_ref, w_ref, *rest, tm_size, label_size, columns):
    (enc_keep, enc_send, pred_keep, pred_send), (enc_acc, sums, pieces) = rest[:4], rest[4:]
    width, _ = w_ref.shape
    frames = enc_acc.shape[1]
    cells = GROUP * frames
    groups = columns // GROUP
    for g in range(groups):
        back = jnp.dot(
            w_ref[...], grad_ref[:, g * cells : (g + 1) * cells], preferred_element_type=jnp.float32
        )
        for c in range(0, width, CHUNK):
            act = act_ref[c : c + CHUNK, g * cells : (g + 1) * cells].astype(jnp.float32)
            cell = back[c : c + CHUNK, :] * (1.0 - act * act)
            parts = [cell[:, j * frames : (j + 1) * frames] for j in range(GROUP)]
            total = (parts[0] + parts[1]) + (parts[2] + parts[3])
            enc_acc[c : c + CHUNK, :] = total if g == 0 else enc_acc[c : c + CHUNK, :] + total
            pairs = [merge(parts[0], parts[2], 64), merge(parts[1], parts[3], 64)]
            folded = merge(pairs[0], pairs[1], 32)
            high = folded.astype(jnp.bfloat16)
            low = (folded - high.astype(jnp.float32)).astype(jnp.bfloat16)
            pieces[c : c + CHUNK, 2 * g * LANES : (2 * g + 1) * LANES] = high
            pieces[c : c + CHUNK, (2 * g + 1) * LANES : (2 * g + 2) * LANES] = low

    depth = 2 * groups * LANES
    place = lax.broadcasted_iota(jnp.int32, (depth, LANES), 0)
    lane = lax.broadcasted_iota(jnp.int32, (depth, LANES), 1)
    segment = (place % LANES) // (LANES // GROUP)
    column = sum(
        jnp.where(place // (2 * LANES) == g, reverse_bits(g, groups), 0) for g in range(groups)
    )
    chosen = jnp.where(column + groups * segment == lane, 1.0, 0.0).astype(jnp.bfloat16)
    sums[...] = jnp.dot(pieces[...], chosen, preferred_element_type=jnp.float32)

    mine, row = lax.axis_index("label"), lax.axis_index("tm")
    enc_width, pred_width = enc_keep.shape[2], pred_keep.shape[2]
    for s in range(label_size):
        start = pl.multiple_of((reverse_bits(s, label_size) ^ mine) * enc_width, enc_width)
        ref = (enc_keep, enc_send)[s // (label_size // 2)]
        ref[s % (label_size // 2)] = enc_acc[pl.ds(start, enc_width), :].T
    for s in range(tm_size):
        start = pl.multiple_of((reverse_bits(s, tm_size) ^ row) * pred_width, pred_width)
        ref = (pred_keep, pred_send)[s // (tm_size // 2)]
        ref[s % (tm_size // 2)] = sums[pl.ds(start, pred_width), :].T[:columns, :]


def halve(keep, send, axis):
    for bit in bits_of(lax.axis_size(axis)):
        if send is None:
            half = keep.shape[0] // 2
            keep, send = keep[:half], keep[half:]
        keep, send = keep + swap(send, axis, bit), None
    return keep


def lattice(
    encoder_out,
    predictor_out,
    label_ids,
    log_alpha,
    log_beta,
    frame_count,
    label_count,
    joint_weight,
    joint_bias,
):
    frames, columns = encoder_out.shape[1], label_ids.shape[1]
    width, vocab = joint_weight.shape
    tm_size, label_size = lax.axis_size("tm"), lax.axis_size("label")
    parts = tm_size * label_size
    rows = width // parts
    split = rows % 8 == 0
    row, mine = lax.axis_index("tm"), lax.axis_index("label")
    alpha, beta = log_alpha[0].T, log_beta[0].T
    enc_width, pred_width = encoder_out.shape[2], predictor_out.shape[2]
    f32, bf16 = jnp.float32, jnp.bfloat16
    shape = jax.ShapeDtypeStruct

    packed = enc_width == frames
    payload = encoder_out[0]
    if packed:
        payload = call(
            pack_encoder, [shape((frames + 16, enc_width), bf16)], (payload, beta), loads=2
        )[0]
    encs = gather_slots(payload, "label")
    sides = encs if packed else gather_slots(beta[0:1, :], "label")
    part, alpha, beta, weight, weight_t, bias_t, label_ids = call(
        prepare,
        [
            shape((columns + 8, pred_width), f32),
            shape(alpha.shape, f32),
            shape(beta.shape, f32),
            shape((width, vocab), bf16),
            shape((vocab, width), bf16),
            shape((vocab, frames), f32),
            shape(label_ids.shape, label_ids.dtype),
        ],
        (predictor_out[0], beta, alpha, joint_weight, joint_bias[None, :], label_ids),
        loads=6,
    )
    payload = call(
        functools.partial(pack_predictor, packed=packed),
        [shape((columns + 8, pred_width), f32)],
        (part, *sides),
    )[0]
    preds = gather_slots(payload, "tm")

    cells = columns * frames
    count, part_rows = (2, width // 2 + 8) if split else (1, width + 8)
    operands = [label_ids, frame_count, label_count, alpha, beta, weight_t, bias_t, *encs, *preds]
    act, grad, *weight_parts = call(
        functools.partial(
            forward_kernel, tm_size=tm_size, label_size=label_size, packed=packed, split=split
        ),
        [shape((width + 16, cells), bf16), shape((vocab, cells), bf16)]
        + [shape((part_rows, vocab), f32)] * count,
        operands + ([] if packed else sides),
        [pltpu.VMEM((width, frames), f32), pltpu.VMEM((width, LANES), f32)]
        + [pltpu.VMEM((columns, frames), f32)] * 3
        + [pltpu.VMEM((width + 16, vocab), f32)]
        + [pltpu.VMEM((vocab, frames), f32)] * (2 * GROUP),
        scalars=3,
        limit=FORWARD_LIMIT,
        flops=4 * width * vocab * cells,
    )
    if split:
        keep, send = weight_parts
        keep, bias_sum = keep[: width // 2], keep[width // 2 :]
    else:
        total, bias_sum = weight_parts[0][:width], weight_parts[0][width:]
        slots = total.reshape(tm_size, label_size, rows, vocab)
        for axis, size, index in ((0, tm_size, row), (1, label_size, mine)):
            order = jnp.array([reverse_bits(s, size) for s in range(size)], jnp.int32) ^ index
            slots = jnp.take(slots, order, axis=axis)
        slots = jnp.swapaxes(slots, 0, 1).reshape(width, vocab)
        keep, send = slots[: width // 2], slots[width // 2 :]
        send = jnp.concatenate([send, bias_sum], axis=0)

    stages = [("label", bit) for bit in bits_of(label_size)] + [("tm", bit) for bit in bits_of(tm_size)]
    arrived = swap(send, *stages[0])
    enc_half = shape((label_size // 2, frames, enc_width), f32)
    pred_half = shape((tm_size // 2, columns, pred_width), f32)
    enc_keep, enc_send, pred_keep, pred_send = call(
        functools.partial(backward_kernel, tm_size=tm_size, label_size=label_size, columns=columns),
        [enc_half, enc_half, pred_half, pred_half],
        (act, grad, weight),
        [
            pltpu.VMEM((width, frames), f32),
            pltpu.VMEM((width, LANES), f32),
            pltpu.VMEM((width, 2 * (columns // GROUP) * LANES), bf16),
        ],
        limit=BACKWARD_LIMIT,
        flops=2 * width * vocab * cells,
    )
    for i, _ in enumerate(stages):
        count = keep.shape[0]
        keep, bias_sum = keep + arrived[:count], bias_sum + arrived[count:]
        if i + 1 < len(stages):
            half = count // 2
            send = jnp.concatenate([keep[half:], bias_sum], axis=0)
            keep = keep[:half]
            arrived = swap(send, *stages[i + 1])
    final = jnp.concatenate([keep, bias_sum], axis=0)
    for bit in bits_of(lax.axis_size("dp")):
        final = final + swap(final, "dp", bit)
    weight_gradient = final[:rows]
    bias_rows = vocab // parts
    position = row * label_size + mine
    bias_gradient = lax.dynamic_slice_in_dim(final[rows], position * bias_rows, bias_rows, 0)

    encoder_gradient = halve(enc_keep, enc_send, "label")
    predictor_gradient = halve(pred_keep, pred_send, "tm")
    return (encoder_gradient, predictor_gradient, weight_gradient, bias_gradient)


FORWARD_LIMIT = 32
BACKWARD_LIMIT = 32


def solution(mesh):
    return jax.shard_map(
        lattice,
        mesh=mesh,
        in_specs=(
            P("dp", "tm", "label"),
            P("dp", "label", "tm"),
            P("dp", "label"),
            P("dp", "tm", "label"),
            P("dp", "tm", "label"),
            P("dp"),
            P("dp"),
            P(),
            P(),
        ),
        out_specs=(
            P("dp", "tm", "label"),
            P("dp", "label", "tm"),
            P(("tm", "label"), None),
            P(("tm", "label")),
        ),
        check_vma=False,
    )
```

time: 287 us -> 60.4 us (0.21)
  blocking collectives: 93.1 us -> 0 us
  waiting for transfers between devices: 90.3 us -> 22.6 us
  other arithmetic: 36.4 us -> 1.51 us
  local copies, waits for them, and re-layouts: 27.2 us -> 1.26 us
  Pallas kernels: 0 us -> 16.4 us
  between operations: 16.3 us -> 2.11 us
  starting transfers between devices: 2.69 us -> 16.3 us
  matrix products: 13.2 us -> 0 us
  loops' own time: 6.44 us -> 0 us
    psum x1 -> x0, waiting for transfers between devices: 89.2 us -> none  [per_device(): lax.psum((weight_sum, bias_sum), ('dp', 'tm', 'label'))]
    psum x2 -> x0, blocking collectives: 75.4 us -> none  [the longest x1 37.9 us: per_device(): lax.psum((weight_sum, bias_sum), ('dp', 'tm', 'label'))]
    ppermute x2 -> x15, waiting for transfers between devices: 0.01 us -> 22.6 us  [swap(): lax.ppermute(value, axis, [(i, i ^ bit) for i in range(lax.axis_size(axis...]
    all_gather x2 -> x0, blocking collectives: 17.7 us -> none  [the longest x1 12.1 us: per_device(): label_full = lax.all_gather(predictor_out, 'tm', axis=2, tiled=True)]
    pallas_call x0 -> x5, Pallas kernels: none -> 16.4 us  [call(): pl.pallas_call(kernel, grid_spec=pltpu.PrefetchScalarGridSpec(num_scalar_...]
    ppermute x2 -> x15, starting transfers between devices: 2.57 us -> 16.3 us  [swap(): lax.ppermute(value, axis, [(i, i ^ bit) for i in range(lax.axis_size(axis...]
    dot_general x24 -> x0, matrix products: 13.2 us -> none  [the longest x8 4.87 us: lattice(): lax.dot_general(joint_act, logit_gradient, (((0,), (0,)), ((), ())), pref...]
    select_n x16 -> x0, other arithmetic: 10.6 us -> none  [the longest x8 5.32 us: lattice(): jnp.where(blank_live, jnp.exp(alpha_rows + blank_score + after_blank - sc...]
  transfers between devices with their start and end apart: 5 -> 15, of which waited for: 1 -> 11; matrix products, arithmetic and copies ran while one was open for 2% -> 2% of each run, Pallas kernels for 0% -> 10%
where the time goes in v2:
time: 60.4 us; the launch traced here: 60.1 us
  waiting for transfers between devices  22.6 us (37%)
  Pallas kernels  16.4 us (27%)
  starting transfers between devices  16.3 us (27%)
  between operations  2.11 us (3%)
  other arithmetic  1.51 us (2%)
  local copies, waits for them, and re-layouts  1.26 us (2%)
    ppermute x15, waiting for transfers between devices, swap(): lax.ppermute(value, axis, [(i, i ^ bit) for i in range(lax.axis_size(axis...  22.6 us
    pallas_call x5, Pallas kernels, call(): pl.pallas_call(kernel, grid_spec=pltpu.PrefetchScalarGridSpec(num_scalar_...  16.4 us
    ppermute x15, starting transfers between devices, swap(): lax.ppermute(value, axis, [(i, i ^ bit) for i in range(lax.axis_size(axis...  16.3 us
    add x4, other arithmetic, halve(): keep, send = (keep + swap(send, axis, bit), None)  1.27 us
  transfers between devices with their start and end apart: 15, of which 11 were waited for; matrix products, arithmetic and copies ran while one was open for 2% of the time, Pallas kernels for 10%

profile of v2, /device:TPU:0, one launch (start us, length us, event | category | flops | bytes accessed | tf_op | source)
XLA Modules:
  0.0 60.1 jit_solution(5061272502473627512)
XLA Ops:
  0.6 0.8 %shard_map.121.rest_0_.refs_7_ = bf16[144,128]{1,0:T(8,128)(2,1)S(1)} custom-call(bf16[128,128]{1,0:T(8,128)(2,1)} %bitcast.13, f32[32,128]{1,0:T(8,128)} %bitcast.11), custom_call_target="tpu_custom_call" | custom-call | tf_op jit(solution)/shard_map/pallas_call | solution.py:68
  1.4 0.6 collective-permute-start
  2.0 2.6 %collective-permute-start.1 = (bf16[144,128]{1,0:T(8,128)(2,1)S(1)}, bf16[144,128]{1,0:T(8,128)(2,1)S(1)}, u32[]{:S(2)}, u32[]{:S(2)}) collective-permute-start(bf16[144,128]{1,0:T(8,128)(2,1)S(1)} %shard_map.121.rest_0_.refs_7_), channel_id=1, source_target_pairs={{0,2},{1,3},{2,0},{3,1},{4,6},{5,7},{6,4},{7,5},{8,10},{9,11},{10,... | collective-permute-start | bytes 110600 | tf_op jit(solution)/shard_map/ppermute | solution.py:30
  4.6 1.5 %shard_map.120 = (f32[40,128]{1,0:T(8,128)S(1)}, f32[32,128]{1,0:T(8,128)S(1)}, f32[32,128]{1,0:T(8,128)S(1)}, bf16[512,512]{1,0:T(8,128)(2,1)S(1)}, bf16[512,51...) custom-call(bf16[32,128]{1,0:T(8,128)(2,1)} %bitcast.15, f32[32,128]{1,0:T(8,128)} %bitcast.12, ...), custom_call_target="tpu_custom_call" | custom-call | tf_op jit(solution)/shard_map/pallas_call | solution.py:68
  6.1 0.6 collective-permute-done.1.rest_2_.refs_9_
  6.6 1.4 %collective-permute-done.2.rest_3_.refs_10_ = bf16[144,128]{1,0:T(8,128)(2,1)S(1)} collective-permute-done((bf16[144,128]{1,0:T(8,128)(2,1)S(1)}, bf16[144,128]{1,0:T(8,128)(2,1)S(1)}, u32[]{:S(2)}, u32[]{:S(2)}) %collective-permute-start.2) | collective-permute-done | bytes 36896 | tf_op jit(solution)/shard_map/ppermute | solution.py:30
  8.0 0.1 shard_map.122.refs_11_
  8.1 1.6 %collective-permute-start.3 = (f32[40,128]{1,0:T(8,128)S(1)}, f32[40,128]{1,0:T(8,128)S(1)}, u32[]{:S(2)}, u32[]{:S(2)}) collective-permute-start(f32[40,128]{1,0:T(8,128)S(1)} %shard_map.122.refs_11_), channel_id=1, source_target_pairs={{0,4},{4,0},{8,12},{12,8},{1,5},{5,1},{9,13},{13,9},{2,6},{6,2},{1... | collective-permute-start | bytes 61448 | tf_op jit(solution)/shard_map/ppermute | solution.py:30
  9.6 2.6 %collective-permute-start.4 = (f32[40,128]{1,0:T(8,128)S(1)}, f32[40,128]{1,0:T(8,128)S(1)}, u32[]{:S(2)}, u32[]{:S(2)}) collective-permute-start(f32[40,128]{1,0:T(8,128)S(1)} %shard_map.122.refs_11_), channel_id=1, source_target_pairs={{0,8},{4,12},{8,0},{12,4},{1,9},{5,13},{9,1},{13,5},{2,10},{6,14},... | collective-permute-start | bytes 61448 | tf_op jit(solution)/shard_map/ppermute | solution.py:30
  12.2 0.2 collective-permute-start.5
  13.8 0.8 %collective-permute-done.4.refs_13_ = f32[40,128]{1,0:T(8,128)S(1)} collective-permute-done((f32[40,128]{1,0:T(8,128)S(1)}, f32[40,128]{1,0:T(8,128)S(1)}, u32[]{:S(2)}, u32[]{:S(2)}) %collective-permute-start.4) | collective-permute-done | bytes 20512 | tf_op jit(solution)/shard_map/ppermute | solution.py:30
  14.6 3.3 %collective-permute-done.5.refs_14_ = f32[40,128]{1,0:T(8,128)S(1)} collective-permute-done((f32[40,128]{1,0:T(8,128)S(1)}, f32[40,128]{1,0:T(8,128)S(1)}, u32[]{:S(2)}, u32[]{:S(2)}) %collective-permute-start.5) | collective-permute-done | bytes 20512 | tf_op jit(solution)/shard_map/ppermute | solution.py:30
  17.8 9.3 %shard_map.123 = (bf16[528,4096]{1,0:T(8,128)(2,1)S(1)}, bf16[512,4096]{1,0:T(8,128)(2,1)S(1)}, f32[264,512]{1,0:T(8,128)S(1)}, f32[264,512]{1,0:T(8,128)S(1)}) custom-call(s32[1,32]{1,0:T(1,128)S(1)} %get-tuple-element.19.refs_0_, s32[1]{0:T(128)S(6)} %copy.13.refs_1_, s32[1]{0:T(128)S(6)} %copy.14.refs_2_, f32[32,128]{1,0:T(8,128)S(1)} %get-tuple-element.20.refs_3_, ...), custom_call_target="tpu_custom_call" | custom-call | flops 4294967296 | tf_op jit(solution)/shard_map/pallas_call | solution.py:68
  27.2 1.9 %collective-permute-done.10 = f32[264,512]{1,0:T(8,128)S(1)} collective-permute-done((f32[264,512]{1,0:T(8,128)S(1)}, f32[264,512]{1,0:T(8,128)S(1)}, u32[]{:S(2)}, u32[]{:S(2)}) %collective-permute-start.10) | collective-permute-done | bytes 540704 | tf_op jit(solution)/shard_map/ppermute | solution.py:30
  29.1 0.1 slice_add_fusion
  29.3 0.9 %collective-permute-start.11 = (f32[136,512]{1,0:T(8,128)S(1)}, f32[136,512]{1,0:T(8,128)S(1)}, u32[]{:S(2)}, u32[]{:S(2)}) collective-permute-start(f32[136,512]{1,0:T(8,128)S(1)} %pad_maximum_fusion), channel_id=1, source_target_pairs={{0,2},{1,3},{2,0},{3,1},{4,6},{5,7},{6,4},{7,5},{8,10},{9,11},{10,... | collective-permute-start | bytes 835592 | tf_op jit(solution)/shard_map/ppermute | solution.py:30
  30.2 7.8 %collective-permute-done.11 = f32[136,512]{1,0:T(8,128)S(1)} collective-permute-done((f32[136,512]{1,0:T(8,128)S(1)}, f32[136,512]{1,0:T(8,128)S(1)}, u32[]{:S(2)}, u32[]{:S(2)}) %collective-permute-start.11) | collective-permute-done | bytes 278560 | tf_op jit(solution)/shard_map/ppermute | solution.py:30
  38.2 4.8 %shard_map.124 = (f32[2,128,128]{2,1,0:T(8,128)S(1)}, f32[2,128,128]{2,1,0:T(8,128)S(1)}, f32[2,32,128]{2,1,0:T(8,128)S(1)}, f32[2,32,128]{2,1,0:T(8,128)S(1)}) custom-call(bf16[528,4096]{1,0:T(8,128)(2,1)S(1)} %get-tuple-element.25.act_ref, bf16[512,4096]{1,0:T(8,128)(2,1)S(1)} %get-tuple-element.26.grad_ref, bf16[512,512]{1,0:T(8,128)(2,1)S(1)} %get-tuple-element.27.w_ref), custom_call_target="tpu_custom_call" | custom-call | flops 2147483648 | tf_op jit(solution)/shard_map/pallas_call | solution.py:68
  43.0 2.1 %collective-permute-start.8 = (f32[2,32,128]{2,1,0:T(8,128)S(1)}, f32[2,32,128]{2,1,0:T(8,128)S(1)}, u32[]{:S(2)}, u32[]{:S(2)}) collective-permute-start(f32[2,32,128]{2,1,0:T(8,128)S(1)} %get-tuple-element.31), channel_id=1, source_target_pairs={{0,4},{4,0},{8,12},{12,8},{1,5},{5,1},{9,13},{13,9},{2,6},{6,2},{1... | collective-permute-start | bytes 98312 | tf_op jit(solution)/shard_map/ppermute | solution.py:30
  45.0 1.9 %collective-permute-done.8 = f32[2,32,128]{2,1,0:T(8,128)S(1)} collective-permute-done((f32[2,32,128]{2,1,0:T(8,128)S(1)}, f32[2,32,128]{2,1,0:T(8,128)S(1)}, u32[]{:S(2)}, u32[]{:S(2)}) %collective-permute-start.8) | collective-permute-done | bytes 32800 | tf_op jit(solution)/shard_map/ppermute | solution.py:30
  47.0 0.8 %collective-permute-start.9 = (f32[1,32,128]{2,1,0:T(8,128)S(1)}, f32[1,32,128]{2,1,0:T(8,128)S(1)}, u32[]{:S(2)}, u32[]{:S(2)}) collective-permute-start(f32[1,32,128]{2,1,0:T(8,128)S(1)} %slice.91), channel_id=1, source_target_pairs={{0,8},{4,12},{8,0},{12,4},{1,9},{5,13},{9,1},{13,5},{2,10},{6,14},... | collective-permute-start | bytes 49160 | tf_op jit(solution)/shard_map/ppermute | solution.py:30
  47.9 2.2 %collective-permute-start.13 = (f32[40,512]{1,0:T(8,128)S(1)}, f32[40,512]{1,0:T(8,128)S(1)}, u32[]{:S(2)}, u32[]{:S(2)}) collective-permute-start(f32[40,512]{1,0:T(8,128)S(1)} %pad_maximum_fusion.2), channel_id=1, source_target_pairs={{0,8},{4,12},{8,0},{12,4},{1,9},{5,13},{9,1},{13,5},{2,10},{6,14},... | collective-permute-start | bytes 245768 | tf_op jit(solution)/shard_map/ppermute | solution.py:30
  50.1 1.6 %collective-permute-done.9 = f32[1,32,128]{2,1,0:T(8,128)S(1)} collective-permute-done((f32[1,32,128]{2,1,0:T(8,128)S(1)}, f32[1,32,128]{2,1,0:T(8,128)S(1)}, u32[]{:S(2)}, u32[]{:S(2)}) %collective-permute-start.9) | collective-permute-done | bytes 16416 | tf_op jit(solution)/shard_map/ppermute | solution.py:30
  51.7 0.6 %slice_add_fusion.9 = f32[1,32,128]{2,1,0:T(8,128)} fusion(f32[1,32,128]{2,1,0:T(8,128)S(1)} %collective-permute-done.9, f32[2,32,128]{2,1,0:T(8,128)S(1)} %add.47), kind=kLoop, calls=%fused_computation.13 | loop fusion | flops 4096 | bytes 49152 | tf_op jit(solution)/shard_map/add | solution.py:326
  52.3 0.9 %collective-permute-start.7 = (f32[1,128,128]{2,1,0:T(8,128)S(1)}, f32[1,128,128]{2,1,0:T(8,128)S(1)}, u32[]{:S(2)}, u32[]{:S(2)}) collective-permute-start(f32[1,128,128]{2,1,0:T(8,128)S(1)} %slice.89), channel_id=1, source_target_pairs={{0,2},{1,3},{2,0},{3,1},{4,6},{5,7},{6,4},{7,5},{8,10},{9,11},{10,... | collective-permute-start | bytes 196616 | tf_op jit(solution)/shard_map/ppermute | solution.py:30
  53.2 1.1 %collective-permute-done.13 = f32[40,512]{1,0:T(8,128)S(1)} collective-permute-done((f32[40,512]{1,0:T(8,128)S(1)}, f32[40,512]{1,0:T(8,128)S(1)}, u32[]{:S(2)}, u32[]{:S(2)}) %collective-permute-start.13) | collective-permute-done | bytes 81952 | tf_op jit(solution)/shard_map/ppermute | solution.py:30
  54.4 1.6 %collective-permute-start.14 = (f32[40,512]{1,0:T(8,128)S(1)}, f32[40,512]{1,0:T(8,128)S(1)}, u32[]{:S(2)}, u32[]{:S(2)}) collective-permute-start(f32[40,512]{1,0:T(8,128)S(1)} %pad_maximum_fusion.3), channel_id=1, source_target_pairs={{0,16},{16,0},{1,17},{17,1},{2,18},{18,2},{3,19},{19,3},{4,20},{20... | collective-permute-start | bytes 245768 | tf_op jit(solution)/shard_map/ppermute | solution.py:30
  55.9 0.7 %collective-permute-done.7 = f32[1,128,128]{2,1,0:T(8,128)S(1)} collective-permute-done((f32[1,128,128]{2,1,0:T(8,128)S(1)}, f32[1,128,128]{2,1,0:T(8,128)S(1)}, u32[]{:S(2)}, u32[]{:S(2)}) %collective-permute-start.7) | collective-permute-done | bytes 65568 | tf_op jit(solution)/shard_map/ppermute | solution.py:30
  56.6 0.6 %slice_add_fusion.4 = f32[1,128,128]{2,1,0:T(8,128)} fusion(f32[1,128,128]{2,1,0:T(8,128)S(1)} %collective-permute-done.7, f32[2,128,128]{2,1,0:T(8,128)S(1)} %add.45), kind=kLoop, calls=%fused_computation.8 | loop fusion | flops 16384 | bytes 196608 | tf_op jit(solution)/shard_map/add | solution.py:326
  57.3 1.6 %collective-permute-done.14 = f32[40,512]{1,0:T(8,128)S(1)} collective-permute-done((f32[40,512]{1,0:T(8,128)S(1)}, f32[40,512]{1,0:T(8,128)S(1)}, u32[]{:S(2)}, u32[]{:S(2)}) %collective-permute-start.14) | collective-permute-done | bytes 81952 | tf_op jit(solution)/shard_map/ppermute | solution.py:30
  58.9 0.6 %slice.106 = f32[32,512]{1,0:T(8,128)} slice(f32[40,512]{1,0:T(8,128)S(1)} %fusion), slice={[0:32], [0:512]} | slice | bytes 131072 | tf_op jit(solution)/shard_map/slice | solution.py:440
  59.5 0.6 dynamic-slice_bitcast_fusion
  (28 shorter events, 0.4 us)
Async XLA Ops:
  1.4 4.6 %collective-permute-start = (bf16[144,128]{1,0:T(8,128)(2,1)S(1)}, bf16[144,128]{1,0:T(8,128)(2,1)S(1)}, u32[]{:S(2)}, u32[]{:S(2)}) collective-permute-start(bf16[144,128]{1,0:T(8,128)(2,1)S(1)} %shard_map.121.rest_0_.refs_7_), channel_id=1, source_target_pairs={{0,1},{1,0},{2,3},{3,2},{4,5},{5,4},{6,7},{7,6},{8,9},{9,8},{10,11... | collective-permute-start | bytes 110600 | tf_op jit(solution)/shard_map/ppermute | solution.py:30
  2.0 4.6 %collective-permute-start.1 = (bf16[144,128]{1,0:T(8,128)(2,1)S(1)}, bf16[144,128]{1,0:T(8,128)(2,1)S(1)}, u32[]{:S(2)}, u32[]{:S(2)}) collective-permute-start(bf16[144,128]{1,0:T(8,128)(2,1)S(1)} %shard_map.121.rest_0_.refs_7_), channel_id=1, source_target_pairs={{0,2},{1,3},{2,0},{3,1},{4,6},{5,7},{6,4},{7,5},{8,10},{9,11},{10,... | collective-permute-start | bytes 110600 | tf_op jit(solution)/shard_map/ppermute | solution.py:30
  4.5 3.4 %collective-permute-start.2 = (bf16[144,128]{1,0:T(8,128)(2,1)S(1)}, bf16[144,128]{1,0:T(8,128)(2,1)S(1)}, u32[]{:S(2)}, u32[]{:S(2)}) collective-permute-start(bf16[144,128]{1,0:T(8,128)(2,1)S(1)} %shard_map.121.rest_0_.refs_7_), channel_id=1, source_target_pairs={{0,3},{1,2},{2,1},{3,0},{4,7},{5,6},{6,5},{7,4},{8,11},{9,10},{10,... | collective-permute-start | bytes 110600 | tf_op jit(solution)/shard_map/ppermute | solution.py:30
  8.1 5.7 %collective-permute-start.3 = (f32[40,128]{1,0:T(8,128)S(1)}, f32[40,128]{1,0:T(8,128)S(1)}, u32[]{:S(2)}, u32[]{:S(2)}) collective-permute-start(f32[40,128]{1,0:T(8,128)S(1)} %shard_map.122.refs_11_), channel_id=1, source_target_pairs={{0,4},{4,0},{8,12},{12,8},{1,5},{5,1},{9,13},{13,9},{2,6},{6,2},{1... | collective-permute-start | bytes 61448 | tf_op jit(solution)/shard_map/ppermute | solution.py:30
  9.6 4.9 %collective-permute-start.4 = (f32[40,128]{1,0:T(8,128)S(1)}, f32[40,128]{1,0:T(8,128)S(1)}, u32[]{:S(2)}, u32[]{:S(2)}) collective-permute-start(f32[40,128]{1,0:T(8,128)S(1)} %shard_map.122.refs_11_), channel_id=1, source_target_pairs={{0,8},{4,12},{8,0},{12,4},{1,9},{5,13},{9,1},{13,5},{2,10},{6,14},... | collective-permute-start | bytes 61448 | tf_op jit(solution)/shard_map/ppermute | solution.py:30
  12.2 5.6 %collective-permute-start.5 = (f32[40,128]{1,0:T(8,128)S(1)}, f32[40,128]{1,0:T(8,128)S(1)}, u32[]{:S(2)}, u32[]{:S(2)}) collective-permute-start(f32[40,128]{1,0:T(8,128)S(1)} %shard_map.122.refs_11_), channel_id=1, source_target_pairs={{0,12},{4,8},{8,4},{12,0},{1,13},{5,9},{9,5},{13,1},{2,14},{6,10},... | collective-permute-start | bytes 61448 | tf_op jit(solution)/shard_map/ppermute | solution.py:30
  27.1 2.0 %collective-permute-start.10 = (f32[264,512]{1,0:T(8,128)S(1)}, f32[264,512]{1,0:T(8,128)S(1)}, u32[]{:S(2)}, u32[]{:S(2)}) collective-permute-start(f32[264,512]{1,0:T(8,128)S(1)} %get-tuple-element.33), channel_id=1, source_target_pairs={{0,1},{1,0},{2,3},{3,2},{4,5},{5,4},{6,7},{7,6},{8,9},{9,8},{10,11... | collective-permute-start | bytes 1622024 | tf_op jit(solution)/shard_map/ppermute | solution.py:30
  29.3 8.8 %collective-permute-start.11 = (f32[136,512]{1,0:T(8,128)S(1)}, f32[136,512]{1,0:T(8,128)S(1)}, u32[]{:S(2)}, u32[]{:S(2)}) collective-permute-start(f32[136,512]{1,0:T(8,128)S(1)} %pad_maximum_fusion), channel_id=1, source_target_pairs={{0,2},{1,3},{2,0},{3,1},{4,6},{5,7},{6,4},{7,5},{8,10},{9,11},{10,... | collective-permute-start | bytes 835592 | tf_op jit(solution)/shard_map/ppermute | solution.py:30
  38.1 9.7 %collective-permute-start.12 = (f32[72,512]{1,0:T(8,128)S(1)}, f32[72,512]{1,0:T(8,128)S(1)}, u32[]{:S(2)}, u32[]{:S(2)}) collective-permute-start(f32[72,512]{1,0:T(8,128)S(1)} %pad_maximum_fusion.1), channel_id=1, source_target_pairs={{0,4},{4,0},{8,12},{12,8},{1,5},{5,1},{9,13},{13,9},{2,6},{6,2},{1... | collective-permute-start | bytes 442376 | tf_op jit(solution)/shard_map/ppermute | solution.py:30
  43.0 4.0 %collective-permute-start.8 = (f32[2,32,128]{2,1,0:T(8,128)S(1)}, f32[2,32,128]{2,1,0:T(8,128)S(1)}, u32[]{:S(2)}, u32[]{:S(2)}) collective-permute-start(f32[2,32,128]{2,1,0:T(8,128)S(1)} %get-tuple-element.31), channel_id=1, source_target_pairs={{0,4},{4,0},{8,12},{12,8},{1,5},{5,1},{9,13},{13,9},{2,6},{6,2},{1... | collective-permute-start | bytes 98312 | tf_op jit(solution)/shard_map/ppermute | solution.py:30
  45.0 7.2 %collective-permute-start.6 = (f32[2,128,128]{2,1,0:T(8,128)S(1)}, f32[2,128,128]{2,1,0:T(8,128)S(1)}, u32[]{:S(2)}, u32[]{:S(2)}) collective-permute-start(f32[2,128,128]{2,1,0:T(8,128)S(1)} %get-tuple-element.29), channel_id=1, source_target_pairs={{0,1},{1,0},{2,3},{3,2},{4,5},{5,4},{6,7},{7,6},{8,9},{9,8},{10,11... | collective-permute-start | bytes 393224 | tf_op jit(solution)/shard_map/ppermute | solution.py:30
  47.0 4.7 %collective-permute-start.9 = (f32[1,32,128]{2,1,0:T(8,128)S(1)}, f32[1,32,128]{2,1,0:T(8,128)S(1)}, u32[]{:S(2)}, u32[]{:S(2)}) collective-permute-start(f32[1,32,128]{2,1,0:T(8,128)S(1)} %slice.91), channel_id=1, source_target_pairs={{0,8},{4,12},{8,0},{12,4},{1,9},{5,13},{9,1},{13,5},{2,10},{6,14},... | collective-permute-start | bytes 49160 | tf_op jit(solution)/shard_map/ppermute | solution.py:30
  47.9 6.5 %collective-permute-start.13 = (f32[40,512]{1,0:T(8,128)S(1)}, f32[40,512]{1,0:T(8,128)S(1)}, u32[]{:S(2)}, u32[]{:S(2)}) collective-permute-start(f32[40,512]{1,0:T(8,128)S(1)} %pad_maximum_fusion.2), channel_id=1, source_target_pairs={{0,8},{4,12},{8,0},{12,4},{1,9},{5,13},{9,1},{13,5},{2,10},{6,14},... | collective-permute-start | bytes 245768 | tf_op jit(solution)/shard_map/ppermute | solution.py:30
  52.3 4.3 %collective-permute-start.7 = (f32[1,128,128]{2,1,0:T(8,128)S(1)}, f32[1,128,128]{2,1,0:T(8,128)S(1)}, u32[]{:S(2)}, u32[]{:S(2)}) collective-permute-start(f32[1,128,128]{2,1,0:T(8,128)S(1)} %slice.89), channel_id=1, source_target_pairs={{0,2},{1,3},{2,0},{3,1},{4,6},{5,7},{6,4},{7,5},{8,10},{9,11},{10,... | collective-permute-start | bytes 196616 | tf_op jit(solution)/shard_map/ppermute | solution.py:30
  54.4 4.5 %collective-permute-start.14 = (f32[40,512]{1,0:T(8,128)S(1)}, f32[40,512]{1,0:T(8,128)S(1)}, u32[]{:S(2)}, u32[]{:S(2)}) collective-permute-start(f32[40,512]{1,0:T(8,128)S(1)} %pad_maximum_fusion.3), channel_id=1, source_target_pairs={{0,16},{16,0},{1,17},{17,1},{2,18},{18,2},{3,19},{19,3},{4,20},{20... | collective-permute-start | bytes 245768 | tf_op jit(solution)/shard_map/ppermute | solution.py:30

commit v3 on v2

--- a/solution.py
+++ b/solution.py
@@ -103,9 +103,24 @@
 
 
 def prepare(
-    pred_ref, beta_ref, alpha_ref, w_ref, bias_ref, ids_ref, pred_out, alpha_out, beta_out, w_out, wt_out, bias_t, ids_out
+    pred_ref,
+    beta_ref,
+    alpha_ref,
+    w_ref,
+    bias_ref,
+    ids_ref,
+    limits_ref,
+    pred_out,
+    alpha_out,
+    beta_out,
+    w_out,
+    wt_out,
+    bias_t,
+    ids_out,
+    limits_out,
 ):
     ids_out[...] = ids_ref[...]
+    limits_out[...] = limits_ref[...]
     columns = pred_ref.shape[0]
     pred_out[:columns, :] = pred_ref[...].astype(jnp.float32)
     pred_out[columns:, :] = jnp.zeros((8, pred_out.shape[1]), jnp.float32)
@@ -128,7 +143,7 @@
 def forward_kernel(*refs, tm_size, label_size, packed, split):
     refs = iter(refs)
     take = lambda count: [next(refs) for _ in range(count)]
-    ids_ref, frames_ref, labels_ref, alpha_ref, beta_ref, wt_ref, bias_t = take(7)
+    ids_ref, limits_ref, alpha_ref, beta_ref, wt_ref, bias_t = take(6)
     enc_refs, pred_refs = take(label_size), take(tm_size)
     side_refs = enc_refs if packed else take(label_size)
     act_ref, grad_ref = take(2)
@@ -163,7 +178,7 @@
     down = jnp.where(lane == frames - 1, below, pltpu.roll(beta, frames - 1, 1))
     right = jnp.where(line == columns - 1, beside, pltpu.roll(beta, columns - 1, 0))
     frame, column = row * frames + lane, mine * columns + line
-    frame_limit, label_limit = frames_ref[0], labels_ref[0]
+    frame_limit, label_limit = limits_ref[0:1, 0:1], limits_ref[1:2, 0:1]
     inside = (frame < frame_limit) & (column <= label_limit)
     more = frame + 1 < frame_limit
     occ_s[...] = jnp.where(inside, jnp.exp(alpha + beta - score), 0.0)
@@ -240,27 +255,35 @@
 
     activate(0)
     score_logits(0)
+    activate(1)
     for g in range(groups):
+        if g > 0:
+            accumulate(g - 1, 1)
+        if g + 2 < groups:
+            activate(g + 2)
         if g + 1 < groups:
-            activate(g + 1)
             score_logits(g + 1)
         differentiate(g)
-        if g % 2 == 1:
-            accumulate(g - 1, 2)
+    accumulate(groups - 1, 1)
 
     if not split:
         out_refs[0][...] = acc[: width + 8, :]
         return
-    parts = tm_size * label_size
+    parts, tiles = tm_size * label_size, vocab // LANES
     rows = width // parts
     for s in range(parts):
         label = reverse_bits(s // tm_size, label_size) ^ mine
         tm = reverse_bits(s % tm_size, tm_size) ^ row
         start = pl.multiple_of((tm * label_size + label) * rows, rows)
-        to = (s % (parts // 2)) * rows
-        out_refs[s // (parts // 2)][to : to + rows, :] = acc[pl.ds(start, rows), :]
+        to = (s % (parts // 2)) * rows * tiles
+        for k in range(tiles):
+            block = acc[pl.ds(start, rows), k * LANES : (k + 1) * LANES]
+            out_refs[s // (parts // 2)][to + k * rows : to + (k + 1) * rows, :] = block
     for ref in out_refs:
-        ref[width // 2 :, :] = acc[width : width + 8, :]
+        ref[width * tiles // 2 :, :] = jnp.zeros((8, LANES), jnp.float32)
+        for k in range(tiles):
+            at = width * tiles // 2 + k
+            ref[at : at + 1, :] = acc[width : width + 1, k * LANES : (k + 1) * LANES]
 
 
 def lane_swap(value, distance):
@@ -318,8 +341,54 @@
         ref[s % (tm_size // 2)] = sums[pl.ds(start, pred_width), :].T[:columns, :]
 
 
-def halve(keep, send, axis):
-    for bit in bits_of(lax.axis_size(axis)):
+def finish(final_ref, weight_out, bias_out, weight_s, bias_s, done, *, label_size):
+    rows, vocab = weight_s.shape
+    tiles, count = vocab // LANES, bias_s.shape[1]
+    for k in range(tiles):
+        weight_s[:, k * LANES : (k + 1) * LANES] = final_ref[k * rows : (k + 1) * rows, :]
+    copy = pltpu.make_async_copy(weight_s, weight_out, done.at[0])
+    copy.start()
+    first = (lax.axis_index("tm") * label_size + lax.axis_index("label")) * count
+    line = jnp.zeros((1, LANES), jnp.float32)
+    for k in range(tiles):
+        at = rows * tiles + k
+        line = line + jnp.where(first // LANES == k, final_ref[at : at + 1, :], 0.0)
+    line = pltpu.roll(jnp.broadcast_to(line, (8, LANES)), lax.rem(LANES - first % LANES, LANES), 1)
+    bias_s[...] = line[0:1, :count]
+    other = pltpu.make_async_copy(bias_s, bias_out, done.at[1])
+    other.start()
+    copy.wait()
+    other.wait()
+
+
+def add_halves(keep_ref, arrived_ref, low_ref, high_ref):
+    half = low_ref.shape[0]
+    low_ref[...] = keep_ref[:half] + arrived_ref[:half]
+    high_ref[...] = keep_ref[-half:] + arrived_ref[-half:]
+
+
+def add_out(keep_ref, arrived_ref, out_ref, total, done, *, first):
+    count = total.shape[0]
+    total[...] = keep_ref[...] + arrived_ref[first : first + count]
+    copy = pltpu.make_async_copy(total, out_ref.at[0], done)
+    copy.start()
+    copy.wait()
+
+
+def write_sum(keep, arrived, first):
+    rows, lanes = keep.shape
+    return pl.pallas_call(
+        functools.partial(add_out, first=first),
+        in_specs=[vmem()] * 2,
+        out_specs=pl.BlockSpec(memory_space=pltpu.HBM),
+        out_shape=jax.ShapeDtypeStruct((1, rows, lanes), jnp.float32),
+        scratch_shapes=[pltpu.VMEM((rows, lanes), jnp.float32), pltpu.SemaphoreType.DMA(())],
+        compiler_params=pltpu.CompilerParams(vmem_limit_bytes=16 * MIB),
+    )(keep, arrived)
+
+
+def halve(keep, send, axis, bits):
+    for bit in bits:
         if send is None:
             half = keep.shape[0] // 2
             keep, send = keep[:half], keep[half:]
@@ -358,7 +427,7 @@
         )[0]
     encs = gather_slots(payload, "label")
     sides = encs if packed else gather_slots(beta[0:1, :], "label")
-    part, alpha, beta, weight, weight_t, bias_t, label_ids = call(
+    part, alpha, beta, weight, weight_t, bias_t, label_ids, limits = call(
         prepare,
         [
             shape((columns + 8, pred_width), f32),
@@ -368,8 +437,17 @@
             shape((vocab, width), bf16),
             shape((vocab, frames), f32),
             shape(label_ids.shape, label_ids.dtype),
+            shape((2, LANES), jnp.int32),
         ],
-        (predictor_out[0], beta, alpha, joint_weight, joint_bias[None, :], label_ids),
+        (
+            predictor_out[0],
+            beta,
+            alpha,
+            joint_weight,
+            joint_bias[None, :],
+            label_ids,
+            jnp.broadcast_to(jnp.concatenate([frame_count, label_count])[:, None], (2, LANES)),
+        ),
         loads=6,
     )
     payload = call(
@@ -380,35 +458,36 @@
     preds = gather_slots(payload, "tm")
 
     cells = columns * frames
-    count, part_rows = (2, width // 2 + 8) if split else (1, width + 8)
-    operands = [label_ids, frame_count, label_count, alpha, beta, weight_t, bias_t, *encs, *preds]
+    tiles = vocab // LANES
+    part_shape = (width * tiles // 2 + 8, LANES) if split else (width + 8, vocab)
+    operands = [label_ids, limits, alpha, beta, weight_t, bias_t, *encs, *preds]
     act, grad, *weight_parts = call(
         functools.partial(
             forward_kernel, tm_size=tm_size, label_size=label_size, packed=packed, split=split
         ),
         [shape((width + 16, cells), bf16), shape((vocab, cells), bf16)]
-        + [shape((part_rows, vocab), f32)] * count,
+        + [shape(part_shape, f32)] * (2 if split else 1),
         operands + ([] if packed else sides),
         [pltpu.VMEM((width, frames), f32), pltpu.VMEM((width, LANES), f32)]
         + [pltpu.VMEM((columns, frames), f32)] * 3
         + [pltpu.VMEM((width + 16, vocab), f32)]
         + [pltpu.VMEM((vocab, frames), f32)] * (2 * GROUP),
-        scalars=3,
+        scalars=1,
         limit=FORWARD_LIMIT,
         flops=4 * width * vocab * cells,
     )
+    half = width * tiles // 2
     if split:
         keep, send = weight_parts
-        keep, bias_sum = keep[: width // 2], keep[width // 2 :]
+        keep, bias_sum = keep[:half], keep[half:]
     else:
-        total, bias_sum = weight_parts[0][:width], weight_parts[0][width:]
-        slots = total.reshape(tm_size, label_size, rows, vocab)
+        slots = weight_parts[0][:width].reshape(tm_size, label_size, rows, tiles, LANES)
         for axis, size, index in ((0, tm_size, row), (1, label_size, mine)):
             order = jnp.array([reverse_bits(s, size) for s in range(size)], jnp.int32) ^ index
             slots = jnp.take(slots, order, axis=axis)
-        slots = jnp.swapaxes(slots, 0, 1).reshape(width, vocab)
-        keep, send = slots[: width // 2], slots[width // 2 :]
-        send = jnp.concatenate([send, bias_sum], axis=0)
+        slots = jnp.transpose(slots, (1, 0, 3, 2, 4)).reshape(width * tiles, LANES)
+        bias_sum = jnp.pad(weight_parts[0][width].reshape(tiles, LANES), ((0, 8 - tiles), (0, 0)))
+        keep, send = slots[:half], jnp.concatenate([slots[half:], bias_sum], axis=0)
 
     stages = [("label", bit) for bit in bits_of(label_size)] + [("tm", bit) for bit in bits_of(tm_size)]
     arrived = swap(send, *stages[0])
@@ -426,25 +505,60 @@
         limit=BACKWARD_LIMIT,
         flops=2 * width * vocab * cells,
     )
-    for i, _ in enumerate(stages):
+    joined = pred_width == LANES
+    enc_stages = bits_of(label_size)
+    enc_sum, enc_rest = call(
+        add_halves,
+        [shape((max(label_size // 4, 1), frames, enc_width), f32)] * 2,
+        (enc_keep, swap(enc_send, "label", enc_stages[0])),
+    )
+    pred_sum, pred_rest = pred_keep, pred_send
+    for i, (axis, _) in enumerate(stages):
         count = keep.shape[0]
-        keep, bias_sum = keep + arrived[:count], bias_sum + arrived[count:]
+        keep, bias_sum = keep + arrived[:count], bias_sum + arrived[count : count + 8]
+        if joined and axis == "tm":
+            pred_rest = None
+            if i + 1 < len(stages):
+                pred_sum = pred_sum + arrived[count + 8 :].reshape(pred_sum.shape)
+            else:
+                predictor_gradient = write_sum(pred_sum[0], arrived, count + 8)
         if i + 1 < len(stages):
             half = count // 2
-            send = jnp.concatenate([keep[half:], bias_sum], axis=0)
+            pieces = [keep[half:], bias_sum]
+            if joined and stages[i + 1][0] == "tm":
+                if pred_rest is None:
+                    middle = pred_sum.shape[0] // 2
+                    pred_sum, pred_rest = pred_sum[:middle], pred_sum[middle:]
+                pieces.append(pred_rest.reshape(-1, LANES))
             keep = keep[:half]
-            arrived = swap(send, *stages[i + 1])
+            arrived = swap(jnp.concatenate(pieces, axis=0), *stages[i + 1])
     final = jnp.concatenate([keep, bias_sum], axis=0)
     for bit in bits_of(lax.axis_size("dp")):
-        final = final + swap(final, "dp", bit)
-    weight_gradient = final[:rows]
+        other = swap(final, "dp", bit)
+        final = final + other
+    for bit in enc_stages[1:-1]:
+        enc_sum = enc_sum + swap(enc_rest, "label", bit)
+        half = enc_sum.shape[0] // 2
+        enc_sum, enc_rest = enc_sum[:half], enc_sum[half:]
+    enc_rest = swap(enc_rest[0], "label", enc_stages[-1])
+    encoder_gradient = write_sum(enc_sum[0], enc_rest, 0)
+    if not joined:
+        predictor_gradient = halve(pred_keep, pred_send, "tm", bits_of(tm_size))
     bias_rows = vocab // parts
-    position = row * label_size + mine
-    bias_gradient = lax.dynamic_slice_in_dim(final[rows], position * bias_rows, bias_rows, 0)
-
-    encoder_gradient = halve(enc_keep, enc_send, "label")
-    predictor_gradient = halve(pred_keep, pred_send, "tm")
-    return (encoder_gradient, predictor_gradient, weight_gradient, bias_gradient)
+    weight_gradient, bias_gradient = pl.pallas_call(
+        functools.partial(finish, label_size=label_size),
+        in_specs=[vmem()],
+        out_specs=[pl.BlockSpec(memory_space=pltpu.HBM)] * 2,
+        out_shape=[shape((rows, vocab), f32), shape((1, bias_rows), f32)],
+        scratch_shapes=[
+            pltpu.VMEM((rows, vocab), f32),
+            pltpu.VMEM((1, bias_rows), f32),
+            pltpu.SemaphoreType.DMA((2,)),
+        ],
+        compiler_params=pltpu.CompilerParams(vmem_limit_bytes=16 * MIB),
+        name="finish",
+    )(final)
+    return (encoder_gradient, predictor_gradient, weight_gradient, bias_gradient[0])
 
 
 FORWARD_LIMIT = 32

time: 60.4 us -> 55.8 us (0.924)
  starting transfers between devices: 16.3 us -> 14.1 us
  waiting for transfers between devices: 22.6 us -> 21.3 us
  other arithmetic: 1.51 us -> 0.3 us
  Pallas kernels: 16.4 us -> 17.6 us
  local copies, waits for them, and re-layouts: 1.26 us -> 0.12 us
    ppermute x15 -> x13, starting transfers between devices: 16.3 us -> 14.1 us  [swap(): lax.ppermute(value, axis, [(i, i ^ bit) for i in range(lax.axis_size(axis...]
    pallas_call x0 -> x3, Pallas kernels: none -> 1.93 us  [the longest x2 1.26 us: write_sum(): pl.pallas_call(functools.partial(add_out, first=first), in_specs=[vmem()]...]
    ppermute x15 -> x13, waiting for transfers between devices: 22.6 us -> 21.3 us  [swap(): lax.ppermute(value, axis, [(i, i ^ bit) for i in range(lax.axis_size(axis...]
    add x13 -> x10, other arithmetic: 1.46 us -> 0.18 us  [the longest x4 0.14 us: lattice(): keep + arrived[:count]]
    pallas_call x5 -> x6, Pallas kernels: 16.4 us -> 15.7 us  [call(): pl.pallas_call(kernel, grid_spec=pltpu.PrefetchScalarGridSpec(num_scalar_...]
    slice x7 -> x4, local copies, waits for them, and re-layouts: 0.68 us -> 0.04 us  [the longest x3 0.04 us: lattice(): pieces = [keep[half:], bias_sum]]
  transfers between devices with their start and end apart: 15 -> 13, of which waited for: 11 -> 8; matrix products, arithmetic and copies ran while one was open for 2% -> 0% of each run, Pallas kernels for 10% -> 13%
where the time goes in v3:
time: 55.8 us; the launch traced here: 55.6 us
  waiting for transfers between devices  21.3 us (38%)
  Pallas kernels  17.6 us (32%)
  starting transfers between devices  14.1 us (25%)
  between operations  2.12 us (4%)
    ppermute x13, waiting for transfers between devices, swap(): lax.ppermute(value, axis, [(i, i ^ bit) for i in range(lax.axis_size(axis...  21.3 us
    pallas_call x6, Pallas kernels, call(): pl.pallas_call(kernel, grid_spec=pltpu.PrefetchScalarGridSpec(num_scalar_...  15.7 us
    ppermute x13, starting transfers between devices, swap(): lax.ppermute(value, axis, [(i, i ^ bit) for i in range(lax.axis_size(axis...  14.1 us
    pallas_call x2, Pallas kernels, write_sum(): pl.pallas_call(functools.partial(add_out, first=first), in_specs=[vmem()]...  1.26 us
  transfers between devices with their start and end apart: 13, of which 8 were waited for; matrix products, arithmetic and copies ran while one was open for 0% of the time, Pallas kernels for 13%

profile of v3, /device:TPU:0, one launch (start us, length us, event | category | flops | bytes accessed | tf_op | source)
XLA Modules:
  0.0 55.6 jit_solution(10848409354459593082)
XLA Ops:
  0.6 0.8 %shard_map.121.rest_0_.refs_6_ = bf16[144,128]{1,0:T(8,128)(2,1)S(1)} custom-call(bf16[128,128]{1,0:T(8,128)(2,1)} %bitcast.24, f32[32,128]{1,0:T(8,128)} %bitcast.22), custom_call_target="tpu_custom_call" | custom-call | tf_op jit(solution)/shard_map/pallas_call | solution.py:68
  1.4 2.5 %collective-permute-start.2 = (bf16[144,128]{1,0:T(8,128)(2,1)S(1)}, bf16[144,128]{1,0:T(8,128)(2,1)S(1)}, u32[]{:S(2)}, u32[]{:S(2)}) collective-permute-start(bf16[144,128]{1,0:T(8,128)(2,1)S(1)} %shard_map.121.rest_0_.refs_6_), channel_id=1, source_target_pairs={{0,3},{1,2},{2,1},{3,0},{4,7},{5,6},{6,5},{7,4},{8,11},{9,10},{10,... | collective-permute-start | bytes 110600 | tf_op jit(solution)/shard_map/ppermute | solution.py:30
  3.9 0.6 %collective-permute-start.1 = (bf16[144,128]{1,0:T(8,128)(2,1)S(1)}, bf16[144,128]{1,0:T(8,128)(2,1)S(1)}, u32[]{:S(2)}, u32[]{:S(2)}) collective-permute-start(bf16[144,128]{1,0:T(8,128)(2,1)S(1)} %shard_map.121.rest_0_.refs_6_), channel_id=1, source_target_pairs={{0,2},{1,3},{2,0},{3,1},{4,6},{5,7},{6,4},{7,5},{8,10},{9,11},{10,... | collective-permute-start | bytes 110600 | tf_op jit(solution)/shard_map/ppermute | solution.py:30
  4.5 0.0 collective-permute-start
  5.9 0.1 pad_add_fusion
  6.0 0.1 broadcast_in_dim.10.refs_6_
  6.0 1.5 %shard_map.120 = (f32[40,128]{1,0:T(8,128)S(1)}, f32[32,128]{1,0:T(8,128)S(1)}, f32[32,128]{1,0:T(8,128)S(1)}, bf16[512,512]{1,0:T(8,128)(2,1)S(1)}, bf16[512,51...) custom-call(bf16[32,128]{1,0:T(8,128)(2,1)} %bitcast.26, ...), custom_call_target="tpu_custom_call" | custom-call | tf_op jit(solution)/shard_map/pallas_call | solution.py:68
  7.5 0.0 collective-permute-done.2.rest_3_.refs_9_
  7.5 0.5 collective-permute-done.1.rest_2_.refs_8_
  8.0 0.1 shard_map.122.refs_10_
  8.0 3.6 %collective-permute-start.5 = (f32[40,128]{1,0:T(8,128)S(1)}, f32[40,128]{1,0:T(8,128)S(1)}, u32[]{:S(2)}, u32[]{:S(2)}) collective-permute-start(f32[40,128]{1,0:T(8,128)S(1)} %shard_map.122.refs_10_), channel_id=1, source_target_pairs={{0,12},{4,8},{8,4},{12,0},{1,13},{5,9},{9,5},{13,1},{2,14},{6,10},... | collective-permute-start | bytes 61448 | tf_op jit(solution)/shard_map/ppermute | solution.py:30
  11.7 0.8 %collective-permute-start.3 = (f32[40,128]{1,0:T(8,128)S(1)}, f32[40,128]{1,0:T(8,128)S(1)}, u32[]{:S(2)}, u32[]{:S(2)}) collective-permute-start(f32[40,128]{1,0:T(8,128)S(1)} %shard_map.122.refs_10_), channel_id=1, source_target_pairs={{0,4},{4,0},{8,12},{12,8},{1,5},{5,1},{9,13},{13,9},{2,6},{6,2},{1... | collective-permute-start | bytes 61448 | tf_op jit(solution)/shard_map/ppermute | solution.py:30
  12.4 1.2 %collective-permute-done.5.refs_13_ = f32[40,128]{1,0:T(8,128)S(1)} collective-permute-done((f32[40,128]{1,0:T(8,128)S(1)}, f32[40,128]{1,0:T(8,128)S(1)}, u32[]{:S(2)}, u32[]{:S(2)}) %collective-permute-start.5) | collective-permute-done | bytes 20512 | tf_op jit(solution)/shard_map/ppermute | solution.py:30
  13.6 2.7 %collective-permute-done.4.refs_12_ = f32[40,128]{1,0:T(8,128)S(1)} collective-permute-done((f32[40,128]{1,0:T(8,128)S(1)}, f32[40,128]{1,0:T(8,128)S(1)}, u32[]{:S(2)}, u32[]{:S(2)}) %collective-permute-start.4) | collective-permute-done | bytes 20512 | tf_op jit(solution)/shard_map/ppermute | solution.py:30
  16.3 8.8 %shard_map.123 = (bf16[528,4096]{1,0:T(8,128)(2,1)S(1)}, bf16[512,4096]{1,0:T(8,128)(2,1)S(1)}, f32[1032,128]{1,0:T(8,128)S(1)}, f32[1032,128]{1,0:T(8,128)S(1)}) custom-call(s32[1,32]{1,0:T(1,128)S(1)} %get-tuple-element.24.refs_0_, s32[2,128]{1,0:T(2,128)S(1)} %get-tuple-element.25.refs_1_, f32[32,128]{1,0:T(8,128)S(1)} %get-tuple-element.26.refs_2_, ...), custom_call_target="tpu_custom_call" | custom-call | flops 4294967296 | tf_op jit(solution)/shard_map/pallas_call | solution.py:68
  25.2 0.1 collective-permute-start.8
  25.3 1.9 %collective-permute-done.8 = f32[1032,128]{1,0:T(8,128)S(1)} collective-permute-done((f32[1032,128]{1,0:T(8,128)S(1)}, f32[1032,128]{1,0:T(8,128)S(1)}, u32[]{:S(2)}, u32[]{:S(2)}) %collective-permute-start.8) | collective-permute-done | bytes 528416 | tf_op jit(solution)/shard_map/ppermute | solution.py:30
  27.2 0.1 slice_add_fusion
  27.3 1.4 %collective-permute-start.9 = (f32[520,128]{1,0:T(8,128)S(1)}, f32[520,128]{1,0:T(8,128)S(1)}, u32[]{:S(2)}, u32[]{:S(2)}) collective-permute-start(f32[520,128]{1,0:T(8,128)S(1)} %pad_maximum_fusion), channel_id=1, source_target_pairs={{0,2},{1,3},{2,0},{3,1},{4,6},{5,7},{6,4},{7,5},{8,10},{9,11},{10,... | collective-permute-start | bytes 798728 | tf_op jit(solution)/shard_map/ppermute | solution.py:30
  28.7 4.5 %shard_map.124 = (f32[2,128,128]{2,1,0:T(8,128)S(1)}, f32[2,128,128]{2,1,0:T(8,128)S(1)}, f32[2,32,128]{2,1,0:T(8,128)S(1)}, f32[2,32,128]{2,1,0:T(8,128)S(1)}) custom-call(bf16[528,4096]{1,0:T(8,128)(2,1)S(1)} %get-tuple-element.31.act_ref, bf16[512,4096]{1,0:T(8,128)(2,1)S(1)} %get-tuple-element.32.grad_ref, bf16[512,512]{1,0:T(8,128)(2,1)S(1)} %get-tuple-element.33.w_ref), custom_call_target="tpu_custom_call" | custom-call | flops 2147483648 | tf_op jit(solution)/shard_map/pallas_call | solution.py:68
  33.2 2.6 %collective-permute-done.9 = f32[520,128]{1,0:T(8,128)S(1)} collective-permute-done((f32[520,128]{1,0:T(8,128)S(1)}, f32[520,128]{1,0:T(8,128)S(1)}, u32[]{:S(2)}, u32[]{:S(2)}) %collective-permute-start.9) | collective-permute-done | bytes 266272 | tf_op jit(solution)/shard_map/ppermute | solution.py:30
  35.9 0.1 collective-permute-start.10
  36.0 5.5 %collective-permute-done.10 = f32[328,128]{1,0:T(8,128)S(1)} collective-permute-done((f32[328,128]{1,0:T(8,128)S(1)}, f32[328,128]{1,0:T(8,128)S(1)}, u32[]{:S(2)}, u32[]{:S(2)}) %collective-permute-start.10) | collective-permute-done | bytes 167968 | tf_op jit(solution)/shard_map/ppermute | solution.py:30
  41.5 2.1 %collective-permute-start.11 = (f32[168,128]{1,0:T(8,128)S(1)}, f32[168,128]{1,0:T(8,128)S(1)}, u32[]{:S(2)}, u32[]{:S(2)}) collective-permute-start(f32[168,128]{1,0:T(8,128)S(1)} %pad_maximum_fusion.2), channel_id=1, source_target_pairs={{0,8},{4,12},{8,0},{12,4},{1,9},{5,13},{9,1},{13,5},{2,10},{6,14},... | collective-permute-start | bytes 258056 | tf_op jit(solution)/shard_map/ppermute | solution.py:30
  43.6 4.0 %collective-permute-done.11.arrived_ref = f32[168,128]{1,0:T(8,128)S(1)} collective-permute-done((f32[168,128]{1,0:T(8,128)S(1)}, f32[168,128]{1,0:T(8,128)S(1)}, u32[]{:S(2)}, u32[]{:S(2)}) %collective-permute-start.11) | collective-permute-done | bytes 86048 | tf_op jit(solution)/shard_map/ppermute | solution.py:30
  47.7 1.6 %collective-permute-start.12 = (f32[136,128]{1,0:T(8,128)S(1)}, f32[136,128]{1,0:T(8,128)S(1)}, u32[]{:S(2)}, u32[]{:S(2)}) collective-permute-start(f32[136,128]{1,0:T(8,128)S(1)} %pad_maximum_fusion.3), channel_id=1, source_target_pairs={{0,16},{16,0},{1,17},{17,1},{2,18},{18,2},{3,19},{19,3},{4,20},{20... | collective-permute-start | bytes 208904 | tf_op jit(solution)/shard_map/ppermute | solution.py:30
  49.2 0.0 collective-permute-done.6.arrived_ref
  49.3 1.4 %collective-permute-start.7 = (f32[128,128]{1,0:T(8,128)S(1)}, f32[128,128]{1,0:T(8,128)S(1)}, u32[]{:S(2)}, u32[]{:S(2)}) collective-permute-start(f32[128,128]{1,0:T(8,128)S(1)} %bitcast.20), channel_id=1, source_target_pairs={{0,2},{1,3},{2,0},{3,1},{4,6},{5,7},{6,4},{7,5},{8,10},{9,11},{10,... | collective-permute-start | bytes 196616 | tf_op jit(solution)/shard_map/ppermute | solution.py:30
  50.6 2.9 %collective-permute-done.7.arrived_ref = f32[128,128]{1,0:T(8,128)S(1)} collective-permute-done((f32[128,128]{1,0:T(8,128)S(1)}, f32[128,128]{1,0:T(8,128)S(1)}, u32[]{:S(2)}, u32[]{:S(2)}) %collective-permute-start.7) | collective-permute-done | bytes 65568 | tf_op jit(solution)/shard_map/ppermute | solution.py:30
  53.6 0.6 %shard_map.126 = f32[1,128,128]{2,1,0:T(8,128)} custom-call(f32[128,128]{1,0:T(8,128)S(1)} %bitcast.18, f32[128,128]{1,0:T(8,128)S(1)} %collective-permute-done.7.arrived_ref), custom_call_target="tpu_custom_call" | custom-call | tf_op jit(solution)/shard_map/pallas_call | solution.py:380
  54.2 0.6 %shard_map.127 = f32[1,32,128]{2,1,0:T(8,128)} custom-call(f32[32,128]{1,0:T(8,128)S(1)} %get-tuple-element.45.keep_ref, f32[168,128]{1,0:T(8,128)S(1)} %collective-permute-done.11.arrived_ref), custom_call_target="tpu_custom_call" | custom-call | tf_op jit(solution)/shard_map/pallas_call | solution.py:380
  54.9 0.7 %finish.1 = (f32[32,512]{1,0:T(8,128)}, f32[1,32]{1,0:T(1,128)}) custom-call(f32[136,128]{1,0:T(8,128)S(1)} %fusion.final_ref), custom_call_target="tpu_custom_call" | custom-call | tf_op jit(solution)/shard_map/finish/pallas_call | solution.py:548
  (24 shorter events, 0.2 us)
Async XLA Ops:
  1.4 6.1 %collective-permute-start.2 = (bf16[144,128]{1,0:T(8,128)(2,1)S(1)}, bf16[144,128]{1,0:T(8,128)(2,1)S(1)}, u32[]{:S(2)}, u32[]{:S(2)}) collective-permute-start(bf16[144,128]{1,0:T(8,128)(2,1)S(1)} %shard_map.121.rest_0_.refs_6_), channel_id=1, source_target_pairs={{0,3},{1,2},{2,1},{3,0},{4,7},{5,6},{6,5},{7,4},{8,11},{9,10},{10,... | collective-permute-start | bytes 110600 | tf_op jit(solution)/shard_map/ppermute | solution.py:30
  3.9 4.1 %collective-permute-start.1 = (bf16[144,128]{1,0:T(8,128)(2,1)S(1)}, bf16[144,128]{1,0:T(8,128)(2,1)S(1)}, u32[]{:S(2)}, u32[]{:S(2)}) collective-permute-start(bf16[144,128]{1,0:T(8,128)(2,1)S(1)} %shard_map.121.rest_0_.refs_6_), channel_id=1, source_target_pairs={{0,2},{1,3},{2,0},{3,1},{4,6},{5,7},{6,4},{7,5},{8,10},{9,11},{10,... | collective-permute-start | bytes 110600 | tf_op jit(solution)/shard_map/ppermute | solution.py:30
  4.5 3.4 %collective-permute-start = (bf16[144,128]{1,0:T(8,128)(2,1)S(1)}, bf16[144,128]{1,0:T(8,128)(2,1)S(1)}, u32[]{:S(2)}, u32[]{:S(2)}) collective-permute-start(bf16[144,128]{1,0:T(8,128)(2,1)S(1)} %shard_map.121.rest_0_.refs_6_), channel_id=1, source_target_pairs={{0,1},{1,0},{2,3},{3,2},{4,5},{5,4},{6,7},{7,6},{8,9},{9,8},{10,11... | collective-permute-start | bytes 110600 | tf_op jit(solution)/shard_map/ppermute | solution.py:30
  8.0 5.6 %collective-permute-start.5 = (f32[40,128]{1,0:T(8,128)S(1)}, f32[40,128]{1,0:T(8,128)S(1)}, u32[]{:S(2)}, u32[]{:S(2)}) collective-permute-start(f32[40,128]{1,0:T(8,128)S(1)} %shard_map.122.refs_10_), channel_id=1, source_target_pairs={{0,12},{4,8},{8,4},{12,0},{1,13},{5,9},{9,5},{13,1},{2,14},{6,10},... | collective-permute-start | bytes 61448 | tf_op jit(solution)/shard_map/ppermute | solution.py:30
  11.6 4.7 %collective-permute-start.4 = (f32[40,128]{1,0:T(8,128)S(1)}, f32[40,128]{1,0:T(8,128)S(1)}, u32[]{:S(2)}, u32[]{:S(2)}) collective-permute-start(f32[40,128]{1,0:T(8,128)S(1)} %shard_map.122.refs_10_), channel_id=1, source_target_pairs={{0,8},{4,12},{8,0},{12,4},{1,9},{5,13},{9,1},{13,5},{2,10},{6,14},... | collective-permute-start | bytes 61448 | tf_op jit(solution)/shard_map/ppermute | solution.py:30
  11.7 4.7 %collective-permute-start.3 = (f32[40,128]{1,0:T(8,128)S(1)}, f32[40,128]{1,0:T(8,128)S(1)}, u32[]{:S(2)}, u32[]{:S(2)}) collective-permute-start(f32[40,128]{1,0:T(8,128)S(1)} %shard_map.122.refs_10_), channel_id=1, source_target_pairs={{0,4},{4,0},{8,12},{12,8},{1,5},{5,1},{9,13},{13,9},{2,6},{6,2},{1... | collective-permute-start | bytes 61448 | tf_op jit(solution)/shard_map/ppermute | solution.py:30
  25.2 2.0 %collective-permute-start.8 = (f32[1032,128]{1,0:T(8,128)S(1)}, f32[1032,128]{1,0:T(8,128)S(1)}, u32[]{:S(2)}, u32[]{:S(2)}) collective-permute-start(f32[1032,128]{1,0:T(8,128)S(1)} %get-tuple-element.40), channel_id=1, source_target_pairs={{0,1},{1,0},{2,3},{3,2},{4,5},{5,4},{6,7},{7,6},{8,9},{9,8},{10,11... | collective-permute-start | bytes 1585160 | tf_op jit(solution)/shard_map/ppermute | solution.py:30
  27.3 8.5 %collective-permute-start.9 = (f32[520,128]{1,0:T(8,128)S(1)}, f32[520,128]{1,0:T(8,128)S(1)}, u32[]{:S(2)}, u32[]{:S(2)}) collective-permute-start(f32[520,128]{1,0:T(8,128)S(1)} %pad_maximum_fusion), channel_id=1, source_target_pairs={{0,2},{1,3},{2,0},{3,1},{4,6},{5,7},{6,4},{7,5},{8,10},{9,11},{10,... | collective-permute-start | bytes 798728 | tf_op jit(solution)/shard_map/ppermute | solution.py:30
  35.9 5.5 %collective-permute-start.10 = (f32[328,128]{1,0:T(8,128)S(1)}, f32[328,128]{1,0:T(8,128)S(1)}, u32[]{:S(2)}, u32[]{:S(2)}) collective-permute-start(f32[328,128]{1,0:T(8,128)S(1)} %pad_maximum_fusion.1), channel_id=1, source_target_pairs={{0,4},{4,0},{8,12},{12,8},{1,5},{5,1},{9,13},{13,9},{2,6},{6,2},{1... | collective-permute-start | bytes 503816 | tf_op jit(solution)/shard_map/ppermute | solution.py:30
  41.5 6.1 %collective-permute-start.11 = (f32[168,128]{1,0:T(8,128)S(1)}, f32[168,128]{1,0:T(8,128)S(1)}, u32[]{:S(2)}, u32[]{:S(2)}) collective-permute-start(f32[168,128]{1,0:T(8,128)S(1)} %pad_maximum_fusion.2), channel_id=1, source_target_pairs={{0,8},{4,12},{8,0},{12,4},{1,9},{5,13},{9,1},{13,5},{2,10},{6,14},... | collective-permute-start | bytes 258056 | tf_op jit(solution)/shard_map/ppermute | solution.py:30
  43.6 5.6 %collective-permute-start.6 = (f32[2,128,128]{2,1,0:T(8,128)S(1)}, f32[2,128,128]{2,1,0:T(8,128)S(1)}, u32[]{:S(2)}, u32[]{:S(2)}) collective-permute-start(f32[2,128,128]{2,1,0:T(8,128)S(1)} %get-tuple-element.35), channel_id=1, source_target_pairs={{0,1},{1,0},{2,3},{3,2},{4,5},{5,4},{6,7},{7,6},{8,9},{9,8},{10,11... | collective-permute-start | bytes 393224 | tf_op jit(solution)/shard_map/ppermute | solution.py:30
  47.7 7.2 %collective-permute-start.12 = (f32[136,128]{1,0:T(8,128)S(1)}, f32[136,128]{1,0:T(8,128)S(1)}, u32[]{:S(2)}, u32[]{:S(2)}) collective-permute-start(f32[136,128]{1,0:T(8,128)S(1)} %pad_maximum_fusion.3), channel_id=1, source_target_pairs={{0,16},{16,0},{1,17},{17,1},{2,18},{18,2},{3,19},{19,3},{4,20},{20... | collective-permute-start | bytes 208904 | tf_op jit(solution)/shard_map/ppermute | solution.py:30
  49.3 4.3 %collective-permute-start.7 = (f32[128,128]{1,0:T(8,128)S(1)}, f32[128,128]{1,0:T(8,128)S(1)}, u32[]{:S(2)}, u32[]{:S(2)}) collective-permute-start(f32[128,128]{1,0:T(8,128)S(1)} %bitcast.20), channel_id=1, source_target_pairs={{0,2},{1,3},{2,0},{3,1},{4,6},{5,7},{6,4},{7,5},{8,10},{9,11},{10,... | collective-permute-start | bytes 196616 | tf_op jit(solution)/shard_map/ppermute | solution.py:30

commit v4 on v3

--- a/solution.py
+++ b/solution.py
@@ -109,7 +109,6 @@
     w_ref,
     bias_ref,
     ids_ref,
-    limits_ref,
     pred_out,
     alpha_out,
     beta_out,
@@ -117,10 +116,8 @@
     wt_out,
     bias_t,
     ids_out,
-    limits_out,
 ):
     ids_out[...] = ids_ref[...]
-    limits_out[...] = limits_ref[...]
     columns = pred_ref.shape[0]
     pred_out[:columns, :] = pred_ref[...].astype(jnp.float32)
     pred_out[columns:, :] = jnp.zeros((8, pred_out.shape[1]), jnp.float32)
@@ -273,7 +270,7 @@
     rows = width // parts
     for s in range(parts):
         label = reverse_bits(s // tm_size, label_size) ^ mine
-        tm = reverse_bits(s % tm_size, tm_size) ^ row
+        tm = s % tm_size ^ row
         start = pl.multiple_of((tm * label_size + label) * rows, rows)
         to = (s % (parts // 2)) * rows * tiles
         for k in range(tiles):
@@ -297,7 +294,7 @@
 
 
 def backward_kernel(act_ref, grad_ref, w_ref, *rest, tm_size, label_size, columns):
-    (enc_keep, enc_send, pred_keep, pred_send), (enc_acc, sums, pieces) = rest[:4], rest[4:]
+    enc_keep, enc_send, pred_out, enc_acc, sums, pieces = rest
     width, _ = w_ref.shape
     frames = enc_acc.shape[1]
     cells = GROUP * frames
@@ -330,15 +327,14 @@
     sums[...] = jnp.dot(pieces[...], chosen, preferred_element_type=jnp.float32)
 
     mine, row = lax.axis_index("label"), lax.axis_index("tm")
-    enc_width, pred_width = enc_keep.shape[2], pred_keep.shape[2]
+    enc_width, pred_width = enc_keep.shape[2], pred_out.shape[2]
     for s in range(label_size):
         start = pl.multiple_of((reverse_bits(s, label_size) ^ mine) * enc_width, enc_width)
         ref = (enc_keep, enc_send)[s // (label_size // 2)]
         ref[s % (label_size // 2)] = enc_acc[pl.ds(start, enc_width), :].T
     for s in range(tm_size):
-        start = pl.multiple_of((reverse_bits(s, tm_size) ^ row) * pred_width, pred_width)
-        ref = (pred_keep, pred_send)[s // (tm_size // 2)]
-        ref[s % (tm_size // 2)] = sums[pl.ds(start, pred_width), :].T[:columns, :]
+        start = pl.multiple_of((s ^ row) * pred_width, pred_width)
+        pred_out[s] = sums[pl.ds(start, pred_width), :].T[:columns, :]
 
 
 def finish(final_ref, weight_out, bias_out, weight_s, bias_s, done, *, label_size):
@@ -367,33 +363,27 @@
     high_ref[...] = keep_ref[-half:] + arrived_ref[-half:]
 
 
-def add_out(keep_ref, arrived_ref, out_ref, total, done, *, first):
+def add_out(*refs, first):
+    (*sources, out_ref, total, done) = refs
     count = total.shape[0]
-    total[...] = keep_ref[...] + arrived_ref[first : first + count]
+    total[...] = functools.reduce(
+        jnp.add, [ref[at : at + count] for ref, at in zip(sources, first, strict=True)]
+    )
     copy = pltpu.make_async_copy(total, out_ref.at[0], done)
     copy.start()
     copy.wait()
 
 
-def write_sum(keep, arrived, first):
-    rows, lanes = keep.shape
+def write_sum(sources, first, rows):
+    lanes = sources[0].shape[1]
     return pl.pallas_call(
         functools.partial(add_out, first=first),
-        in_specs=[vmem()] * 2,
+        in_specs=[vmem()] * len(sources),
         out_specs=pl.BlockSpec(memory_space=pltpu.HBM),
         out_shape=jax.ShapeDtypeStruct((1, rows, lanes), jnp.float32),
         scratch_shapes=[pltpu.VMEM((rows, lanes), jnp.float32), pltpu.SemaphoreType.DMA(())],
         compiler_params=pltpu.CompilerParams(vmem_limit_bytes=16 * MIB),
-    )(keep, arrived)
-
-
-def halve(keep, send, axis, bits):
-    for bit in bits:
-        if send is None:
-            half = keep.shape[0] // 2
-            keep, send = keep[:half], keep[half:]
-        keep, send = keep + swap(send, axis, bit), None
-    return keep
+    )(*sources)
 
 
 def lattice(
@@ -427,7 +417,7 @@
         )[0]
     encs = gather_slots(payload, "label")
     sides = encs if packed else gather_slots(beta[0:1, :], "label")
-    part, alpha, beta, weight, weight_t, bias_t, label_ids, limits = call(
+    part, alpha, beta, weight, weight_t, bias_t, label_ids = call(
         prepare,
         [
             shape((columns + 8, pred_width), f32),
@@ -437,7 +427,6 @@
             shape((vocab, width), bf16),
             shape((vocab, frames), f32),
             shape(label_ids.shape, label_ids.dtype),
-            shape((2, LANES), jnp.int32),
         ],
         (
             predictor_out[0],
@@ -446,10 +435,11 @@
             joint_weight,
             joint_bias[None, :],
             label_ids,
-            jnp.broadcast_to(jnp.concatenate([frame_count, label_count])[:, None], (2, LANES)),
         ),
         loads=6,
     )
+    limits = jnp.concatenate([frame_count, label_count])
+    limits = jnp.broadcast_to(limits[:, None], (2, LANES))
     payload = call(
         functools.partial(pack_predictor, packed=packed),
         [shape((columns + 8, pred_width), f32)],
@@ -482,20 +472,19 @@
         keep, bias_sum = keep[:half], keep[half:]
     else:
         slots = weight_parts[0][:width].reshape(tm_size, label_size, rows, tiles, LANES)
-        for axis, size, index in ((0, tm_size, row), (1, label_size, mine)):
-            order = jnp.array([reverse_bits(s, size) for s in range(size)], jnp.int32) ^ index
-            slots = jnp.take(slots, order, axis=axis)
+        order = jnp.array([reverse_bits(s, label_size) for s in range(label_size)], jnp.int32)
+        slots = jnp.take(slots, jnp.arange(tm_size) ^ row, axis=0)
+        slots = jnp.take(slots, order ^ mine, axis=1)
         slots = jnp.transpose(slots, (1, 0, 3, 2, 4)).reshape(width * tiles, LANES)
         bias_sum = jnp.pad(weight_parts[0][width].reshape(tiles, LANES), ((0, 8 - tiles), (0, 0)))
         keep, send = slots[:half], jnp.concatenate([slots[half:], bias_sum], axis=0)
 
-    stages = [("label", bit) for bit in bits_of(label_size)] + [("tm", bit) for bit in bits_of(tm_size)]
-    arrived = swap(send, *stages[0])
+    label_bits = bits_of(label_size)
+    arrived = swap(send, "label", label_bits[0])
     enc_half = shape((label_size // 2, frames, enc_width), f32)
-    pred_half = shape((tm_size // 2, columns, pred_width), f32)
-    enc_keep, enc_send, pred_keep, pred_send = call(
+    enc_keep, enc_send, pred_slots = call(
         functools.partial(backward_kernel, tm_size=tm_size, label_size=label_size, columns=columns),
-        [enc_half, enc_half, pred_half, pred_half],
+        [enc_half, enc_half, shape((tm_size, columns, pred_width), f32)],
         (act, grad, weight),
         [
             pltpu.VMEM((width, frames), f32),
@@ -505,45 +494,44 @@
         limit=BACKWARD_LIMIT,
         flops=2 * width * vocab * cells,
     )
-    joined = pred_width == LANES
-    enc_stages = bits_of(label_size)
     enc_sum, enc_rest = call(
         add_halves,
         [shape((max(label_size // 4, 1), frames, enc_width), f32)] * 2,
-        (enc_keep, swap(enc_send, "label", enc_stages[0])),
-    )
-    pred_sum, pred_rest = pred_keep, pred_send
-    for i, (axis, _) in enumerate(stages):
-        count = keep.shape[0]
-        keep, bias_sum = keep + arrived[:count], bias_sum + arrived[count : count + 8]
-        if joined and axis == "tm":
-            pred_rest = None
-            if i + 1 < len(stages):
-                pred_sum = pred_sum + arrived[count + 8 :].reshape(pred_sum.shape)
-            else:
-                predictor_gradient = write_sum(pred_sum[0], arrived, count + 8)
-        if i + 1 < len(stages):
-            half = count // 2
-            pieces = [keep[half:], bias_sum]
-            if joined and stages[i + 1][0] == "tm":
-                if pred_rest is None:
-                    middle = pred_sum.shape[0] // 2
-                    pred_sum, pred_rest = pred_sum[:middle], pred_sum[middle:]
-                pieces.append(pred_rest.reshape(-1, LANES))
-            keep = keep[:half]
-            arrived = swap(jnp.concatenate(pieces, axis=0), *stages[i + 1])
-    final = jnp.concatenate([keep, bias_sum], axis=0)
+        (enc_keep, swap(enc_send, "label", label_bits[0])),
+    )
+    for bit in label_bits[1:]:
+        half = keep.shape[0]
+        keep, bias_sum = keep + arrived[:half], bias_sum + arrived[half:]
+        half = half // 2
+        arrived = swap(jnp.concatenate([keep[half:], bias_sum], axis=0), "label", bit)
+        keep = keep[:half]
+    for bit in label_bits[1:-1]:
+        enc_sum = enc_sum + swap(enc_rest, "label", bit)
+        half = enc_sum.shape[0] // 2
+        enc_sum, enc_rest = enc_sum[:half], enc_sum[half:]
+    enc_rest = swap(enc_rest[0], "label", label_bits[-1])
+    encoder_gradient = write_sum((enc_sum[0], enc_rest), (0, 0), frames)
+
+    half, block = keep.shape[0], rows * tiles
+    keep, bias_sum = keep + arrived[:half], bias_sum + arrived[half:]
+    joined = pred_width == LANES
+    others, pred_others = [], []
+    for s in range(1, tm_size):
+        pieces = [keep[s * block : (s + 1) * block], bias_sum]
+        if joined:
+            pieces.append(pred_slots[s])
+        others.append(swap(jnp.concatenate(pieces, axis=0), "tm", s))
+        if not joined:
+            pred_others.append(swap(pred_slots[s], "tm", s))
+    final = jnp.concatenate([keep[:block], bias_sum], axis=0)
+    final = final + functools.reduce(jnp.add, [x[: block + 8] for x in others])
     for bit in bits_of(lax.axis_size("dp")):
         other = swap(final, "dp", bit)
         final = final + other
-    for bit in enc_stages[1:-1]:
-        enc_sum = enc_sum + swap(enc_rest, "label", bit)
-        half = enc_sum.shape[0] // 2
-        enc_sum, enc_rest = enc_sum[:half], enc_sum[half:]
-    enc_rest = swap(enc_rest[0], "label", enc_stages[-1])
-    encoder_gradient = write_sum(enc_sum[0], enc_rest, 0)
-    if not joined:
-        predictor_gradient = halve(pred_keep, pred_send, "tm", bits_of(tm_size))
+    first = [block + 8] * len(others) if joined else [0] * len(others)
+    predictor_gradient = write_sum(
+        (pred_slots[0], *(others if joined else pred_others)), (0, *first), columns
+    )
     bias_rows = vocab // parts
     weight_gradient, bias_gradient = pl.pallas_call(
         functools.partial(finish, label_size=label_size),

time: 55.8 us -> 54.3 us (0.973)
  waiting for transfers between devices: 21.3 us -> 17.8 us
  starting transfers between devices: 14.1 us -> 16.1 us
    ppermute x13 -> x14, waiting for transfers between devices: 21.3 us -> 17.8 us  [swap(): lax.ppermute(value, axis, [(i, i ^ bit) for i in range(lax.axis_size(axis...]
    ppermute x13 -> x14, starting transfers between devices: 14.1 us -> 16.1 us  [swap(): lax.ppermute(value, axis, [(i, i ^ bit) for i in range(lax.axis_size(axis...]
  transfers between devices with their start and end apart: 13 -> 14, of which waited for: 8 -> 8; matrix products, arithmetic and copies ran while one was open for 0% -> 0% of each run, Pallas kernels for 13% -> 13%
where the time goes in v4:
time: 54.3 us; the launch traced here: 54 us
  waiting for transfers between devices  17.8 us (33%)
  Pallas kernels  17.6 us (32%)
  starting transfers between devices  16.1 us (30%)
  between operations  2.08 us (4%)
    ppermute x14, waiting for transfers between devices, swap(): lax.ppermute(value, axis, [(i, i ^ bit) for i in range(lax.axis_size(axis...  17.8 us
    ppermute x14, starting transfers between devices, swap(): lax.ppermute(value, axis, [(i, i ^ bit) for i in range(lax.axis_size(axis...  16.1 us
    pallas_call x6, Pallas kernels, call(): pl.pallas_call(kernel, grid_spec=pltpu.PrefetchScalarGridSpec(num_scalar_...  15.7 us
    pallas_call x2, Pallas kernels, write_sum(): pl.pallas_call(functools.partial(add_out, first=first), in_specs=[vmem()]...  1.27 us
  transfers between devices with their start and end apart: 14, of which 8 were waited for; matrix products, arithmetic and copies ran while one was open for 0% of the time, Pallas kernels for 13%

profile of v4, /device:TPU:0, one launch (start us, length us, event | category | flops | bytes accessed | tf_op | source)
XLA Modules:
  0.0 54.0 jit_solution(6626970254399032415)
XLA Ops:
  0.6 0.8 %shard_map.121.rest_0_.refs_6_ = bf16[144,128]{1,0:T(8,128)(2,1)S(1)} custom-call(bf16[128,128]{1,0:T(8,128)(2,1)} %bitcast.24, f32[32,128]{1,0:T(8,128)} %bitcast.22), custom_call_target="tpu_custom_call" | custom-call | tf_op jit(solution)/shard_map/pallas_call | solution.py:68
  1.4 2.5 %collective-permute-start.2 = (bf16[144,128]{1,0:T(8,128)(2,1)S(1)}, bf16[144,128]{1,0:T(8,128)(2,1)S(1)}, u32[]{:S(2)}, u32[]{:S(2)}) collective-permute-start(bf16[144,128]{1,0:T(8,128)(2,1)S(1)} %shard_map.121.rest_0_.refs_6_), channel_id=1, source_target_pairs={{0,3},{1,2},{2,1},{3,0},{4,7},{5,6},{6,5},{7,4},{8,11},{9,10},{10,... | collective-permute-start | bytes 110600 | tf_op jit(solution)/shard_map/ppermute | solution.py:30
  3.9 0.6 %collective-permute-start.1 = (bf16[144,128]{1,0:T(8,128)(2,1)S(1)}, bf16[144,128]{1,0:T(8,128)(2,1)S(1)}, u32[]{:S(2)}, u32[]{:S(2)}) collective-permute-start(bf16[144,128]{1,0:T(8,128)(2,1)S(1)} %shard_map.121.rest_0_.refs_6_), channel_id=1, source_target_pairs={{0,2},{1,3},{2,0},{3,1},{4,6},{5,7},{6,4},{7,5},{8,10},{9,11},{10,... | collective-permute-start | bytes 110600 | tf_op jit(solution)/shard_map/ppermute | solution.py:30
  4.5 0.0 collective-permute-start
  5.9 1.5 %shard_map.120 = (f32[40,128]{1,0:T(8,128)S(1)}, f32[32,128]{1,0:T(8,128)S(1)}, f32[32,128]{1,0:T(8,128)S(1)}, bf16[512,512]{1,0:T(8,128)(2,1)S(1)}, bf16[512,51...) custom-call(bf16[32,128]{1,0:T(8,128)(2,1)} %bitcast.26, f32[32,128]{1,0:T(8,128)} %bitcast.23, ...), custom_call_target="tpu_custom_call" | custom-call | tf_op jit(solution)/shard_map/pallas_call | solution.py:68
  7.4 0.0 collective-permute-done.2.rest_3_.refs_9_
  7.4 0.6 %collective-permute-done.1.rest_2_.refs_8_ = bf16[144,128]{1,0:T(8,128)(2,1)S(1)} collective-permute-done((bf16[144,128]{1,0:T(8,128)(2,1)S(1)}, bf16[144,128]{1,0:T(8,128)(2,1)S(1)}, u32[]{:S(2)}, u32[]{:S(2)}) %collective-permute-start.1) | collective-permute-done | bytes 36896 | tf_op jit(solution)/shard_map/ppermute | solution.py:30
  8.0 0.1 shard_map.122.refs_10_
  8.0 3.6 %collective-permute-start.5 = (f32[40,128]{1,0:T(8,128)S(1)}, f32[40,128]{1,0:T(8,128)S(1)}, u32[]{:S(2)}, u32[]{:S(2)}) collective-permute-start(f32[40,128]{1,0:T(8,128)S(1)} %shard_map.122.refs_10_), channel_id=1, source_target_pairs={{0,12},{4,8},{8,4},{12,0},{1,13},{5,9},{9,5},{13,1},{2,14},{6,10},... | collective-permute-start | bytes 61448 | tf_op jit(solution)/shard_map/ppermute | solution.py:30
  11.7 0.8 %collective-permute-start.3 = (f32[40,128]{1,0:T(8,128)S(1)}, f32[40,128]{1,0:T(8,128)S(1)}, u32[]{:S(2)}, u32[]{:S(2)}) collective-permute-start(f32[40,128]{1,0:T(8,128)S(1)} %shard_map.122.refs_10_), channel_id=1, source_target_pairs={{0,4},{4,0},{8,12},{12,8},{1,5},{5,1},{9,13},{13,9},{2,6},{6,2},{1... | collective-permute-start | bytes 61448 | tf_op jit(solution)/shard_map/ppermute | solution.py:30
  12.4 0.1 pad_add_fusion
  12.5 1.1 %collective-permute-done.5.refs_13_ = f32[40,128]{1,0:T(8,128)S(1)} collective-permute-done((f32[40,128]{1,0:T(8,128)S(1)}, f32[40,128]{1,0:T(8,128)S(1)}, u32[]{:S(2)}, u32[]{:S(2)}) %collective-permute-start.5) | collective-permute-done | bytes 20512 | tf_op jit(solution)/shard_map/ppermute | solution.py:30
  13.6 2.7 %collective-permute-done.4.refs_12_ = f32[40,128]{1,0:T(8,128)S(1)} collective-permute-done((f32[40,128]{1,0:T(8,128)S(1)}, f32[40,128]{1,0:T(8,128)S(1)}, u32[]{:S(2)}, u32[]{:S(2)}) %collective-permute-start.4) | collective-permute-done | bytes 20512 | tf_op jit(solution)/shard_map/ppermute | solution.py:30
  16.3 0.1 broadcast_in_dim.10.refs_1_
  16.4 8.8 %shard_map.123 = (bf16[528,4096]{1,0:T(8,128)(2,1)S(1)}, bf16[512,4096]{1,0:T(8,128)(2,1)S(1)}, f32[1032,128]{1,0:T(8,128)S(1)}, f32[1032,128]{1,0:T(8,128)S(1)}) custom-call(s32[1,32]{1,0:T(1,128)S(1)} %get-tuple-element.22.refs_0_, s32[2,128]{1,0:T(2,128)S(1)} %broadcast_in_dim.10.refs_1_, f32[32,128]{1,0:T(8,128)S(1)} %get-tuple-element.23.refs_2_, ...), custom_call_target="tpu_custom_call" | custom-call | flops 4294967296 | tf_op jit(solution)/shard_map/pallas_call | solution.py:68
  25.2 0.1 collective-permute-start.8
  25.3 1.9 %collective-permute-done.8 = f32[1032,128]{1,0:T(8,128)S(1)} collective-permute-done((f32[1032,128]{1,0:T(8,128)S(1)}, f32[1032,128]{1,0:T(8,128)S(1)}, u32[]{:S(2)}, u32[]{:S(2)}) %collective-permute-start.8) | collective-permute-done | bytes 528416 | tf_op jit(solution)/shard_map/ppermute | solution.py:30
  27.2 0.1 slice_add_fusion
  27.4 1.2 %collective-permute-start.9 = (f32[520,128]{1,0:T(8,128)S(1)}, f32[520,128]{1,0:T(8,128)S(1)}, u32[]{:S(2)}, u32[]{:S(2)}) collective-permute-start(f32[520,128]{1,0:T(8,128)S(1)} %pad_maximum_fusion), channel_id=1, source_target_pairs={{0,2},{1,3},{2,0},{3,1},{4,6},{5,7},{6,4},{7,5},{8,10},{9,11},{10,... | collective-permute-start | bytes 798728 | tf_op jit(solution)/shard_map/ppermute | solution.py:30
  28.6 4.5 %shard_map.124 = (f32[2,128,128]{2,1,0:T(8,128)S(1)}, f32[2,128,128]{2,1,0:T(8,128)S(1)}, f32[4,32,128]{2,1,0:T(8,128)S(1)}) custom-call(bf16[528,4096]{1,0:T(8,128)(2,1)S(1)} %get-tuple-element.28.act_ref, bf16[512,4096]{1,0:T(8,128)(2,1)S(1)} %get-tuple-element.29.grad_ref, bf16[512,512]{1,0:T(8,128)(2,1)S(1)} %get-tuple-element.30.w_ref), custom_call_target="tpu_custom_call" | custom-call | flops 2147483648 | tf_op jit(solution)/shard_map/pallas_call | solution.py:68
  33.2 2.7 %collective-permute-done.9 = f32[520,128]{1,0:T(8,128)S(1)} collective-permute-done((f32[520,128]{1,0:T(8,128)S(1)}, f32[520,128]{1,0:T(8,128)S(1)}, u32[]{:S(2)}, u32[]{:S(2)}) %collective-permute-start.9) | collective-permute-done | bytes 266272 | tf_op jit(solution)/shard_map/ppermute | solution.py:30
  36.0 1.5 %collective-permute-start.12 = (f32[168,128]{1,0:T(8,128)S(1)}, f32[168,128]{1,0:T(8,128)S(1)}, u32[]{:S(2)}, u32[]{:S(2)}) collective-permute-start(f32[168,128]{1,0:T(8,128)S(1)} %get-tuple-element.48), channel_id=1, source_target_pairs={{0,12},{4,8},{8,4},{12,0},{1,13},{5,9},{9,5},{13,1},{2,14},{6,10},... | collective-permute-start | bytes 258056 | tf_op jit(solution)/shard_map/ppermute | solution.py:30
  37.5 0.6 %collective-permute-start.11 = (f32[168,128]{1,0:T(8,128)S(1)}, f32[168,128]{1,0:T(8,128)S(1)}, u32[]{:S(2)}, u32[]{:S(2)}) collective-permute-start(f32[168,128]{1,0:T(8,128)S(1)} %get-tuple-element.49), channel_id=1, source_target_pairs={{0,8},{4,12},{8,0},{12,4},{1,9},{5,13},{9,1},{13,5},{2,10},{6,14},... | collective-permute-start | bytes 258056 | tf_op jit(solution)/shard_map/ppermute | solution.py:30
  38.1 2.3 %collective-permute-start.10 = (f32[168,128]{1,0:T(8,128)S(1)}, f32[168,128]{1,0:T(8,128)S(1)}, u32[]{:S(2)}, u32[]{:S(2)}) collective-permute-start(f32[168,128]{1,0:T(8,128)S(1)} %get-tuple-element.50), channel_id=1, source_target_pairs={{0,4},{4,0},{8,12},{12,8},{1,5},{5,1},{9,13},{13,9},{2,6},{6,2},{1... | collective-permute-start | bytes 258056 | tf_op jit(solution)/shard_map/ppermute | solution.py:30
  40.4 2.8 %collective-permute-done.12.refs_3_ = f32[168,128]{1,0:T(8,128)S(1)} collective-permute-done((f32[168,128]{1,0:T(8,128)S(1)}, f32[168,128]{1,0:T(8,128)S(1)}, u32[]{:S(2)}, u32[]{:S(2)}) %collective-permute-start.12) | collective-permute-done | bytes 86048 | tf_op jit(solution)/shard_map/ppermute | solution.py:30
  43.2 2.8 %collective-permute-done.11.refs_2_ = f32[168,128]{1,0:T(8,128)S(1)} collective-permute-done((f32[168,128]{1,0:T(8,128)S(1)}, f32[168,128]{1,0:T(8,128)S(1)}, u32[]{:S(2)}, u32[]{:S(2)}) %collective-permute-start.11) | collective-permute-done | bytes 86048 | tf_op jit(solution)/shard_map/ppermute | solution.py:30
  46.1 1.6 %collective-permute-start.13 = (f32[136,128]{1,0:T(8,128)S(1)}, f32[136,128]{1,0:T(8,128)S(1)}, u32[]{:S(2)}, u32[]{:S(2)}) collective-permute-start(f32[136,128]{1,0:T(8,128)S(1)} %fusion.3), channel_id=1, source_target_pairs={{0,16},{16,0},{1,17},{17,1},{2,18},{18,2},{3,19},{19,3},{4,20},{20... | collective-permute-start | bytes 208904 | tf_op jit(solution)/shard_map/ppermute | solution.py:30
  47.7 1.2 %collective-permute-start.7 = (f32[128,128]{1,0:T(8,128)S(1)}, f32[128,128]{1,0:T(8,128)S(1)}, u32[]{:S(2)}, u32[]{:S(2)}) collective-permute-start(f32[128,128]{1,0:T(8,128)S(1)} %bitcast.21), channel_id=1, source_target_pairs={{0,2},{1,3},{2,0},{3,1},{4,6},{5,7},{6,4},{7,5},{8,10},{9,11},{10,... | collective-permute-start | bytes 196616 | tf_op jit(solution)/shard_map/ppermute | solution.py:30
  48.9 3.1 %collective-permute-done.7.refs_1_ = f32[128,128]{1,0:T(8,128)S(1)} collective-permute-done((f32[128,128]{1,0:T(8,128)S(1)}, f32[128,128]{1,0:T(8,128)S(1)}, u32[]{:S(2)}, u32[]{:S(2)}) %collective-permute-start.7) | collective-permute-done | bytes 65568 | tf_op jit(solution)/shard_map/ppermute | solution.py:30
  52.0 0.6 %shard_map.126 = f32[1,128,128]{2,1,0:T(8,128)} custom-call(f32[128,128]{1,0:T(8,128)S(1)} %bitcast.20, f32[128,128]{1,0:T(8,128)S(1)} %collective-permute-done.7.refs_1_), custom_call_target="tpu_custom_call" | custom-call | tf_op jit(solution)/shard_map/pallas_call | solution.py:379
  52.7 0.6 %shard_map.127 = f32[1,32,128]{2,1,0:T(8,128)} custom-call(f32[32,128]{1,0:T(8,128)S(1)} %get-tuple-element.47.refs_0_, f32[168,128]{1,0:T(8,128)S(1)} %collective-permute-done.10.refs_1_, f32[168,128]{1,0:T(8,128)S(1)} %collective-permute-done.11.refs_2_, f32[168,128]{1,0:T(8,128)S(1)} %collective-permute-done.12.refs_3_), custom_call_target="tpu_custom_call" | custom-call | tf_op jit(solution)/shard_map/pallas_call | solution.py:379
  53.3 0.7 %finish.1 = (f32[32,512]{1,0:T(8,128)}, f32[1,32]{1,0:T(1,128)}) custom-call(f32[136,128]{1,0:T(8,128)S(1)} %add.31.final_ref), custom_call_target="tpu_custom_call" | custom-call | tf_op jit(solution)/shard_map/finish/pallas_call | solution.py:536
  (18 shorter events, 0.2 us)
Async XLA Ops:
  1.4 5.9 %collective-permute-start.2 = (bf16[144,128]{1,0:T(8,128)(2,1)S(1)}, bf16[144,128]{1,0:T(8,128)(2,1)S(1)}, u32[]{:S(2)}, u32[]{:S(2)}) collective-permute-start(bf16[144,128]{1,0:T(8,128)(2,1)S(1)} %shard_map.121.rest_0_.refs_6_), channel_id=1, source_target_pairs={{0,3},{1,2},{2,1},{3,0},{4,7},{5,6},{6,5},{7,4},{8,11},{9,10},{10,... | collective-permute-start | bytes 110600 | tf_op jit(solution)/shard_map/ppermute | solution.py:30
  3.9 4.1 %collective-permute-start.1 = (bf16[144,128]{1,0:T(8,128)(2,1)S(1)}, bf16[144,128]{1,0:T(8,128)(2,1)S(1)}, u32[]{:S(2)}, u32[]{:S(2)}) collective-permute-start(bf16[144,128]{1,0:T(8,128)(2,1)S(1)} %shard_map.121.rest_0_.refs_6_), channel_id=1, source_target_pairs={{0,2},{1,3},{2,0},{3,1},{4,6},{5,7},{6,4},{7,5},{8,10},{9,11},{10,... | collective-permute-start | bytes 110600 | tf_op jit(solution)/shard_map/ppermute | solution.py:30
  4.5 3.4 %collective-permute-start = (bf16[144,128]{1,0:T(8,128)(2,1)S(1)}, bf16[144,128]{1,0:T(8,128)(2,1)S(1)}, u32[]{:S(2)}, u32[]{:S(2)}) collective-permute-start(bf16[144,128]{1,0:T(8,128)(2,1)S(1)} %shard_map.121.rest_0_.refs_6_), channel_id=1, source_target_pairs={{0,1},{1,0},{2,3},{3,2},{4,5},{5,4},{6,7},{7,6},{8,9},{9,8},{10,11... | collective-permute-start | bytes 110600 | tf_op jit(solution)/shard_map/ppermute | solution.py:30
  8.0 5.6 %collective-permute-start.5 = (f32[40,128]{1,0:T(8,128)S(1)}, f32[40,128]{1,0:T(8,128)S(1)}, u32[]{:S(2)}, u32[]{:S(2)}) collective-permute-start(f32[40,128]{1,0:T(8,128)S(1)} %shard_map.122.refs_10_), channel_id=1, source_target_pairs={{0,12},{4,8},{8,4},{12,0},{1,13},{5,9},{9,5},{13,1},{2,14},{6,10},... | collective-permute-start | bytes 61448 | tf_op jit(solution)/shard_map/ppermute | solution.py:30
  11.6 4.7 %collective-permute-start.4 = (f32[40,128]{1,0:T(8,128)S(1)}, f32[40,128]{1,0:T(8,128)S(1)}, u32[]{:S(2)}, u32[]{:S(2)}) collective-permute-start(f32[40,128]{1,0:T(8,128)S(1)} %shard_map.122.refs_10_), channel_id=1, source_target_pairs={{0,8},{4,12},{8,0},{12,4},{1,9},{5,13},{9,1},{13,5},{2,10},{6,14},... | collective-permute-start | bytes 61448 | tf_op jit(solution)/shard_map/ppermute | solution.py:30
  11.7 4.7 %collective-permute-start.3 = (f32[40,128]{1,0:T(8,128)S(1)}, f32[40,128]{1,0:T(8,128)S(1)}, u32[]{:S(2)}, u32[]{:S(2)}) collective-permute-start(f32[40,128]{1,0:T(8,128)S(1)} %shard_map.122.refs_10_), channel_id=1, source_target_pairs={{0,4},{4,0},{8,12},{12,8},{1,5},{5,1},{9,13},{13,9},{2,6},{6,2},{1... | collective-permute-start | bytes 61448 | tf_op jit(solution)/shard_map/ppermute | solution.py:30
  25.2 2.0 %collective-permute-start.8 = (f32[1032,128]{1,0:T(8,128)S(1)}, f32[1032,128]{1,0:T(8,128)S(1)}, u32[]{:S(2)}, u32[]{:S(2)}) collective-permute-start(f32[1032,128]{1,0:T(8,128)S(1)} %get-tuple-element.37), channel_id=1, source_target_pairs={{0,1},{1,0},{2,3},{3,2},{4,5},{5,4},{6,7},{7,6},{8,9},{9,8},{10,11... | collective-permute-start | bytes 1585160 | tf_op jit(solution)/shard_map/ppermute | solution.py:30
  27.4 8.5 %collective-permute-start.9 = (f32[520,128]{1,0:T(8,128)S(1)}, f32[520,128]{1,0:T(8,128)S(1)}, u32[]{:S(2)}, u32[]{:S(2)}) collective-permute-start(f32[520,128]{1,0:T(8,128)S(1)} %pad_maximum_fusion), channel_id=1, source_target_pairs={{0,2},{1,3},{2,0},{3,1},{4,6},{5,7},{6,4},{7,5},{8,10},{9,11},{10,... | collective-permute-start | bytes 798728 | tf_op jit(solution)/shard_map/ppermute | solution.py:30
  36.0 7.3 %collective-permute-start.12 = (f32[168,128]{1,0:T(8,128)S(1)}, f32[168,128]{1,0:T(8,128)S(1)}, u32[]{:S(2)}, u32[]{:S(2)}) collective-permute-start(f32[168,128]{1,0:T(8,128)S(1)} %get-tuple-element.48), channel_id=1, source_target_pairs={{0,12},{4,8},{8,4},{12,0},{1,13},{5,9},{9,5},{13,1},{2,14},{6,10},... | collective-permute-start | bytes 258056 | tf_op jit(solution)/shard_map/ppermute | solution.py:30
  37.5 8.6 %collective-permute-start.11 = (f32[168,128]{1,0:T(8,128)S(1)}, f32[168,128]{1,0:T(8,128)S(1)}, u32[]{:S(2)}, u32[]{:S(2)}) collective-permute-start(f32[168,128]{1,0:T(8,128)S(1)} %get-tuple-element.49), channel_id=1, source_target_pairs={{0,8},{4,12},{8,0},{12,4},{1,9},{5,13},{9,1},{13,5},{2,10},{6,14},... | collective-permute-start | bytes 258056 | tf_op jit(solution)/shard_map/ppermute | solution.py:30
  38.1 7.9 %collective-permute-start.10 = (f32[168,128]{1,0:T(8,128)S(1)}, f32[168,128]{1,0:T(8,128)S(1)}, u32[]{:S(2)}, u32[]{:S(2)}) collective-permute-start(f32[168,128]{1,0:T(8,128)S(1)} %get-tuple-element.50), channel_id=1, source_target_pairs={{0,4},{4,0},{8,12},{12,8},{1,5},{5,1},{9,13},{13,9},{2,6},{6,2},{1... | collective-permute-start | bytes 258056 | tf_op jit(solution)/shard_map/ppermute | solution.py:30
  40.4 7.2 %collective-permute-start.6 = (f32[2,128,128]{2,1,0:T(8,128)S(1)}, f32[2,128,128]{2,1,0:T(8,128)S(1)}, u32[]{:S(2)}, u32[]{:S(2)}) collective-permute-start(f32[2,128,128]{2,1,0:T(8,128)S(1)} %get-tuple-element.32), channel_id=1, source_target_pairs={{0,1},{1,0},{2,3},{3,2},{4,5},{5,4},{6,7},{7,6},{8,9},{9,8},{10,11... | collective-permute-start | bytes 393224 | tf_op jit(solution)/shard_map/ppermute | solution.py:30
  46.1 7.2 %collective-permute-start.13 = (f32[136,128]{1,0:T(8,128)S(1)}, f32[136,128]{1,0:T(8,128)S(1)}, u32[]{:S(2)}, u32[]{:S(2)}) collective-permute-start(f32[136,128]{1,0:T(8,128)S(1)} %fusion.3), channel_id=1, source_target_pairs={{0,16},{16,0},{1,17},{17,1},{2,18},{18,2},{3,19},{19,3},{4,20},{20... | collective-permute-start | bytes 208904 | tf_op jit(solution)/shard_map/ppermute | solution.py:30
  47.7 4.3 %collective-permute-start.7 = (f32[128,128]{1,0:T(8,128)S(1)}, f32[128,128]{1,0:T(8,128)S(1)}, u32[]{:S(2)}, u32[]{:S(2)}) collective-permute-start(f32[128,128]{1,0:T(8,128)S(1)} %bitcast.21), channel_id=1, source_target_pairs={{0,2},{1,3},{2,0},{3,1},{4,6},{5,7},{6,4},{7,5},{8,10},{9,11},{10,... | collective-permute-start | bytes 196616 | tf_op jit(solution)/shard_map/ppermute | solution.py:30

commit v5 on v4

--- a/solution.py
+++ b/solution.py
@@ -335,6 +335,24 @@
     for s in range(tm_size):
         start = pl.multiple_of((s ^ row) * pred_width, pred_width)
         pred_out[s] = sums[pl.ds(start, pred_width), :].T[:columns, :]
+
+
+def split_kernel(keep_ref, bias_ref, arrived_ref, near_keep, far_keep, near_send, far_send):
+    rows = near_keep.shape[0]
+    for i, ref in enumerate((near_keep, far_keep, near_send, far_send)):
+        here = slice(i * rows, (i + 1) * rows)
+        ref[:rows, :] = keep_ref[here, :] + arrived_ref[here, :]
+    far_send[rows:, :] = bias_ref[...] + arrived_ref[4 * rows :, :]
+
+
+def block_kernel(keep_ref, bias_ref, arrived_ref, bias_more, pred_ref, *out_refs, block, first):
+    bias = bias_ref[-8:, :] + bias_more[-8:, :]
+    for i, ref in enumerate(out_refs):
+        here = slice(i * block, (i + 1) * block)
+        ref[:block, :] = keep_ref[here, :] + arrived_ref[here, :]
+        ref[block : block + 8, :] = bias
+        if ref.shape[0] > block + 8:
+            ref[block + 8 :, :] = pred_ref[first + i]
 
 
 def finish(final_ref, weight_out, bias_out, weight_s, bias_s, done, *, label_size):
@@ -499,12 +517,20 @@
         [shape((max(label_size // 4, 1), frames, enc_width), f32)] * 2,
         (enc_keep, swap(enc_send, "label", label_bits[0])),
     )
-    for bit in label_bits[1:]:
+    for bit in label_bits[1:-1]:
         half = keep.shape[0]
         keep, bias_sum = keep + arrived[:half], bias_sum + arrived[half:]
         half = half // 2
         arrived = swap(jnp.concatenate([keep[half:], bias_sum], axis=0), "label", bit)
         keep = keep[:half]
+    middle = keep.shape[0] // 4
+    near_keep, far_keep, near_send, far_send = call(
+        split_kernel,
+        [shape((middle, LANES), f32)] * 3 + [shape((middle + 8, LANES), f32)],
+        (keep, bias_sum, arrived),
+    )
+    far = swap(far_send, "label", label_bits[-1])
+    near = swap(near_send, "label", label_bits[-1])
     for bit in label_bits[1:-1]:
         enc_sum = enc_sum + swap(enc_rest, "label", bit)
         half = enc_sum.shape[0] // 2
@@ -512,19 +538,25 @@
     enc_rest = swap(enc_rest[0], "label", label_bits[-1])
     encoder_gradient = write_sum((enc_sum[0], enc_rest), (0, 0), frames)
 
-    half, block = keep.shape[0], rows * tiles
-    keep, bias_sum = keep + arrived[:half], bias_sum + arrived[half:]
-    joined = pred_width == LANES
+    block, joined = rows * tiles, pred_width == LANES
+    payload = shape((block + 8 + columns * joined, LANES), f32)
+    far_blocks = call(
+        functools.partial(block_kernel, block=block, first=tm_size // 2),
+        [payload] * (tm_size // 2),
+        (far_keep, far_send, far, far, pred_slots),
+    )
+    near_blocks = call(
+        functools.partial(block_kernel, block=block, first=0),
+        [payload] * (tm_size // 2),
+        (near_keep, far_send, near, far, pred_slots),
+    )
+    blocks = near_blocks + far_blocks
     others, pred_others = [], []
     for s in range(1, tm_size):
-        pieces = [keep[s * block : (s + 1) * block], bias_sum]
-        if joined:
-            pieces.append(pred_slots[s])
-        others.append(swap(jnp.concatenate(pieces, axis=0), "tm", s))
+        others.append(swap(blocks[s], "tm", s))
         if not joined:
             pred_others.append(swap(pred_slots[s], "tm", s))
-    final = jnp.concatenate([keep[:block], bias_sum], axis=0)
-    final = final + functools.reduce(jnp.add, [x[: block + 8] for x in others])
+    final = functools.reduce(jnp.add, [x[: block + 8] for x in [blocks[0], *others]])
     for bit in bits_of(lax.axis_size("dp")):
         other = swap(final, "dp", bit)
         final = final + other

time: 54.3 us -> 51 us (0.939)
  waiting for transfers between devices: 17.8 us -> 13.6 us
  starting transfers between devices: 16.1 us -> 17.1 us
    ppermute x14 -> x15, waiting for transfers between devices: 17.8 us -> 13.6 us  [swap(): lax.ppermute(value, axis, [(i, i ^ bit) for i in range(lax.axis_size(axis...]
    ppermute x14 -> x15, starting transfers between devices: 16.1 us -> 17.1 us  [swap(): lax.ppermute(value, axis, [(i, i ^ bit) for i in range(lax.axis_size(axis...]
    pallas_call x6 -> x9, Pallas kernels: 15.7 us -> 15.8 us  [call(): pl.pallas_call(kernel, grid_spec=pltpu.PrefetchScalarGridSpec(num_scalar_...]
  transfers between devices with their start and end apart: 14 -> 15, of which waited for: 8 -> 7; matrix products, arithmetic and copies ran while one was open for 0% -> 0% of each run, Pallas kernels for 13% -> 14%
where the time goes in v5:
time: 51 us; the launch traced here: 50.7 us
  Pallas kernels  17.8 us (35%)
  starting transfers between devices  17.1 us (34%)
  waiting for transfers between devices  13.6 us (27%)
  between operations  2.05 us (4%)
    ppermute x15, starting transfers between devices, swap(): lax.ppermute(value, axis, [(i, i ^ bit) for i in range(lax.axis_size(axis...  17.1 us
    pallas_call x9, Pallas kernels, call(): pl.pallas_call(kernel, grid_spec=pltpu.PrefetchScalarGridSpec(num_scalar_...  15.8 us
    ppermute x15, waiting for transfers between devices, swap(): lax.ppermute(value, axis, [(i, i ^ bit) for i in range(lax.axis_size(axis...  13.6 us
    pallas_call x2, Pallas kernels, write_sum(): pl.pallas_call(functools.partial(add_out, first=first), in_specs=[vmem()]...  1.27 us
  transfers between devices with their start and end apart: 15, of which 7 were waited for; matrix products, arithmetic and copies ran while one was open for 0% of the time, Pallas kernels for 14%

profile of v5, /device:TPU:0, one launch (start us, length us, event | category | flops | bytes accessed | tf_op | source)
XLA Modules:
  0.0 50.7 jit_solution(7414272599394560564)
XLA Ops:
  0.6 0.8 %shard_map.121.rest_0_.refs_6_ = bf16[144,128]{1,0:T(8,128)(2,1)S(1)} custom-call(bf16[128,128]{1,0:T(8,128)(2,1)} %bitcast.18, f32[32,128]{1,0:T(8,128)} %bitcast.16), custom_call_target="tpu_custom_call" | custom-call | tf_op jit(solution)/shard_map/pallas_call | solution.py:68
  1.4 2.5 %collective-permute-start.2 = (bf16[144,128]{1,0:T(8,128)(2,1)S(1)}, bf16[144,128]{1,0:T(8,128)(2,1)S(1)}, u32[]{:S(2)}, u32[]{:S(2)}) collective-permute-start(bf16[144,128]{1,0:T(8,128)(2,1)S(1)} %shard_map.121.rest_0_.refs_6_), channel_id=1, source_target_pairs={{0,3},{1,2},{2,1},{3,0},{4,7},{5,6},{6,5},{7,4},{8,11},{9,10},{10,... | collective-permute-start | bytes 110600 | tf_op jit(solution)/shard_map/ppermute | solution.py:30
  3.9 0.6 %collective-permute-start.1 = (bf16[144,128]{1,0:T(8,128)(2,1)S(1)}, bf16[144,128]{1,0:T(8,128)(2,1)S(1)}, u32[]{:S(2)}, u32[]{:S(2)}) collective-permute-start(bf16[144,128]{1,0:T(8,128)(2,1)S(1)} %shard_map.121.rest_0_.refs_6_), channel_id=1, source_target_pairs={{0,2},{1,3},{2,0},{3,1},{4,6},{5,7},{6,4},{7,5},{8,10},{9,11},{10,... | collective-permute-start | bytes 110600 | tf_op jit(solution)/shard_map/ppermute | solution.py:30
  4.5 0.0 collective-permute-start
  5.9 1.5 %shard_map.120 = (f32[40,128]{1,0:T(8,128)S(1)}, f32[32,128]{1,0:T(8,128)S(1)}, f32[32,128]{1,0:T(8,128)S(1)}, bf16[512,512]{1,0:T(8,128)(2,1)S(1)}, bf16[512,51...) custom-call(bf16[32,128]{1,0:T(8,128)(2,1)} %bitcast.20, f32[32,128]{1,0:T(8,128)} %bitcast.17, ...), custom_call_target="tpu_custom_call" | custom-call | tf_op jit(solution)/shard_map/pallas_call | solution.py:68
  7.4 0.6 %collective-permute-done.1.rest_2_.refs_8_ = bf16[144,128]{1,0:T(8,128)(2,1)S(1)} collective-permute-done((bf16[144,128]{1,0:T(8,128)(2,1)S(1)}, bf16[144,128]{1,0:T(8,128)(2,1)S(1)}, u32[]{:S(2)}, u32[]{:S(2)}) %collective-permute-start.1) | collective-permute-done | bytes 36896 | tf_op jit(solution)/shard_map/ppermute | solution.py:30
  8.0 0.1 shard_map.122.refs_10_
  8.0 3.6 %collective-permute-start.5 = (f32[40,128]{1,0:T(8,128)S(1)}, f32[40,128]{1,0:T(8,128)S(1)}, u32[]{:S(2)}, u32[]{:S(2)}) collective-permute-start(f32[40,128]{1,0:T(8,128)S(1)} %shard_map.122.refs_10_), channel_id=1, source_target_pairs={{0,12},{4,8},{8,4},{12,0},{1,13},{5,9},{9,5},{13,1},{2,14},{6,10},... | collective-permute-start | bytes 61448 | tf_op jit(solution)/shard_map/ppermute | solution.py:30
  11.7 0.8 %collective-permute-start.3 = (f32[40,128]{1,0:T(8,128)S(1)}, f32[40,128]{1,0:T(8,128)S(1)}, u32[]{:S(2)}, u32[]{:S(2)}) collective-permute-start(f32[40,128]{1,0:T(8,128)S(1)} %shard_map.122.refs_10_), channel_id=1, source_target_pairs={{0,4},{4,0},{8,12},{12,8},{1,5},{5,1},{9,13},{13,9},{2,6},{6,2},{1... | collective-permute-start | bytes 61448 | tf_op jit(solution)/shard_map/ppermute | solution.py:30
  12.4 0.1 pad_add_fusion
  12.5 1.1 %collective-permute-done.5.refs_13_ = f32[40,128]{1,0:T(8,128)S(1)} collective-permute-done((f32[40,128]{1,0:T(8,128)S(1)}, f32[40,128]{1,0:T(8,128)S(1)}, u32[]{:S(2)}, u32[]{:S(2)}) %collective-permute-start.5) | collective-permute-done | bytes 20512 | tf_op jit(solution)/shard_map/ppermute | solution.py:30
  13.6 2.7 %collective-permute-done.4.refs_12_ = f32[40,128]{1,0:T(8,128)S(1)} collective-permute-done((f32[40,128]{1,0:T(8,128)S(1)}, f32[40,128]{1,0:T(8,128)S(1)}, u32[]{:S(2)}, u32[]{:S(2)}) %collective-permute-start.4) | collective-permute-done | bytes 20512 | tf_op jit(solution)/shard_map/ppermute | solution.py:30
  16.3 0.1 broadcast_in_dim.10.refs_1_
  16.4 8.8 %shard_map.123 = (bf16[528,4096]{1,0:T(8,128)(2,1)S(1)}, bf16[512,4096]{1,0:T(8,128)(2,1)S(1)}, f32[1032,128]{1,0:T(8,128)S(1)}, f32[1032,128]{1,0:T(8,128)S(1)}) custom-call(s32[1,32]{1,0:T(1,128)S(1)} %get-tuple-element.30.refs_0_, s32[2,128]{1,0:T(2,128)S(1)} %broadcast_in_dim.10.refs_1_, f32[32,128]{1,0:T(8,128)S(1)} %get-tuple-element.31.refs_2_, ...), custom_call_target="tpu_custom_call" | custom-call | flops 4294967296 | tf_op jit(solution)/shard_map/pallas_call | solution.py:68
  25.2 0.1 collective-permute-start.8
  25.4 1.8 %collective-permute-done.8.arrived_ref = f32[1032,128]{1,0:T(8,128)S(1)} collective-permute-done((f32[1032,128]{1,0:T(8,128)S(1)}, f32[1032,128]{1,0:T(8,128)S(1)}, u32[]{:S(2)}, u32[]{:S(2)}) %collective-permute-start.8) | collective-permute-done | bytes 528416 | tf_op jit(solution)/shard_map/ppermute | solution.py:30
  27.2 0.1 shard_map.127
  27.3 1.2 %collective-permute-start.9 = (f32[256,128]{1,0:T(8,128)S(1)}, f32[256,128]{1,0:T(8,128)S(1)}, u32[]{:S(2)}, u32[]{:S(2)}) collective-permute-start(f32[256,128]{1,0:T(8,128)S(1)} %get-tuple-element.48), channel_id=1, source_target_pairs={{0,2},{1,3},{2,0},{3,1},{4,6},{5,7},{6,4},{7,5},{8,10},{9,11},{10,... | collective-permute-start | bytes 393224 | tf_op jit(solution)/shard_map/ppermute | solution.py:30
  28.5 0.8 %collective-permute-start.10 = (f32[264,128]{1,0:T(8,128)S(1)}, f32[264,128]{1,0:T(8,128)S(1)}, u32[]{:S(2)}, u32[]{:S(2)}) collective-permute-start(f32[264,128]{1,0:T(8,128)S(1)} %get-tuple-element.47.bias_ref), channel_id=1, source_target_pairs={{0,2},{1,3},{2,0},{3,1},{4,6},{5,7},{6,4},{7,5},{8,10},{9,11},{10,... | collective-permute-start | bytes 405512 | tf_op jit(solution)/shard_map/ppermute | solution.py:30
  29.4 4.5 %shard_map.124 = (f32[2,128,128]{2,1,0:T(8,128)S(1)}, f32[2,128,128]{2,1,0:T(8,128)S(1)}, f32[4,32,128]{2,1,0:T(8,128)S(1)}) custom-call(bf16[528,4096]{1,0:T(8,128)(2,1)S(1)} %get-tuple-element.36.act_ref, bf16[512,4096]{1,0:T(8,128)(2,1)S(1)} %get-tuple-element.37.grad_ref, bf16[512,512]{1,0:T(8,128)(2,1)S(1)} %get-tuple-element.38.w_ref), custom_call_target="tpu_custom_call" | custom-call | flops 2147483648 | tf_op jit(solution)/shard_map/pallas_call | solution.py:68
  33.9 0.1 collective-permute-start.6
  34.0 1.8 %collective-permute-done.10.bias_more.arrived_ref = f32[264,128]{1,0:T(8,128)S(1)} collective-permute-done((f32[264,128]{1,0:T(8,128)S(1)}, f32[264,128]{1,0:T(8,128)S(1)}, u32[]{:S(2)}, u32[]{:S(2)}) %collective-permute-start.10) | collective-permute-done | bytes 135200 | tf_op jit(solution)/shard_map/ppermute | solution.py:30
  35.8 0.1 collective-permute-start.11
  35.9 2.1 %collective-permute-start.12 = (f32[168,128]{1,0:T(8,128)S(1)}, f32[168,128]{1,0:T(8,128)S(1)}, u32[]{:S(2)}, u32[]{:S(2)}) collective-permute-start(f32[168,128]{1,0:T(8,128)S(1)} %get-tuple-element.51), channel_id=1, source_target_pairs={{0,8},{4,12},{8,0},{12,4},{1,9},{5,13},{9,1},{13,5},{2,10},{6,14},... | collective-permute-start | bytes 258056 | tf_op jit(solution)/shard_map/ppermute | solution.py:30
  38.0 2.3 %collective-permute-start.13 = (f32[168,128]{1,0:T(8,128)S(1)}, f32[168,128]{1,0:T(8,128)S(1)}, u32[]{:S(2)}, u32[]{:S(2)}) collective-permute-start(f32[168,128]{1,0:T(8,128)S(1)} %get-tuple-element.52), channel_id=1, source_target_pairs={{0,12},{4,8},{8,4},{12,0},{1,13},{5,9},{9,5},{13,1},{2,14},{6,10},... | collective-permute-start | bytes 258056 | tf_op jit(solution)/shard_map/ppermute | solution.py:30
  40.4 1.2 %collective-permute-start.7 = (f32[128,128]{1,0:T(8,128)S(1)}, f32[128,128]{1,0:T(8,128)S(1)}, u32[]{:S(2)}, u32[]{:S(2)}) collective-permute-start(f32[128,128]{1,0:T(8,128)S(1)} %bitcast.15), channel_id=1, source_target_pairs={{0,2},{1,3},{2,0},{3,1},{4,6},{5,7},{6,4},{7,5},{8,10},{9,11},{10,... | collective-permute-start | bytes 196616 | tf_op jit(solution)/shard_map/ppermute | solution.py:30
  41.6 4.0 %collective-permute-done.12.refs_2_ = f32[168,128]{1,0:T(8,128)S(1)} collective-permute-done((f32[168,128]{1,0:T(8,128)S(1)}, f32[168,128]{1,0:T(8,128)S(1)}, u32[]{:S(2)}, u32[]{:S(2)}) %collective-permute-start.12) | collective-permute-done | bytes 86048 | tf_op jit(solution)/shard_map/ppermute | solution.py:30
  45.7 1.6 %collective-permute-start.14 = (f32[136,128]{1,0:T(8,128)S(1)}, f32[136,128]{1,0:T(8,128)S(1)}, u32[]{:S(2)}, u32[]{:S(2)}) collective-permute-start(f32[136,128]{1,0:T(8,128)S(1)} %slice_add_fusion), channel_id=1, source_target_pairs={{0,16},{16,0},{1,17},{17,1},{2,18},{18,2},{3,19},{19,3},{4,20},{20... | collective-permute-start | bytes 208904 | tf_op jit(solution)/shard_map/ppermute | solution.py:30
  47.3 0.6 %shard_map.126 = f32[1,128,128]{2,1,0:T(8,128)} custom-call(f32[128,128]{1,0:T(8,128)S(1)} %bitcast.14, f32[128,128]{1,0:T(8,128)S(1)} %collective-permute-done.7.refs_1_), custom_call_target="tpu_custom_call" | custom-call | tf_op jit(solution)/shard_map/pallas_call | solution.py:397
  47.9 0.6 %shard_map.130 = f32[1,32,128]{2,1,0:T(8,128)} custom-call(f32[32,128]{1,0:T(8,128)S(1)} %slice_bitcast_fusion.refs_0_, f32[168,128]{1,0:T(8,128)S(1)} %collective-permute-done.11.refs_1_, f32[168,128]{1,0:T(8,128)S(1)} %collective-permute-done.12.refs_2_, f32[168,128]{1,0:T(8,128)S(1)} %collective-permute-done.13.refs_3_), custom_call_target="tpu_custom_call" | custom-call | tf_op jit(solution)/shard_map/pallas_call | solution.py:397
  48.5 1.5 %collective-permute-done.14 = f32[136,128]{1,0:T(8,128)S(1)} collective-permute-done((f32[136,128]{1,0:T(8,128)S(1)}, f32[136,128]{1,0:T(8,128)S(1)}, u32[]{:S(2)}, u32[]{:S(2)}) %collective-permute-start.14) | collective-permute-done | bytes 69664 | tf_op jit(solution)/shard_map/ppermute | solution.py:30
  50.1 0.7 %finish.1 = (f32[32,512]{1,0:T(8,128)}, f32[1,32]{1,0:T(1,128)}) custom-call(f32[136,128]{1,0:T(8,128)S(1)} %add.15.final_ref), custom_call_target="tpu_custom_call" | custom-call | tf_op jit(solution)/shard_map/finish/pallas_call | solution.py:568
  (17 shorter events, 0.2 us)
Async XLA Ops:
  1.4 5.9 %collective-permute-start.2 = (bf16[144,128]{1,0:T(8,128)(2,1)S(1)}, bf16[144,128]{1,0:T(8,128)(2,1)S(1)}, u32[]{:S(2)}, u32[]{:S(2)}) collective-permute-start(bf16[144,128]{1,0:T(8,128)(2,1)S(1)} %shard_map.121.rest_0_.refs_6_), channel_id=1, source_target_pairs={{0,3},{1,2},{2,1},{3,0},{4,7},{5,6},{6,5},{7,4},{8,11},{9,10},{10,... | collective-permute-start | bytes 110600 | tf_op jit(solution)/shard_map/ppermute | solution.py:30
  3.9 4.1 %collective-permute-start.1 = (bf16[144,128]{1,0:T(8,128)(2,1)S(1)}, bf16[144,128]{1,0:T(8,128)(2,1)S(1)}, u32[]{:S(2)}, u32[]{:S(2)}) collective-permute-start(bf16[144,128]{1,0:T(8,128)(2,1)S(1)} %shard_map.121.rest_0_.refs_6_), channel_id=1, source_target_pairs={{0,2},{1,3},{2,0},{3,1},{4,6},{5,7},{6,4},{7,5},{8,10},{9,11},{10,... | collective-permute-start | bytes 110600 | tf_op jit(solution)/shard_map/ppermute | solution.py:30
  4.5 3.4 %collective-permute-start = (bf16[144,128]{1,0:T(8,128)(2,1)S(1)}, bf16[144,128]{1,0:T(8,128)(2,1)S(1)}, u32[]{:S(2)}, u32[]{:S(2)}) collective-permute-start(bf16[144,128]{1,0:T(8,128)(2,1)S(1)} %shard_map.121.rest_0_.refs_6_), channel_id=1, source_target_pairs={{0,1},{1,0},{2,3},{3,2},{4,5},{5,4},{6,7},{7,6},{8,9},{9,8},{10,11... | collective-permute-start | bytes 110600 | tf_op jit(solution)/shard_map/ppermute | solution.py:30
  8.0 5.6 %collective-permute-start.5 = (f32[40,128]{1,0:T(8,128)S(1)}, f32[40,128]{1,0:T(8,128)S(1)}, u32[]{:S(2)}, u32[]{:S(2)}) collective-permute-start(f32[40,128]{1,0:T(8,128)S(1)} %shard_map.122.refs_10_), channel_id=1, source_target_pairs={{0,12},{4,8},{8,4},{12,0},{1,13},{5,9},{9,5},{13,1},{2,14},{6,10},... | collective-permute-start | bytes 61448 | tf_op jit(solution)/shard_map/ppermute | solution.py:30
  11.6 4.7 %collective-permute-start.4 = (f32[40,128]{1,0:T(8,128)S(1)}, f32[40,128]{1,0:T(8,128)S(1)}, u32[]{:S(2)}, u32[]{:S(2)}) collective-permute-start(f32[40,128]{1,0:T(8,128)S(1)} %shard_map.122.refs_10_), channel_id=1, source_target_pairs={{0,8},{4,12},{8,0},{12,4},{1,9},{5,13},{9,1},{13,5},{2,10},{6,14},... | collective-permute-start | bytes 61448 | tf_op jit(solution)/shard_map/ppermute | solution.py:30
  11.7 4.7 %collective-permute-start.3 = (f32[40,128]{1,0:T(8,128)S(1)}, f32[40,128]{1,0:T(8,128)S(1)}, u32[]{:S(2)}, u32[]{:S(2)}) collective-permute-start(f32[40,128]{1,0:T(8,128)S(1)} %shard_map.122.refs_10_), channel_id=1, source_target_pairs={{0,4},{4,0},{8,12},{12,8},{1,5},{5,1},{9,13},{13,9},{2,6},{6,2},{1... | collective-permute-start | bytes 61448 | tf_op jit(solution)/shard_map/ppermute | solution.py:30
  25.2 2.0 %collective-permute-start.8 = (f32[1032,128]{1,0:T(8,128)S(1)}, f32[1032,128]{1,0:T(8,128)S(1)}, u32[]{:S(2)}, u32[]{:S(2)}) collective-permute-start(f32[1032,128]{1,0:T(8,128)S(1)} %get-tuple-element.45), channel_id=1, source_target_pairs={{0,1},{1,0},{2,3},{3,2},{4,5},{5,4},{6,7},{7,6},{8,9},{9,8},{10,11... | collective-permute-start | bytes 1585160 | tf_op jit(solution)/shard_map/ppermute | solution.py:30
  27.3 6.7 %collective-permute-start.9 = (f32[256,128]{1,0:T(8,128)S(1)}, f32[256,128]{1,0:T(8,128)S(1)}, u32[]{:S(2)}, u32[]{:S(2)}) collective-permute-start(f32[256,128]{1,0:T(8,128)S(1)} %get-tuple-element.48), channel_id=1, source_target_pairs={{0,2},{1,3},{2,0},{3,1},{4,6},{5,7},{6,4},{7,5},{8,10},{9,11},{10,... | collective-permute-start | bytes 393224 | tf_op jit(solution)/shard_map/ppermute | solution.py:30
  28.5 7.2 %collective-permute-start.10 = (f32[264,128]{1,0:T(8,128)S(1)}, f32[264,128]{1,0:T(8,128)S(1)}, u32[]{:S(2)}, u32[]{:S(2)}) collective-permute-start(f32[264,128]{1,0:T(8,128)S(1)} %get-tuple-element.47.bias_ref), channel_id=1, source_target_pairs={{0,2},{1,3},{2,0},{3,1},{4,6},{5,7},{6,4},{7,5},{8,10},{9,11},{10,... | collective-permute-start | bytes 405512 | tf_op jit(solution)/shard_map/ppermute | solution.py:30
  33.9 6.4 %collective-permute-start.6 = (f32[2,128,128]{2,1,0:T(8,128)S(1)}, f32[2,128,128]{2,1,0:T(8,128)S(1)}, u32[]{:S(2)}, u32[]{:S(2)}) collective-permute-start(f32[2,128,128]{2,1,0:T(8,128)S(1)} %get-tuple-element.40), channel_id=1, source_target_pairs={{0,1},{1,0},{2,3},{3,2},{4,5},{5,4},{6,7},{7,6},{8,9},{9,8},{10,11... | collective-permute-start | bytes 393224 | tf_op jit(solution)/shard_map/ppermute | solution.py:30
  35.8 5.8 %collective-permute-start.11 = (f32[168,128]{1,0:T(8,128)S(1)}, f32[168,128]{1,0:T(8,128)S(1)}, u32[]{:S(2)}, u32[]{:S(2)}) collective-permute-start(f32[168,128]{1,0:T(8,128)S(1)} %get-tuple-element.49), channel_id=1, source_target_pairs={{0,4},{4,0},{8,12},{12,8},{1,5},{5,1},{9,13},{13,9},{2,6},{6,2},{1... | collective-permute-start | bytes 258056 | tf_op jit(solution)/shard_map/ppermute | solution.py:30
  35.9 9.7 %collective-permute-start.12 = (f32[168,128]{1,0:T(8,128)S(1)}, f32[168,128]{1,0:T(8,128)S(1)}, u32[]{:S(2)}, u32[]{:S(2)}) collective-permute-start(f32[168,128]{1,0:T(8,128)S(1)} %get-tuple-element.51), channel_id=1, source_target_pairs={{0,8},{4,12},{8,0},{12,4},{1,9},{5,13},{9,1},{13,5},{2,10},{6,14},... | collective-permute-start | bytes 258056 | tf_op jit(solution)/shard_map/ppermute | solution.py:30
  38.0 7.6 %collective-permute-start.13 = (f32[168,128]{1,0:T(8,128)S(1)}, f32[168,128]{1,0:T(8,128)S(1)}, u32[]{:S(2)}, u32[]{:S(2)}) collective-permute-start(f32[168,128]{1,0:T(8,128)S(1)} %get-tuple-element.52), channel_id=1, source_target_pairs={{0,12},{4,8},{8,4},{12,0},{1,13},{5,9},{9,5},{13,1},{2,14},{6,10},... | collective-permute-start | bytes 258056 | tf_op jit(solution)/shard_map/ppermute | solution.py:30
  40.4 6.9 %collective-permute-start.7 = (f32[128,128]{1,0:T(8,128)S(1)}, f32[128,128]{1,0:T(8,128)S(1)}, u32[]{:S(2)}, u32[]{:S(2)}) collective-permute-start(f32[128,128]{1,0:T(8,128)S(1)} %bitcast.15), channel_id=1, source_target_pairs={{0,2},{1,3},{2,0},{3,1},{4,6},{5,7},{6,4},{7,5},{8,10},{9,11},{10,... | collective-permute-start | bytes 196616 | tf_op jit(solution)/shard_map/ppermute | solution.py:30
  45.7 4.4 %collective-permute-start.14 = (f32[136,128]{1,0:T(8,128)S(1)}, f32[136,128]{1,0:T(8,128)S(1)}, u32[]{:S(2)}, u32[]{:S(2)}) collective-permute-start(f32[136,128]{1,0:T(8,128)S(1)} %slice_add_fusion), channel_id=1, source_target_pairs={{0,16},{16,0},{1,17},{17,1},{2,18},{18,2},{3,19},{19,3},{4,20},{20... | collective-permute-start | bytes 208904 | tf_op jit(solution)/shard_map/ppermute | solution.py:30
